TPU v7x, 32 devices: a whole 2x2x4 slice. The times are simulated.
32 devices in a mesh: obj: 4 (over z), plane: 4 (over y, core), tile: 2 (over x).
Axes of the slice: x: 2, y: 2, z: 4, core: 2. Of those that a mesh axis runs over, the one named last changes fastest.
Arguments:
- tokens: bfloat16 [8, 3, 32, 32, 1024], P('obj', None, 'plane', 'tile'), may hold values from -6 to 6
- gout: bfloat16 [8, 3, 128, 128, 128], P('obj', None, 'plane', 'tile'), may hold values from -6 to 6
- deconv_weight: bfloat16 [1024, 2048], replicated, may hold values from -0.1875 to 0.1875
- deconv_bias: float32 [128], replicated, may hold values from -4 to 4
- conv_kernels: bfloat16 [2, 1152, 128], replicated, may hold values from -0.1875 to 0.1875
- conv_biases: float32 [2, 128], replicated, may hold values from -4 to 4
Outputs:
- d_tokens: bfloat16 [8, 3, 32, 32, 1024], P('obj', None, 'plane', 'tile')
- d_deconv_weight: float32 [1024, 2048], P(('obj', 'plane', 'tile'))
- d_deconv_bias: float32 [128], replicated
- d_conv_kernels: float32 [2, 1152, 128], replicated
- d_conv_biases: float32 [2, 128], replicated
All inputs are finite; a program needn't handle non-finite values.
Results may differ from a plain program's by a relative error of at most 0.01.
Values may be sent and summed in bfloat16 or wider, within the bound.
No kernel may reach another device: no remote copies, remote signals or barrier semaphores. Data moves between devices by JAX's collectives and lax.ppermute only.
A program may use at most 192 MiB of HBM per device.

v0:
```python
import jax
import jax.numpy as jnp
from jax import lax
from jax.sharding import PartitionSpec as P


def padded_2(array, sides, width):
    for axis, dim in sides:
        size, length = (lax.axis_size(axis), array.shape[dim])
        up = [(i, (i + 1) % size) for i in range(size - 1)]
        down = [(j, i) for i, j in up]
        last = lax.slice_in_dim(array, length - width, length, axis=dim)
        initial = lax.slice_in_dim(array, 0, width, axis=dim)
        before = lax.ppermute(last, axis, up)
        after = lax.ppermute(initial, axis, down)
        array = jnp.concatenate([before, array, after], axis=dim)
    return array


def columns(padded, height, breadth, flipped):
    pieces = []
    for tap_y in range(3):
        for tap_x in range(3):
            shift_y = 2 - tap_y if flipped else tap_y
            shift_x = 2 - tap_x if flipped else tap_x
            pieces.append(padded[..., shift_y : shift_y + height, shift_x : shift_x + breadth, :])
    return jnp.concatenate(pieces, axis=-1)


def convolve(padded, kernel, height, breadth, flipped):
    gathered = columns(padded, height, breadth, flipped)
    products = jnp.dot(
        gathered.reshape(-1, gathered.shape[-1]), kernel, preferred_element_type=jnp.float32
    )
    return products.reshape(padded.shape[:-3] + (height, breadth, kernel.shape[1]))


def upsample(tokens_here, weight, offsets):
    planes, tok_rows, tok_cols, fan_width = tokens_here.shape
    products = jnp.dot(
        tokens_here.reshape(-1, fan_width), weight, preferred_element_type=jnp.float32
    )
    products = products.reshape(planes, tok_rows, tok_cols, 4, 4, -1).transpose(0, 1, 3, 2, 4, 5)
    return products.reshape(planes, 4 * tok_rows, 4 * tok_cols, -1) + offsets


def tap_layout(gradient):
    planes, height, breadth, channels = gradient.shape
    blocks = gradient.reshape(planes, height // 4, 4, breadth // 4, 4, channels).transpose(
        0, 1, 3, 2, 4, 5
    )
    return blocks.reshape(-1, 16 * channels)


def contexts(row_sum, col_sum, extent):
    row_mean = row_sum / extent
    col_mean = col_sum / extent
    row_ctx = jnp.stack([row_mean[1], row_mean[0], col_mean[0]])
    col_ctx = jnp.stack([row_mean[2], col_mean[2], col_mean[1]])
    return (row_ctx, col_ctx)


def adjoint_contexts(row_sum, col_sum, extent):
    row_adjoint = jnp.stack([row_sum[1], row_sum[0], col_sum[0]])
    col_adjoint = jnp.stack([row_sum[2], col_sum[2], col_sum[1]])
    return (row_adjoint / extent, col_adjoint / extent)


def flip_kernel(kernel):
    channels = kernel.shape[1]
    return kernel.reshape(9, channels, channels).transpose(0, 2, 1).reshape(9 * channels, channels)


def pooled_sums(row_part, col_part, row_start, col_start, extent):
    zero_index = jnp.zeros((), jnp.int32)
    row_full = lax.dynamic_update_slice(
        jnp.zeros((row_part.shape[0], extent, row_part.shape[2]), jnp.float32),
        row_part,
        (zero_index, row_start, zero_index),
    )
    col_full = lax.dynamic_update_slice(
        jnp.zeros((col_part.shape[0], extent, col_part.shape[2]), jnp.float32),
        col_part,
        (zero_index, col_start, zero_index),
    )
    result = lax.psum((row_full, col_full), ("plane", "tile"))
    return result


def object_pass(tokens_here, grad_out, deconv_weight, deconv_bias, conv_kernels, conv_biases):
    hidden = upsample(tokens_here, deconv_weight, deconv_bias)
    planes, height, breadth, channels = hidden.shape
    extent = height * lax.axis_size("plane")
    row_start = lax.axis_index("plane") * height
    col_start = lax.axis_index("tile") * breadth
    layers = conv_kernels.shape[0]
    stored = []
    for layer_index in range(layers):
        row_sum, col_sum = pooled_sums(
            jnp.sum(hidden, 2), jnp.sum(hidden, 1), row_start, col_start, extent
        )
        row_ctx, col_ctx = contexts(row_sum, col_sum, extent)
        row_band = lax.dynamic_slice_in_dim(row_ctx, row_start, height, 1)
        col_band = lax.dynamic_slice_in_dim(col_ctx, col_start, breadth, 1)
        preact = hidden + row_band[:, :, None, :] + col_band[:, None, :, :]
        activated = jax.nn.silu(preact).astype(jnp.bfloat16)
        padded = padded_2(activated, (("plane", 1), ("tile", 2)), 1)
        conv_out = convolve(padded, conv_kernels[layer_index], height, breadth, False)
        hidden = hidden + conv_out + conv_biases[layer_index]
        stored.append((preact, padded))
    gradient = grad_out.astype(jnp.float32)
    kernel_grads = []
    bias_grads = []
    for layer_index in reversed(range(layers)):
        preact, padded = stored[layer_index]
        grad_bf = gradient.astype(jnp.bfloat16)
        bias_grads.insert(0, jnp.sum(gradient, (0, 1, 2)))
        grad_pad = padded_2(grad_bf, (("plane", 1), ("tile", 2)), 1)
        act_grad = convolve(grad_pad, flip_kernel(conv_kernels[layer_index]), height, breadth, True)
        gathered = columns(padded, height, breadth, False)
        kernel_grads.insert(
            0,
            lax.dot_general(
                gathered.reshape(-1, gathered.shape[-1]),
                grad_bf.reshape(-1, channels),
                (((0,), (0,)), ((), ())),
                preferred_element_type=jnp.float32,
            ),
        )
        sigmoid_pre = jax.nn.sigmoid(preact)
        pre_grad = act_grad * sigmoid_pre * (1.0 + preact * (1.0 - sigmoid_pre))
        row_sum, col_sum = pooled_sums(
            jnp.sum(pre_grad, 2), jnp.sum(pre_grad, 1), row_start, col_start, extent
        )
        row_adjoint, col_adjoint = adjoint_contexts(row_sum, col_sum, extent)
        row_band = lax.dynamic_slice_in_dim(row_adjoint, row_start, height, 1)
        col_band = lax.dynamic_slice_in_dim(col_adjoint, col_start, breadth, 1)
        gradient = gradient + pre_grad + row_band[:, :, None, :] + col_band[:, None, :, :]
    grad_bf = gradient.astype(jnp.bfloat16)
    tap_grads = tap_layout(grad_bf)
    tok_grad = lax.dot_general(
        tap_grads, deconv_weight, (((1,), (1,)), ((), ())), preferred_element_type=jnp.float32
    )
    tok_grad = tok_grad.astype(jnp.bfloat16).reshape(tokens_here.shape)
    return (
        tok_grad,
        tap_grads,
        jnp.sum(gradient, (0, 1, 2)),
        jnp.stack(kernel_grads),
        jnp.stack(bias_grads),
    )


def per_device(tokens, gout, deconv_weight, deconv_bias, conv_kernels, conv_biases):
    tok_list = []
    tap_list = []
    flat_list = []
    bias_grad = jnp.zeros((deconv_bias.shape[0],), jnp.float32)
    kernel_sum = jnp.zeros(conv_kernels.shape, jnp.float32)
    conv_bias_sum = jnp.zeros(conv_biases.shape, jnp.float32)
    for object_index in range(tokens.shape[0]):
        tokens_here = tokens[object_index]
        tok_grad, tap_grads, bias_part, kernel_part, conv_bias_part = object_pass(
            tokens_here, gout[object_index], deconv_weight, deconv_bias, conv_kernels, conv_biases
        )
        tok_list.append(tok_grad)
        tap_list.append(tap_grads)
        flat_list.append(tokens_here.reshape(-1, tokens_here.shape[-1]))
        bias_grad = bias_grad + bias_part
        kernel_sum = kernel_sum + kernel_part
        conv_bias_sum = conv_bias_sum + conv_bias_part
    tok_out = jnp.stack(tok_list)
    tap_all = jnp.concatenate(tap_list, axis=0)
    tok_flat = jnp.concatenate(flat_list, axis=0)
    object_part = lax.psum_scatter(
        lax.dot_general(
            tok_flat, tap_all, (((0,), (0,)), ((), ())), preferred_element_type=jnp.float32
        ).astype(jnp.bfloat16),
        "obj",
        scatter_dimension=0,
        tiled=True,
    ).astype(jnp.float32)
    weight_grad = lax.psum_scatter(object_part, ("plane", "tile"), scatter_dimension=0, tiled=True)
    kernel_total, conv_bias_total, bias_total = lax.psum(
        (kernel_sum, conv_bias_sum, bias_grad), ("obj", "plane", "tile")
    )
    return (tok_out, weight_grad, bias_total, kernel_total, conv_bias_total)


def solution(mesh):
    placed = (
        P("obj", None, "plane", "tile", None),
        P("obj", None, "plane", "tile", None),
        P(),
        P(),
        P(),
        P(),
    )
    return jax.shard_map(
        per_device,
        mesh=mesh,
        in_specs=placed,
        out_specs=(
            P("obj", None, "plane", "tile", None),
            P(("obj", "plane", "tile"), None),
            P(),
            P(),
            P(),
        ),
        check_vma=False,
    )
```

profile of v0, /device:TPU:0, one launch (start us, length us, event | category | flops | bytes accessed | tf_op | source)
XLA Modules:
  0.0 781.8 jit_solution(1945525639712762014)
XLA Ops:
  7.2 5.1 fusion.89
  18.0 5.2 collective-permute-start.12
  24.5 7.7 dot_general.56
  32.2 7.5 copy.45
  126.7 5.1 collective-permute-start.4
  170.5 5.7 fusion.88
  176.2 10.6 %fusion.85 = (f32[3,64,128]{2,1,0:T(8,128)S(1)}, f32[3,32,128]{2,1,0:T(8,128)S(1)}, f32[3,32,64,128]{3,2,1,0:T(8,128)}) fusion(f32[128]{0:T(128)S(1)} %slice_bitcast_fusion, bf16[3,32,64,1152]{3,2,1,0:T(8,128)(2,1)} %slice_dynamic-update-slice_fusion.36, bf16[2,1152,128]{2,1,0:T(8,128)(2,1)S(1)} %copy-done.25, f32[3,32,64,128]{3,2,1,0:T(8,128)S(1)} %bitcast.149, ...), kind=kOutput, calls=%fused_computation.314 | convolution fusion | flops 1815834624 | bytes 20890624 | tf_op jit(solution)/shard_map/dot_general | solution.py:32
  193.5 53.1 %all-reduce.17.cloned.1.call-done = (f32[3,128,128]{2,1,0:T(8,128)}, f32[3,128,128]{2,1,0:T(8,128)}, f32[3,128,128]{2,1,0:T(8,128)}, f32[3,128,128]{2,1,0:T(8,128)}) async-done(((f32[3,128,128]{2,1,0:T(8,128)}, f32[3,128,128]{2,1,0:T(8,128)}, f32[3,128,128]{2,1,0:T(8,128)}, f32[3,128,128]{2,1,0:T(8,128)}), (f32[3,128,128]{2,1,0:T(8,128)}, f32[3,128,128]{2,1,0:T(8,128)}, f32[3,128,128]{2,1,0:T(8,128)}, ...) | async-done | bytes 786448 | tf_op jit(solution)/shard_map/psum | solution.py:86
  253.5 12.2 %fusion.87 = (f32[3,64,128]{2,1,0:T(8,128)S(1)}, f32[3,32,128]{2,1,0:T(8,128)S(1)}, f32[3,32,64,128]{3,2,1,0:T(8,128)}) fusion(f32[3,64,128]{2,1,0:T(8,128)S(1)} %fusion.41, f32[3,32,64,128]{3,2,1,0:T(8,128)S(1)} %copy-done.13, f32[3,32,128]{2,1,0:T(8,128)S(1)} %fusion.61, bf16[3,32,64,1152]{3,2,1,0:T(8,128)(2,1)} %slice_dynamic-update-slice_fusion.24, ...), kind=kOutput, calls=%fused_computation.316 | convolution fusion | flops 1821339648 | bytes 21037056 | tf_op jit(solution)/shard_map/dot_general | solution.py:32
  266.7 6.6 fusion.84
  297.0 5.7 collective-permute-start.30
  313.1 32.7 %all-reduce.15.cloned.1.call-done = (f32[3,128,128]{2,1,0:T(8,128)}, f32[3,128,128]{2,1,0:T(8,128)}, f32[3,128,128]{2,1,0:T(8,128)}, f32[3,128,128]{2,1,0:T(8,128)}) async-done(((f32[3,128,128]{2,1,0:T(8,128)}, f32[3,128,128]{2,1,0:T(8,128)}, f32[3,128,128]{2,1,0:T(8,128)}, f32[3,128,128]{2,1,0:T(8,128)}), (f32[3,128,128]{2,1,0:T(8,128)}, f32[3,128,128]{2,1,0:T(8,128)}, f32[3,128,128]{2,1,0:T(8,128)}, ...) | async-done | bytes 786448 | tf_op jit(solution)/shard_map/psum | solution.py:86
  349.6 5.2 fusion.82
  397.2 6.5 fusion.86
  403.8 11.7 %fusion.83 = (f32[3,64,128]{2,1,0:T(8,128)S(1)}, f32[3,32,128]{2,1,0:T(8,128)S(1)}, f32[3,32,64,128]{3,2,1,0:T(8,128)}) fusion(f32[3,64,128]{2,1,0:T(8,128)S(1)} %copy-done.46, f32[3,32,128]{2,1,0:T(8,128)S(1)} %copy-done.52, f32[3,32,64,128]{3,2,1,0:T(8,128)S(1)} %bitcast.150, f32[128]{0:T(128)S(1)} %copy-done.55, ...), kind=kOutput, calls=%fused_computation.312 | convolution fusion | flops 1822126080 | bytes 21037568 | tf_op jit(solution)/shard_map/dot_general | solution.py:32
  424.9 56.5 %all-reduce.13.cloned.1.call-done = (f32[3,128,128]{2,1,0:T(8,128)}, f32[3,128,128]{2,1,0:T(8,128)}, f32[3,128,128]{2,1,0:T(8,128)}, f32[3,128,128]{2,1,0:T(8,128)}) async-done(((f32[3,128,128]{2,1,0:T(8,128)}, f32[3,128,128]{2,1,0:T(8,128)}, f32[3,128,128]{2,1,0:T(8,128)}, f32[3,128,128]{2,1,0:T(8,128)}), (f32[3,128,128]{2,1,0:T(8,128)}, f32[3,128,128]{2,1,0:T(8,128)}, f32[3,128,128]{2,1,0:T(8,128)}, ...) | async-done | bytes 786448 | tf_op jit(solution)/shard_map/psum | solution.py:86
  485.1 7.8 fusion.79
  505.7 7.8 convolution_convert_fusion
  541.1 7.3 convolution_bitcast_fusion.3
  548.5 7.5 convolution_bitcast_fusion.2
  565.2 24.7 %reduce-scatter.3.cloned.1.call-done = bf16[256,2048]{1,0:T(8,128)(2,1)} async-done(((bf16[1024,2048]{1,0:T(8,128)(2,1)}), bf16[256,2048]{1,0:T(8,128)(2,1)}) %reduce-scatter.3.cloned.1.call-update) | async-done | bytes 1048592 | tf_op jit(solution)/shard_map/reduce_scatter | solution.py:175
  592.7 41.2 %all-reduce = (f32[128]{0:T(128)}, f32[2,128]{1,0:T(2,128)}) all-reduce(f32[128]{0:T(128)S(1)} %add.360, f32[2,128]{1,0:T(2,128)S(1)} %maximum_add_fusion.1), channel_id=1, replica_groups=mesh['obj'=4,'plane'=4,'tile'=2] {'obj','plane','tile'}, use_global_device_ids=true, to_apply=%region_36.37 | all-reduce | flops 384 | bytes 3072 | tf_op jit(solution)/shard_map/psum | solution.py:184
  641.2 87.1 %all-reduce.11.cloned.1.call-done = f32[2,1152,128]{2,1,0:T(8,128)} async-done(((f32[2,1152,128]{2,1,0:T(8,128)}), f32[2,1152,128]{2,1,0:T(8,128)}) %all-reduce.11.cloned.1.call-update) | async-done | bytes 1179664 | tf_op jit(solution)/shard_map/psum | solution.py:184
  728.3 43.9 %reduce-scatter.5.cloned.1.call-done = f32[32,2048]{1,0:T(8,128)} async-done(((f32[256,2048]{1,0:T(8,128)}), f32[32,2048]{1,0:T(8,128)}) %reduce-scatter.5.cloned.1.call-update) | async-done | bytes 262160 | tf_op jit(solution)/shard_map/reduce_scatter | solution.py:183
  (410 shorter events, 300.9 us)
Async XLA Ops:
  7.2 107.4 %all-reduce.19.cloned.1.call-start = ((), (), s32[]{:S(2)}) async-start(), calls=%async_computation.8 | async-start | bytes 1572864 | tf_op jit(solution)/shard_map/psum | solution.py:86
  13.1 63.3 %collective-permute-start = (bf16[3,1,64,128]{3,2,1,0:T(8,128)(2,1)}, bf16[3,1,64,128]{3,2,1,0:T(8,128)(2,1)}, u32[]{:S(2)}, u32[]{:S(2)}) collective-permute-start(bf16[3,1,64,128]{3,2,1,0:T(8,128)(2,1)} %get-tuple-element.101), channel_id=1, source_target_pairs={{0,2},{2,4},{4,6},{1,3},{3,5},{5,7},{8,10},{10,12},{12,14},{9,11},... | collective-permute-start | bytes 147464 | tf_op jit(solution)/shard_map/ppermute | solution.py:14
  16.1 60.3 %collective-permute-start.1 = (bf16[3,1,64,128]{3,2,1,0:T(8,128)(2,1)}, bf16[3,1,64,128]{3,2,1,0:T(8,128)(2,1)}, u32[]{:S(2)}, u32[]{:S(2)}) collective-permute-start(bf16[3,1,64,128]{3,2,1,0:T(8,128)(2,1)} %get-tuple-element.102), channel_id=1, source_target_pairs={{2,0},{4,2},{6,4},{3,1},{5,3},{7,5},{10,8},{12,10},{14,12},{11,9},... | collective-permute-start | bytes 147464 | tf_op jit(solution)/shard_map/ppermute | solution.py:15
  18.0 52.8 %collective-permute-start.12 = (bf16[3,1,64,128]{3,2,1,0:T(8,128)(2,1)}, bf16[3,1,64,128]{3,2,1,0:T(8,128)(2,1)}, u32[]{:S(2)}, u32[]{:S(2)}) collective-permute-start(bf16[3,1,64,128]{3,2,1,0:T(8,128)(2,1)} %get-tuple-element.105), channel_id=1, source_target_pairs={{0,2},{2,4},{4,6},{1,3},{3,5},{5,7},{8,10},{10,12},{12,14},{9,11},... | collective-permute-start | bytes 147464 | tf_op jit(solution)/shard_map/ppermute | solution.py:14
  23.2 47.7 %collective-permute-start.13 = (bf16[3,1,64,128]{3,2,1,0:T(8,128)(2,1)}, bf16[3,1,64,128]{3,2,1,0:T(8,128)(2,1)}, u32[]{:S(2)}, u32[]{:S(2)}) collective-permute-start(bf16[3,1,64,128]{3,2,1,0:T(8,128)(2,1)} %get-tuple-element.106), channel_id=1, source_target_pairs={{2,0},{4,2},{6,4},{3,1},{5,3},{7,5},{10,8},{12,10},{14,12},{11,9},... | collective-permute-start | bytes 147464 | tf_op jit(solution)/shard_map/ppermute | solution.py:15
  55.0 191.6 %all-reduce.17.cloned.1.call-start = ((), (), s32[]{:S(2)}) async-start(), calls=%async_computation.7 | async-start | bytes 1572864 | tf_op jit(solution)/shard_map/psum | solution.py:86
  77.2 16.9 %collective-permute-start.3 = (bf16[3,34,1,128]{3,2,1,0:T(2,128)(2,1)S(1)}, bf16[3,34,1,128]{3,2,1,0:T(2,128)(2,1)S(1)}, u32[]{:S(2)}, u32[]{:S(2)}) collective-permute-start(bf16[3,34,1,128]{3,2,1,0:T(2,128)(2,1)S(1)} %get-tuple-element.77), channel_id=1, source_target_pairs={{0,1},{2,3},{4,5},{6,7},{8,9},{10,11},{12,13},{14,15},{16,17},{18,... | collective-permute-start | bytes 78344 | tf_op jit(solution)/shard_map/ppermute | solution.py:14
  81.7 12.3 %collective-permute-start.2 = (bf16[3,34,1,128]{3,2,1,0:T(2,128)(2,1)S(1)}, bf16[3,34,1,128]{3,2,1,0:T(2,128)(2,1)S(1)}, u32[]{:S(2)}, u32[]{:S(2)}) collective-permute-start(bf16[3,34,1,128]{3,2,1,0:T(2,128)(2,1)S(1)} %get-tuple-element.78), channel_id=1, source_target_pairs={{1,0},{3,2},{5,4},{7,6},{9,8},{11,10},{13,12},{15,14},{17,16},{19,... | collective-permute-start | bytes 78344 | tf_op jit(solution)/shard_map/ppermute | solution.py:15
  126.7 12.6 %collective-permute-start.4 = (bf16[3,1,64,128]{3,2,1,0:T(8,128)(2,1)S(1)}, bf16[3,1,64,128]{3,2,1,0:T(8,128)(2,1)S(1)}, u32[]{:S(2)}, u32[]{:S(2)}) collective-permute-start(bf16[3,1,64,128]{3,2,1,0:T(8,128)(2,1)S(1)} %get-tuple-element.103), channel_id=1, source_target_pairs={{0,2},{2,4},{4,6},{1,3},{3,5},{5,7},{8,10},{10,12},{12,14},{9,11},... | collective-permute-start | bytes 147464 | tf_op jit(solution)/shard_map/ppermute | solution.py:14
  139.5 13.5 %collective-permute-start.7 = (bf16[3,34,1,128]{3,2,1,0:T(2,128)(2,1)S(1)}, bf16[3,34,1,128]{3,2,1,0:T(2,128)(2,1)S(1)}, u32[]{:S(2)}, u32[]{:S(2)}) collective-permute-start(bf16[3,34,1,128]{3,2,1,0:T(2,128)(2,1)S(1)} %get-tuple-element.81), channel_id=1, source_target_pairs={{1,0},{3,2},{5,4},{7,6},{9,8},{11,10},{13,12},{15,14},{17,16},{19,... | collective-permute-start | bytes 78344 | tf_op jit(solution)/shard_map/ppermute | solution.py:15
  140.8 12.2 %collective-permute-start.6 = (bf16[3,34,1,128]{3,2,1,0:T(2,128)(2,1)S(1)}, bf16[3,34,1,128]{3,2,1,0:T(2,128)(2,1)S(1)}, u32[]{:S(2)}, u32[]{:S(2)}) collective-permute-start(bf16[3,34,1,128]{3,2,1,0:T(2,128)(2,1)S(1)} %get-tuple-element.82), channel_id=1, source_target_pairs={{0,1},{2,3},{4,5},{6,7},{8,9},{10,11},{12,13},{14,15},{16,17},{18,... | collective-permute-start | bytes 78344 | tf_op jit(solution)/shard_map/ppermute | solution.py:14
  187.8 158.1 %all-reduce.15.cloned.1.call-start = ((), (), s32[]{:S(2)}) async-start(), calls=%async_computation.6 | async-start | bytes 1572864 | tf_op jit(solution)/shard_map/psum | solution.py:86
  273.9 13.4 %collective-permute-start.24 = (bf16[3,1,64,128]{3,2,1,0:T(8,128)(2,1)}, bf16[3,1,64,128]{3,2,1,0:T(8,128)(2,1)}, u32[]{:S(2)}, u32[]{:S(2)}) collective-permute-start(bf16[3,1,64,128]{3,2,1,0:T(8,128)(2,1)} %get-tuple-element.93), channel_id=1, source_target_pairs={{0,2},{2,4},{4,6},{1,3},{3,5},{5,7},{8,10},{10,12},{12,14},{9,11},... | collective-permute-start | bytes 147464 | tf_op jit(solution)/shard_map/ppermute | solution.py:14
  277.7 16.3 %collective-permute-start.28 = (bf16[3,1,64,128]{3,2,1,0:T(8,128)(2,1)}, bf16[3,1,64,128]{3,2,1,0:T(8,128)(2,1)}, u32[]{:S(2)}, u32[]{:S(2)}) collective-permute-start(bf16[3,1,64,128]{3,2,1,0:T(8,128)(2,1)} %get-tuple-element.91), channel_id=1, source_target_pairs={{0,2},{2,4},{4,6},{1,3},{3,5},{5,7},{8,10},{10,12},{12,14},{9,11},... | collective-permute-start | bytes 147464 | tf_op jit(solution)/shard_map/ppermute | solution.py:14
  281.8 12.2 %collective-permute-start.29 = (bf16[3,1,64,128]{3,2,1,0:T(8,128)(2,1)}, bf16[3,1,64,128]{3,2,1,0:T(8,128)(2,1)}, u32[]{:S(2)}, u32[]{:S(2)}) collective-permute-start(bf16[3,1,64,128]{3,2,1,0:T(8,128)(2,1)} %get-tuple-element.92), channel_id=1, source_target_pairs={{2,0},{4,2},{6,4},{3,1},{5,3},{7,5},{10,8},{12,10},{14,12},{11,9},... | collective-permute-start | bytes 147464 | tf_op jit(solution)/shard_map/ppermute | solution.py:15
  287.2 194.2 %all-reduce.13.cloned.1.call-start = ((), (), s32[]{:S(2)}) async-start(), calls=%async_computation.5 | async-start | bytes 1572864 | tf_op jit(solution)/shard_map/psum | solution.py:86
  288.1 14.6 %collective-permute-start.27 = (bf16[3,34,1,128]{3,2,1,0:T(2,128)(2,1)S(1)}, bf16[3,34,1,128]{3,2,1,0:T(2,128)(2,1)S(1)}, u32[]{:S(2)}, u32[]{:S(2)}) collective-permute-start(bf16[3,34,1,128]{3,2,1,0:T(2,128)(2,1)S(1)} %get-tuple-element.65), channel_id=1, source_target_pairs={{1,0},{3,2},{5,4},{7,6},{9,8},{11,10},{13,12},{15,14},{17,16},{19,... | collective-permute-start | bytes 78344 | tf_op jit(solution)/shard_map/ppermute | solution.py:15
  289.4 13.3 %collective-permute-start.26 = (bf16[3,34,1,128]{3,2,1,0:T(2,128)(2,1)S(1)}, bf16[3,34,1,128]{3,2,1,0:T(2,128)(2,1)S(1)}, u32[]{:S(2)}, u32[]{:S(2)}) collective-permute-start(bf16[3,34,1,128]{3,2,1,0:T(2,128)(2,1)S(1)} %get-tuple-element.66), channel_id=1, source_target_pairs={{0,1},{2,3},{4,5},{6,7},{8,9},{10,11},{12,13},{14,15},{16,17},{18,... | collective-permute-start | bytes 78344 | tf_op jit(solution)/shard_map/ppermute | solution.py:14
  295.5 226.8 %collective-permute-start.31 = (bf16[3,34,1,128]{3,2,1,0:T(2,128)(2,1)}, bf16[3,34,1,128]{3,2,1,0:T(2,128)(2,1)}, u32[]{:S(2)}, u32[]{:S(2)}) collective-permute-start(bf16[3,34,1,128]{3,2,1,0:T(2,128)(2,1)} %get-tuple-element.61), channel_id=1, source_target_pairs={{1,0},{3,2},{5,4},{7,6},{9,8},{11,10},{13,12},{15,14},{17,16},{19,... | collective-permute-start | bytes 78344 | tf_op jit(solution)/shard_map/ppermute | solution.py:15
  297.0 225.3 %collective-permute-start.30 = (bf16[3,34,1,128]{3,2,1,0:T(2,128)(2,1)}, bf16[3,34,1,128]{3,2,1,0:T(2,128)(2,1)}, u32[]{:S(2)}, u32[]{:S(2)}) collective-permute-start(bf16[3,34,1,128]{3,2,1,0:T(2,128)(2,1)} %get-tuple-element.62), channel_id=1, source_target_pairs={{0,1},{2,3},{4,5},{6,7},{8,9},{10,11},{12,13},{14,15},{16,17},{18,... | collective-permute-start | bytes 78344 | tf_op jit(solution)/shard_map/ppermute | solution.py:14
  366.7 13.4 %collective-permute-start.11 = (bf16[3,34,1,128]{3,2,1,0:T(2,128)(2,1)S(1)}, bf16[3,34,1,128]{3,2,1,0:T(2,128)(2,1)S(1)}, u32[]{:S(2)}, u32[]{:S(2)}) collective-permute-start(bf16[3,34,1,128]{3,2,1,0:T(2,128)(2,1)S(1)} %get-tuple-element.69), channel_id=1, source_target_pairs={{0,1},{2,3},{4,5},{6,7},{8,9},{10,11},{12,13},{14,15},{16,17},{18,... | collective-permute-start | bytes 78344 | tf_op jit(solution)/shard_map/ppermute | solution.py:14
  420.8 169.1 %reduce-scatter.3.cloned.1.call-start = ((), (), s32[]{:S(2)}) async-start(), calls=%async_computation.2 | async-start | bytes 5242880 | tf_op jit(solution)/shard_map/reduce_scatter | solution.py:175
  513.5 214.8 %all-reduce.11.cloned.1.call-start = ((), (), s32[]{:S(2)}) async-start(), calls=%async_computation.4 | async-start | bytes 2359296 | tf_op jit(solution)/shard_map/psum | solution.py:184
  565.1 207.1 %reduce-scatter.5.cloned.1.call-start = ((), (), s32[]{:S(2)}) async-start(), calls=%async_computation.3 | async-start | bytes 2359296 | tf_op jit(solution)/shard_map/reduce_scatter | solution.py:183
  (84 other events, 836.7 us)
Sparse Core Ops, SparseCore 0:
  55.1 59.0 all-reduce.18
  187.9 58.6 all-reduce.16
  287.3 58.4 all-reduce.14
  420.9 60.4 all-reduce.12
  513.6 76.1 reduce-scatter.2
  595.7 132.5 all-reduce.10
  732.1 40.0 reduce-scatter.4
where the time goes:
time: 792 us; the launch traced here: 782 us
  waiting for transfers between devices  298 us (38%)
  local copies, waits for them, and re-layouts  158 us (20%)
  matrix products  98.1 us (12%)
  other arithmetic  86.1 us (11%)
  starting transfers between devices  83.6 us (11%)
  blocking collectives  41.2 us (5%)
  between operations  16.5 us (2%)
    psum x4, waiting for transfers between devices, pooled_sums(): result = lax.psum((row_full, col_full), ('plane', 'tile'))  142 us
    psum x1, waiting for transfers between devices, per_device(): lax.psum((kernel_sum, conv_bias_sum, bias_grad), ('obj', 'plane', 'tile'))  87.1 us
    unnamed x184, local copies, waits for them, and re-layouts  71.8 us
    ppermute x16, starting transfers between devices, padded_2(): before = lax.ppermute(last, axis, up)  61.8 us
    dot_general x6, matrix products, convolve(): jnp.dot(gathered.reshape(-1, gathered.shape[-1]), kernel, preferred_eleme...  53.3 us
    reduce_scatter x1, waiting for transfers between devices, per_device(): lax.psum_scatter(object_part, ('plane', 'tile'), scatter_dimension=0, til...  43.9 us
    psum x1, blocking collectives, per_device(): lax.psum((kernel_sum, conv_bias_sum, bias_grad), ('obj', 'plane', 'tile'))  41.2 us
    concatenate x16, other arithmetic, padded_2(): array = jnp.concatenate([before, array, after], axis=dim)  27 us
  transfers between devices with their start and end apart: 39, of which 6 were waited for; matrix products, arithmetic and copies ran while one was open for 32% of the time, Pallas kernels for 0%

commit v1 on v0

v1 whole, which is shorter than its diff:
```python
import functools

import jax
import jax.numpy as jnp
from jax import lax
from jax.experimental import pallas as pl
from jax.experimental.pallas import tpu as pltpu
from jax.sharding import PartitionSpec as P

BANDS = ("plane", "tile")
EVERY = ("obj", "plane", "tile")
CONV_DIMS = ("NHWC", "HWIO", "NHWC")
BF = jnp.bfloat16
F32 = jnp.float32


def shifted(array, axis, step):
    size = lax.axis_size(axis)
    pairs = [(i, i + step) for i in range(size) if 0 <= i + step < size]
    return lax.ppermute(array, axis, pairs)


def grow_dim(tok, grad, axis, dim, tok_rim, grad_rim):
    planes, lanes = tok.shape[0], grad.shape[-1]

    def cut(array, rim, last):
        length = array.shape[dim]
        start = length - rim if last else 0
        return lax.slice_in_dim(array, start, start + rim, axis=dim)

    def pack(last):
        parts = [cut(tok, tok_rim, last), cut(grad, grad_rim, last)]
        return jnp.concatenate([part.reshape(planes, -1, lanes) for part in parts], 1)

    def unpack(packed):
        shapes = [cut(tok, tok_rim, False).shape, cut(grad, grad_rim, False).shape]
        rows = shapes[0][1] * shapes[0][2] * shapes[0][3] // lanes
        return packed[:, :rows].reshape(shapes[0]), packed[:, rows:].reshape(shapes[1])

    before = unpack(shifted(pack(True), axis, 1))
    after = unpack(shifted(pack(False), axis, -1))
    return [
        jnp.concatenate([low, mid, high], axis=dim)
        for low, mid, high in zip(before, (tok, grad), after)
    ]


def band_sums(rows, cols):
    height = rows.shape[1]

    def joined(own, other, axis, step):
        upper = (lax.axis_index(axis) & step) != 0
        return jnp.where(
            upper, jnp.concatenate([other, own], 1), jnp.concatenate([own, other], 1)
        )

    rows, cols = rows.astype(BF), cols.astype(BF)
    for axis in ("tile", "plane"):
        size, step = lax.axis_size(axis), 1
        while step < size:
            height = rows.shape[1]
            other = lax.ppermute(
                jnp.concatenate([rows, cols], 1), axis, [(i, i ^ step) for i in range(size)]
            )
            other_rows, other_cols = other[:, :height], other[:, height:]
            if axis == "tile":
                rows = (rows.astype(F32) + other_rows.astype(F32)).astype(BF)
                cols = joined(cols, other_cols, axis, step)
            else:
                rows = joined(rows, other_rows, axis, step)
                cols = (cols.astype(F32) + other_cols.astype(F32)).astype(BF)
            step *= 2
    return rows.astype(F32), cols.astype(F32)


def spread(row_sum, col_sum, extent, ring, row_start, col_start, height, breadth):
    planes, _, channels = row_sum.shape
    rows = row_sum.reshape(planes // 3, 3, extent, channels) / extent
    cols = col_sum.reshape(planes // 3, 3, extent, channels) / extent
    row_ctx = jnp.stack([rows[:, 1], rows[:, 0], cols[:, 0]], 1)
    col_ctx = jnp.stack([rows[:, 2], cols[:, 2], cols[:, 1]], 1)

    def band(ctx, start, length):
        ctx = jnp.pad(ctx, ((0, 0), (0, 0), (ring, ring), (0, 0)))
        ctx = lax.dynamic_slice_in_dim(ctx, start, length + 2 * ring, 2)
        return ctx.reshape(planes, length + 2 * ring, channels)

    row_band = band(row_ctx, row_start, height)
    col_band = band(col_ctx, col_start, breadth)
    return row_band[:, :, None, :] + col_band[:, None, :, :]


def inside(ring, extent, row_start, col_start, height, breadth):
    row = row_start - ring + lax.iota(jnp.int32, height + 2 * ring)
    col = col_start - ring + lax.iota(jnp.int32, breadth + 2 * ring)
    row_ok = (row >= 0) & (row < extent)
    col_ok = (col >= 0) & (col < extent)
    return (row_ok[:, None] & col_ok[None, :])[None, :, :, None]


def conv(padded, kernel):
    return lax.conv_general_dilated(
        padded, kernel, (1, 1), "VALID", dimension_numbers=CONV_DIMS, preferred_element_type=F32
    )


def kernel_gradient(padded, grad):
    return lax.conv_general_dilated(
        padded,
        grad,
        (1, 1),
        "VALID",
        dimension_numbers=("CHWN", "IHWO", "HWNC"),
        preferred_element_type=F32,
    )


def trim(array, ring):
    return array[:, ring:-ring, ring:-ring, :]


def slope(pre):
    sig = jax.nn.sigmoid(pre)
    return sig * (1.0 + pre * (1.0 - sig))


def scattered(parts, axes):
    return jnp.sum(lax.all_to_all(parts, axes, 0, 0, tiled=True).astype(F32), 0)


def scatter_all(blocks, sizes):
    objs, bands = sizes
    blocks = blocks.astype(BF).reshape((objs, bands) + blocks.shape[1:])
    blocks = jnp.moveaxis(blocks, 1, 0)
    part = scattered(blocks, BANDS).astype(BF)
    return scattered(part, "obj")


def call(kernel, planes, ins, outs, scratch=(), flops=0):
    def spec(shape, shared):
        if shared:
            return pl.BlockSpec(shape, lambda p: (0,) * len(shape))
        return pl.BlockSpec((None,) + shape[1:], lambda p: (p,) + (0,) * (len(shape) - 1))

    moved = sum(a.size * a.dtype.itemsize for a, _ in ins)
    return pl.pallas_call(
        kernel,
        grid=(planes,),
        in_specs=[spec(a.shape, shared) for a, shared in ins],
        out_specs=[spec(shape, shared) for shape, _, shared in outs],
        out_shape=[jax.ShapeDtypeStruct(shape, dtype) for shape, dtype, _ in outs],
        scratch_shapes=list(scratch),
        compiler_params=pltpu.CompilerParams(
            dimension_semantics=("arbitrary",), vmem_limit_bytes=60 << 20
        ),
        cost_estimate=pl.CostEstimate(
            flops=flops * planes, bytes_accessed=2 * moved, transcendentals=0
        ),
    )(*[a for a, _ in ins])


def span(row, width, rows=1):
    return pl.ds(pl.multiple_of(row * width, 16), rows * width)


def span8(start, size):
    return pl.ds(pl.multiple_of(start, 8), size)


def loop(rows, body, carry=None, unroll=2):
    return lax.fori_loop(0, rows, body, carry, unroll=unroll)


def convolve_rows(src, base, kernel_ref, prod, rows_out, width, chunks, finish, carry):
    step = rows_out // chunks
    size = step * width

    def chunk(index, carry):
        start = base + index * step
        lhs = jnp.concatenate([src[span(start + dy, width, step), :] for dy in range(3)], 1)
        prod[pl.ds(8, size), :] = jnp.dot(lhs, kernel_ref[...], preferred_element_type=F32)
        channels = prod.shape[1] // 3

        def row(r, carry):
            view = prod.at[span8(r * width, width + 16), :]
            value = (
                view[7 : 7 + width, :channels]
                + view[8 : 8 + width, channels : 2 * channels]
                + view[9 : 9 + width, 2 * channels :]
            )
            return finish(index * step + r, value, carry)

        return loop(step, row, carry)

    return lax.fori_loop(0, chunks, chunk, carry)


def upsample_kernel(dims, tok_ref, ring_ref, weight_ref, raw_ref, sums_ref):
    tok_rows, tok_cols, up, height, breadth, width, channels = dims
    edge = (width - breadth) // 2
    cut = up * channels
    for a in range(up):
        weight = weight_ref[:, a * cut : (a + 1) * cut]
        prod = jnp.dot(tok_ref[...], weight, preferred_element_type=F32)
        rim = jnp.dot(ring_ref[...], weight, preferred_element_type=F32)
        for b in range(up):
            lanes = slice(b * channels, (b + 1) * channels)
            for i in range(tok_rows):
                at = (2 + up * i + a) * width + edge + b
                raw_ref[pl.ds(at, tok_cols, stride=up), :] = prod[
                    i * tok_cols : (i + 1) * tok_cols, lanes
                ]
            if a >= up - 2:
                at = (a - up + 2) * width + edge + b
                raw_ref[pl.ds(at, tok_cols, stride=up), :] = rim[:tok_cols, lanes]
            if a < 2:
                at = (2 + height + a) * width + edge + b
                raw_ref[pl.ds(at, tok_cols, stride=up), :] = rim[tok_cols : 2 * tok_cols, lanes]
            first = 0 if a >= up - 2 else 1
            row = up * first + a - up + 2
            count = tok_rows + 1 if a >= up - 2 or a < 2 else tok_rows
            for side in range(2):
                at = 2 * tok_cols + side * (tok_rows + 2) + first
                column = edge - up + b if side == 0 else edge + breadth + b
                if (b >= up - 2) if side == 0 else (b < 2):
                    raw_ref[pl.ds(row * width + column, count, stride=up * width), :] = rim[
                        at : at + count, lanes
                    ]

    def add(r, total):
        own = raw_ref[span8((r + 2) * width + edge, breadth), :]
        sums_ref[pl.ds(r, 1), :] = jnp.sum(own, 0, keepdims=True)
        return total + own

    sums_ref[pl.ds(height, breadth), :] = loop(height, add, jnp.zeros((breadth, channels), F32))


def forward_kernel(
    dims, raw_ref, row_ref, col_ref, rok_ref, cok_ref, kernel_ref,
    act_ref, slope_ref, next_ref, sums_ref, prod,
):
    height, breadth, width = dims
    edge = (width - breadth) // 2

    def activate(r, carry):
        pre = raw_ref[span(r, width), :] + row_ref[pl.ds(r, 1), :] + col_ref[...]
        sig = 0.5 * jnp.tanh(0.5 * pre) + 0.5
        ok = cok_ref[...] * rok_ref[pl.ds(r, 1), :] > 0.5
        act_ref[span(r, width), :] = jnp.where(ok, pre * sig, 0.0).astype(BF)
        slope_ref[span(r, width), :] = (sig * (1.0 + pre * (1.0 - sig))).astype(BF)
        return carry

    loop(height + 4, activate, 0)
    zero = jnp.zeros((breadth, sums_ref.shape[1]), F32)

    def finish(r, value, total):
        value = raw_ref[span(r + 1, width), :] + value
        next_ref[span(r, width), :] = value
        own = value[edge : edge + breadth]
        inner = (r >= 1) & (r <= height)

        @pl.when(inner)
        def _():
            sums_ref[pl.ds(r - 1, 1), :] = jnp.sum(own, 0, keepdims=True)

        return total + jnp.where(inner, own, 0.0)

    sums_ref[pl.ds(height, breadth), :] = convolve_rows(
        act_ref, 0, kernel_ref, prod, height + 2, width, 2, finish, zero
    )


def adjoint_kernel(
    dims, own_ref, above_ref, below_ref, left_ref, right_ref, kernel_ref, wide_ref, out_ref, prod
):
    height, breadth, width = dims
    edge = (width - breadth) // 2

    def place(r, center):
        row = [left_ref[span8(r * edge, edge), :], center, right_ref[span8(r * edge, edge), :]]
        wide_ref[span(r, width), :] = jnp.concatenate(row, 0).astype(BF)

    for r in range(2):
        place(r, above_ref[r * breadth : (r + 1) * breadth, :].astype(F32))
        place(r + 2 + height, below_ref[r * breadth : (r + 1) * breadth, :].astype(F32))

    def fill(r, carry):
        place(r + 2, own_ref[span(r, breadth), :].astype(F32))
        return carry

    loop(height, fill, 0)

    def finish(r, value, carry):
        out_ref[span(r, width), :] = value
        return carry

    convolve_rows(wide_ref, 0, kernel_ref, prod, height + 2, width, 2, finish, 0)


def context_kernel(dims, ring, side, start_ref, parts_ref, bias_ref, row_ref, col_ref, rows, cols):
    height, breadth, _ = dims
    bands, planes = parts_ref.shape[:2]
    extent = rows.shape[1] - 16
    down, across = extent // height, extent // breadth
    rows[...] = jnp.zeros(rows.shape, F32)
    cols[...] = jnp.zeros(cols.shape, F32)
    scale = 1.0 / extent
    for first in range(0, planes, 3):
        for q in range(3):
            part = lambda p, t, at, size: parts_ref[p * across + t, first + q, at : at + size, :].astype(F32)
            for p in range(down):
                pieces = [part(p, t, 0, height) for t in range(across)]
                rows[q, 8 + p * height : 8 + (p + 1) * height, :] = scale * sum(pieces)
            for t in range(across):
                pieces = [part(p, t, height, breadth) for p in range(down)]
                cols[q, 8 + t * breadth : 8 + (t + 1) * breadth, :] = scale * sum(pieces)
        row_at = span8(start_ref[0], height + 16)
        col_at = span8(start_ref[1], breadth + 16)
        for q, (ref, other) in enumerate(((rows, 1), (rows, 0), (cols, 0))):
            view = ref.at[other, row_at, :]
            row_ref[first + q] = view[8 - ring : 8 + height + ring, :] + 2.0 * bias_ref[...]
        for q, (ref, other) in enumerate(((rows, 2), (cols, 2), (cols, 1))):
            view = ref.at[other, col_at, :]
            col_ref[first + q] = view[8 - side : 8 + breadth + side, :] + bias_ref[...]


def middle_kernel(
    dims, hid_ref, adj_ref, grad_ref, row_ref, col_ref, rok_ref, cok_ref,
    act_ref, next_ref, sums_ref,
):
    height, breadth, width = dims
    edge = (width - breadth) // 2

    def one(r, total):
        pre = hid_ref[span(r, width), :] + row_ref[pl.ds(r, 1), :] + col_ref[...]
        sig = 0.5 * jnp.tanh(0.5 * pre) + 0.5
        ok = cok_ref[...] * rok_ref[pl.ds(r, 1), :] > 0.5
        act_ref[span(r, width), :] = jnp.where(ok, pre * sig, 0.0).astype(BF)
        dz = adj_ref[span(r, width), :] * (sig * (1.0 + pre * (1.0 - sig)))
        next_ref[span(r, width), :] = grad_ref[span(r + 1, width), :].astype(F32) + dz
        own = dz[edge : edge + breadth]
        inner = (r >= 1) & (r <= height)

        @pl.when(inner)
        def _():
            sums_ref[pl.ds(r - 1, 1), :] = jnp.sum(own, 0, keepdims=True)

        return total + jnp.where(inner, own, 0.0)

    sums_ref[pl.ds(height, breadth), :] = loop(height + 2, one, jnp.zeros((breadth, sums_ref.shape[1]), F32))


def backward_kernel(
    dims, part_ref, slope_ref, row_ref, col_ref, rok_ref, cok_ref, kernel_ref,
    grad_ref, next_ref, sums_ref, bias_ref, prod,
):
    height, breadth, width = dims
    edge = (width - breadth) // 2

    def full(r):
        return part_ref[span(r, width), :] + row_ref[pl.ds(r, 1), :] + col_ref[...]

    def round_row(r, carry):
        ok = cok_ref[...] * rok_ref[pl.ds(r, 1), :] > 0.5
        grad_ref[span(r, width), :] = jnp.where(ok, full(r), 0.0).astype(BF)
        return carry

    loop(height + 2, round_row, 0)
    zero = jnp.zeros((breadth, sums_ref.shape[1]), F32)

    def finish(r, value, carry):
        total, bias = carry
        dz = value * slope_ref[span(r + 2, width), :].astype(F32)
        own = dz[edge : edge + breadth]
        grad = full(r + 1)[edge : edge + breadth]
        sums_ref[pl.ds(r, 1), :] = jnp.sum(own, 0, keepdims=True)
        next_ref[pl.ds(pl.multiple_of(r * breadth, 16), breadth), :] = grad + own
        return total + own, bias + grad

    total, bias = convolve_rows(
        grad_ref, 0, kernel_ref, prod, height, width, 2, finish, (zero, zero)
    )
    sums_ref[pl.ds(height, breadth), :] = total
    bias_ref[...] = jnp.sum(bias, 0, keepdims=True)


def taps_kernel(dims, part_ref, row_ref, col_ref, tap_ref, bias_ref, full):
    height, breadth, up, channels = dims

    def one(r, total):
        at = pl.ds(pl.multiple_of(r * breadth, 16), breadth)
        value = part_ref[at, :] + row_ref[pl.ds(r, 1), :] + col_ref[...]
        full[at, :] = value
        return total + value

    total = loop(height, one, jnp.zeros(col_ref.shape, F32))
    bias_ref[...] = jnp.sum(total, 0, keepdims=True)
    tok_cols = breadth // up
    for i in range(height // up):
        for a in range(up):
            for b in range(up):
                piece = full[pl.ds((up * i + a) * breadth + b, tok_cols, stride=up), :]
                tap = a * up + b
                tap_ref[
                    i * tok_cols : (i + 1) * tok_cols, tap * channels : (tap + 1) * channels
                ] = piece.astype(BF)


def kernel_grad_kernel(dims, act_base, grad_base, act_ref, grad_ref, out_ref, wide, moved):
    height, breadth, width = dims
    edge = (width - breadth) // 2
    channels = act_ref.shape[1]
    column = lax.broadcasted_iota(jnp.int32, (width, channels), 0)
    ok = (column >= edge) & (column < edge + breadth)
    wide[pl.ds(0, 8), :] = jnp.zeros((8, channels), F32)
    wide[pl.ds(8 + height * width, 8), :] = jnp.zeros((8, channels), F32)

    def fill(r, carry):
        value = grad_ref[span(r + grad_base, width), :].astype(F32)
        wide[span8(r * width + 8, width), :] = jnp.where(ok, value, 0.0)
        return carry

    loop(height, fill, 0)

    def move(r, carry):
        view = wide.at[span8(r * width, width + 16), :]
        for dx in range(3):
            moved[span(r, width), dx * channels : (dx + 1) * channels] = view[
                9 - dx : 9 - dx + width, :
            ].astype(BF)
        return carry

    loop(height, move, 0)

    @pl.when(pl.program_id(0) == 0)
    def _():
        out_ref[...] = jnp.zeros(out_ref.shape, F32)

    chunks = 2
    step = height // chunks

    def chunk(index, carry):
        start = index * step
        lhs = jnp.concatenate(
            [act_ref[span(start + act_base + dy, width, step), :] for dy in range(3)], 1
        )
        out_ref[...] += lax.dot_general(
            lhs,
            moved[span(start, width, step), :],
            (((0,), (0,)), ((), ())),
            preferred_element_type=F32,
        )
        return carry

    lax.fori_loop(0, chunks, chunk, 0)


def plain_pass(tokens, gout, deconv_weight, deconv_bias, conv_kernels, conv_biases):
    objects, _, tok_rows, tok_cols, fan = tokens.shape
    _, _, height, breadth, channels = gout.shape
    planes = 3 * objects
    up = height // tok_rows
    extent = height * lax.axis_size("plane")
    row_start = lax.axis_index("plane") * height
    col_start = lax.axis_index("tile") * breadth
    place = (extent, row_start, col_start, height, breadth)
    ctx_place = (row_start, col_start, height, breadth)

    tok = tokens.reshape(planes, tok_rows, tok_cols, fan)
    grad_top = gout.reshape(planes, height, breadth, channels)
    tok_wide, grad_wide = grow_dim(tok, grad_top, "plane", 1, 1, 2)
    tok_wide, grad_wide = grow_dim(tok_wide, grad_wide, "tile", 2, 1, 2)

    taps = conv_kernels.reshape(2, 3, 3, channels, channels)
    back = taps[:, ::-1, ::-1].transpose(0, 1, 2, 4, 3)

    raw = jnp.dot(tok_wide.reshape(-1, fan), deconv_weight, preferred_element_type=F32)
    raw = raw.reshape(planes, tok_rows + 2, tok_cols + 2, up, up, channels)
    raw = raw.transpose(0, 1, 3, 2, 4, 5)
    raw = raw.reshape(planes, up * (tok_rows + 2), up * (tok_cols + 2), channels)
    raw = trim(raw, up - 2)

    own = trim(raw, 2)
    row0, col0 = band_sums(jnp.sum(own, 2), jnp.sum(own, 1))
    bias = deconv_bias
    pre0 = raw + bias + spread(
        row0 + extent * bias, col0 + extent * bias, extent, 2, *ctx_place
    )
    act0 = jnp.where(inside(2, *place), jax.nn.silu(pre0), 0.0).astype(BF)
    step0 = conv(act0, taps[0])

    own = trim(step0, 1)
    row1, col1 = band_sums(jnp.sum(own, 2), jnp.sum(own, 1))
    bias = deconv_bias + conv_biases[0]
    pre1 = trim(raw, 1) + step0 + bias + spread(
        row0 + row1 + extent * bias, col0 + col1 + extent * bias, extent, 1, *ctx_place
    )
    ok1 = inside(1, *place)
    act1 = jnp.where(ok1, jax.nn.silu(pre1), 0.0).astype(BF)

    dz1 = conv(grad_wide, back[1]) * slope(pre1)
    own = trim(dz1, 1)
    drow1, dcol1 = band_sums(jnp.sum(own, 2), jnp.sum(own, 1))
    kernel1 = kernel_gradient(act1, grad_top)
    cbias1 = jnp.sum(grad_top.astype(F32), (0, 1, 2))
    grad1 = trim(grad_wide, 1).astype(F32) + dz1 + spread(drow1, dcol1, extent, 1, *ctx_place)
    gb1 = jnp.where(ok1, grad1, 0.0).astype(BF)
    own1 = trim(grad1, 1)
    cbias0 = jnp.sum(own1, (0, 1, 2))

    dz0 = conv(gb1, back[0]) * slope(trim(pre0, 2))
    drow0, dcol0 = band_sums(jnp.sum(dz0, 2), jnp.sum(dz0, 1))
    kernel0 = kernel_gradient(trim(act0, 1), trim(gb1, 1))
    grad0 = own1 + dz0 + spread(drow0, dcol0, extent, 0, *ctx_place)
    bias_part = jnp.sum(grad0, (0, 1, 2))

    gb0 = grad0.astype(BF).reshape(planes, tok_rows, up, tok_cols, up, channels)
    tap_grads = gb0.transpose(0, 1, 3, 2, 4, 5).reshape(-1, up * up * channels)
    tok_grad = lax.dot_general(
        tap_grads, deconv_weight, (((1,), (1,)), ((), ())), preferred_element_type=F32
    )
    tok_grad = tok_grad.astype(BF).reshape(tokens.shape)
    weight_part = lax.dot_general(
        tok.reshape(-1, fan), tap_grads, (((0,), (0,)), ((), ())), preferred_element_type=F32
    )
    small = jnp.concatenate(
        [kernel0.reshape(-1, channels), kernel1.reshape(-1, channels)]
        + [v.reshape(1, channels) for v in (cbias0, cbias1, bias_part)],
        0,
    )
    bands = lax.axis_size("plane") * lax.axis_size("tile")
    total = lax.axis_size("obj") * bands
    weight_grad = scatter_all(
        weight_part.reshape(total, fan // total, -1), (lax.axis_size("obj"), bands)
    )
    return (tok_grad, weight_grad) + finish_small(small, conv_kernels.shape[1])


def edges(ring, extent, start, length, side, channels):
    place = lax.iota(jnp.int32, length + 2 * side) - side
    ok = (place >= -ring) & (place < length + ring)
    ok = ok & (start + place >= 0) & (start + place < extent)
    return jnp.broadcast_to(ok[:, None].astype(F32), (length + 2 * side, channels))


def sent_to_all(array, axes):
    copies = jnp.broadcast_to(array[None], (lax.axis_size(axes),) + array.shape)
    return lax.all_to_all(copies, axes, 0, 0, tiled=True)


def finish_small(small, per_kernel):
    rows, channels = small.shape
    bands = lax.axis_size("plane") * lax.axis_size("tile")
    piece = -(-rows // bands)
    piece += -piece % 16
    parts = jnp.pad(small, ((0, piece * bands - rows), (0, 0))).astype(BF)
    part = scattered(parts.reshape(bands, piece, channels), BANDS).astype(BF)
    part = jnp.sum(sent_to_all(part, "obj").astype(F32), 0).astype(BF)
    small = sent_to_all(part, BANDS).reshape(-1, channels).astype(F32)
    kernel_grads = small[: 2 * per_kernel].reshape(2, per_kernel, channels)
    cbias_grads = small[2 * per_kernel : 2 * per_kernel + 2]
    return (small[2 * per_kernel + 2], kernel_grads, cbias_grads)


def bits_of(size):
    steps = []
    while size > 1:
        size //= 2
        steps.append(size)
    return steps


def halved(parts, dim, axis, step):
    upper = ((lax.axis_index(axis) // step) % 2).astype(jnp.int32)
    size = lax.axis_size(axis)
    mine = lax.dynamic_slice_in_dim(parts, upper, 1, dim)
    theirs = lax.dynamic_slice_in_dim(parts, 1 - upper, 1, dim)
    other = lax.ppermute(theirs, axis, [(i, i ^ step) for i in range(size)])
    return (mine.astype(F32) + other.astype(F32)).astype(BF)


def scatter_weight(product, fan, columns):
    objs = lax.axis_size("obj")
    steps = [("plane", s) for s in bits_of(lax.axis_size("plane"))]
    steps += [("tile", s) for s in bits_of(lax.axis_size("tile"))]
    block = fan // (objs * 2 ** len(steps))
    shape = (objs,) + (2,) * len(steps) + (block, columns)
    parts = product.astype(BF).reshape(shape)
    order = list(range(len(steps)))
    near = order.index(len(bits_of(lax.axis_size("plane"))) - 1)
    parts = halved(parts, 1 + near, *steps[near])
    rest = [i for i in order if i != near]
    streams = [parts[: objs // 2], parts[objs // 2 :]]
    for one, two in zip(rest, reversed(rest)):
        streams[0] = halved(streams[0], 1 + one, *steps[one])
        streams[1] = halved(streams[1], 1 + two, *steps[two])
    parts = jnp.concatenate(streams, 0).reshape(objs, block, columns)
    return scattered(parts, "obj")


def kernel_pass(tokens, gout, deconv_weight, deconv_bias, conv_kernels, conv_biases):
    objects, _, tok_rows, tok_cols, fan = tokens.shape
    _, _, height, breadth, channels = gout.shape
    planes = 3 * objects
    up = height // tok_rows
    edge = 8
    width = breadth + 2 * edge
    extent = height * lax.axis_size("plane")
    row_start = lax.axis_index("plane") * height
    col_start = lax.axis_index("tile") * breadth
    dims = (height, breadth, width)

    tok = tokens.reshape(planes, tok_rows, tok_cols, fan)
    grad_top = gout.reshape(planes, height, breadth, channels)
    tok_above, tok_below = shifted(tok[:, -1:], "plane", 1), shifted(tok[:, :1], "plane", -1)
    above, below = shifted(grad_top[:, -2:], "plane", 1), shifted(grad_top[:, :2], "plane", -1)

    def column(parts, last, rim):
        cut = lambda part: part[:, :, -rim:] if last else part[:, :, :rim]
        return jnp.concatenate([cut(part) for part in parts], 1)

    tok_parts, grad_parts = (tok_above, tok, tok_below), (above, grad_top, below)
    tok_left = shifted(column(tok_parts, True, 1), "tile", 1)
    tok_right = shifted(column(tok_parts, False, 1), "tile", -1)
    left = shifted(column(grad_parts, True, 2), "tile", 1)
    right = shifted(column(grad_parts, False, 2), "tile", -1)
    flat_tok = lambda array: array.reshape(planes, -1, fan)
    ring = jnp.concatenate([flat_tok(a) for a in (tok_above, tok_below, tok_left, tok_right)], 1)
    ring = jnp.pad(ring, ((0, 0), (0, -ring.shape[1] % 16), (0, 0)))
    flat_grad = lambda array: array.reshape(planes, -1, channels)
    left = flat_grad(jnp.pad(left, ((0, 0), (0, 0), (edge - 2, 0), (0, 0))).astype(F32))
    right = flat_grad(jnp.pad(right, ((0, 0), (0, 0), (0, edge - 2), (0, 0))).astype(F32))

    taps = conv_kernels.reshape(2, 3, 3, channels, channels)
    side = 3 * channels
    ahead = taps[0].transpose(0, 2, 1, 3).reshape(side, side)
    back = taps[:, ::-1, ::-1].transpose(0, 1, 4, 2, 3).reshape(2, side, side)

    def oks(rim):
        return (
            edges(rim, extent, row_start, height, rim, channels),
            edges(rim, extent, col_start, breadth, edge, channels),
        )

    flat = lambda rows: (planes, rows * width, channels)
    sums = ((planes, height + breadth, channels), F32, False)
    one = ((planes, 1, channels), F32, False)
    prod = lambda rows: pltpu.VMEM((rows * width + 16, side), F32)
    conv_flops = lambda rows: 2 * rows * width * side * side
    starts = jnp.stack([row_start, col_start]).astype(jnp.int32)

    def contexts(parts, rim, pad, bias, beside=None):
        parts = sent_to_all(parts.astype(BF), BANDS)
        if beside is not None:
            parts, beside = lax.optimization_barrier((parts, beside))
        whole = lambda array: pl.BlockSpec(memory_space=pltpu.VMEM)
        shapes = [
            jax.ShapeDtypeStruct((planes, height + 2 * rim, channels), F32),
            jax.ShapeDtypeStruct((planes, breadth + 2 * pad, channels), F32),
        ]
        terms = pl.pallas_call(
            functools.partial(context_kernel, dims, rim, pad),
            in_specs=[pl.BlockSpec(memory_space=pltpu.SMEM), whole(parts), whole(bias)],
            out_specs=[whole(shape) for shape in shapes],
            out_shape=shapes,
            scratch_shapes=[pltpu.VMEM((3, extent + 16, channels), F32)] * 2,
            compiler_params=pltpu.CompilerParams(vmem_limit_bytes=60 << 20),
            cost_estimate=pl.CostEstimate(
                flops=4 * parts.size, bytes_accessed=2 * parts.size, transcendentals=0
            ),
        )(starts, parts, bias.reshape(1, channels))
        return tuple(terms) if beside is None else tuple(terms) + (beside,)

    raw, parts = call(
        functools.partial(
            upsample_kernel, (tok_rows, tok_cols, up, height, breadth, width, channels)
        ),
        planes,
        [(flat_tok(tok), False), (ring, False), (deconv_weight, True)],
        [(flat(height + 4), F32, False), sums],
        flops=2 * 192 * fan * up * up * channels,
    )
    row_ctx, col_ctx = contexts(parts, 2, edge, deconv_bias)
    grad_wide, adjoint = call(
        functools.partial(adjoint_kernel, dims),
        planes,
        [(flat_grad(a), False) for a in (grad_top, above, below)]
        + [(left, False), (right, False), (back[1], True)],
        [(flat(height + 4), BF, False), (flat(height + 2), F32, False)],
        [prod(height // 2 + 1)],
        conv_flops(height + 2),
    )
    row_ok2, col_ok2 = oks(2)
    act0, slope0, hidden, parts = call(
        functools.partial(forward_kernel, dims),
        planes,
        [(raw, False), (row_ctx, False), (col_ctx, False)]
        + [(row_ok2, True), (col_ok2, True), (ahead, True)],
        [(flat(height + 4), BF, False)] * 2 + [(flat(height + 2), F32, False), sums],
        [prod(height // 2 + 1)],
        conv_flops(height + 2),
    )
    row_ctx, col_ctx = contexts(parts, 1, edge, deconv_bias + conv_biases[0])
    row_ok1, col_ok1 = oks(1)
    act1, part1, parts = call(
        functools.partial(middle_kernel, dims),
        planes,
        [(hidden, False), (adjoint, False), (grad_wide, False)]
        + [(row_ctx, False), (col_ctx, False), (row_ok1, True), (col_ok1, True)],
        [(flat(height + 2), BF, False), (flat(height + 2), F32, False), sums],
    )

    def kernel_gradient_of(act, grad, act_base, grad_base):
        (result,) = call(
            functools.partial(kernel_grad_kernel, dims, act_base, grad_base),
            planes,
            [(act, False), (grad, False)],
            [((side, side), F32, True)],
            [
                pltpu.VMEM((height * width + 16, channels), F32),
                pltpu.VMEM((height * width, side), BF),
            ],
            2 * height * width * side * side,
        )
        result = result.reshape(3, channels, 3, channels).transpose(0, 2, 1, 3)
        return result.reshape(-1, channels)

    none = jnp.zeros((channels,), F32)
    kernel1 = kernel_gradient_of(act1, grad_wide, 0, 2)
    row_ctx, col_ctx, kernel1 = contexts(parts, 1, edge, none, kernel1)
    cbias1 = jnp.sum(grad_top.astype(F32), (0, 1, 2))
    gb1, part0, parts, cbias0 = call(
        functools.partial(backward_kernel, dims),
        planes,
        [(part1, False), (slope0, False), (row_ctx, False), (col_ctx, False)]
        + [(row_ok1, True), (col_ok1, True), (back[0], True)],
        [(flat(height + 2), BF, False), ((planes, height * breadth, channels), F32, False)]
        + [sums, one],
        [prod(height // 2)],
        conv_flops(height),
    )
    kernel0 = kernel_gradient_of(act0, gb1, 1, 1)
    row_ctx, col_ctx, kernel0 = contexts(parts, 0, 0, none, kernel0)
    tap_grads, bias_part = call(
        functools.partial(taps_kernel, (height, breadth, up, channels)),
        planes,
        [(part0, False), (row_ctx, False), (col_ctx, False)],
        [((planes, tok_rows * tok_cols, up * up * channels), BF, False), one],
        [pltpu.VMEM((height * breadth, channels), F32)],
    )
    tap_grads = tap_grads.reshape(-1, up * up * channels)
    product = lax.dot_general(
        tok.reshape(-1, fan), tap_grads, (((0,), (0,)), ((), ())), preferred_element_type=F32
    )
    weight_grad = scatter_weight(product, fan, up * up * channels)
    tok_grad = lax.dot_general(
        tap_grads, deconv_weight, (((1,), (1,)), ((), ())), preferred_element_type=F32
    )
    tok_grad = tok_grad.astype(BF).reshape(tokens.shape)
    small = jnp.concatenate(
        [kernel0, kernel1, jnp.sum(cbias0, 0), cbias1[None], jnp.sum(bias_part, 0)], 0
    )
    return (tok_grad, weight_grad) + finish_small(small, conv_kernels.shape[1])


def per_device(tokens, gout, deconv_weight, deconv_bias, conv_kernels, conv_biases):
    channels = gout.shape[-1]
    sizes = [lax.axis_size(axis) for axis in ("obj", "plane", "tile")]
    fits = gout.shape[3] % 16 == 0 and gout.shape[2] % 16 == 0 and channels % 128 == 0
    fits = fits and all(size & (size - 1) == 0 and size > 1 for size in sizes)
    run = kernel_pass if fits else plain_pass
    return run(tokens, gout, deconv_weight, deconv_bias, conv_kernels, conv_biases)


def solution(mesh):
    placed = (
        P("obj", None, "plane", "tile", None),
        P("obj", None, "plane", "tile", None),
        P(),
        P(),
        P(),
        P(),
    )
    return jax.shard_map(
        per_device,
        mesh=mesh,
        in_specs=placed,
        out_specs=(
            P("obj", None, "plane", "tile", None),
            P(EVERY, None),
            P(),
            P(),
            P(),
        ),
        check_vma=False,
    )
```

time: 792 us -> 344 us (0.43); the launches traced: 782 us -> 342 us
  waiting for transfers between devices: 298 us -> 68.7 us
  Pallas kernels: 0 us -> 137 us
  local copies, waits for them, and re-layouts: 158 us -> 43.3 us
  matrix products: 98.1 us -> 10.2 us
  other arithmetic: 86.1 us -> 15.8 us
  blocking collectives: 41.2 us -> 0 us
  starting transfers between devices: 83.6 us -> 65.9 us
  between operations: 16.5 us -> 1.12 us
    psum x5 -> x0, waiting for transfers between devices: 229 us -> none  [the longest x4 142 us: pooled_sums(): result = lax.psum((row_full, col_full), ('plane', 'tile'))]
    pallas_call x0 -> x12, Pallas kernels: none -> 137 us  [the longest x8 128 us: call(): pl.pallas_call(kernel, grid=(planes,), in_specs=[spec(a.shape, shared) fo...]
    dot_general x15 -> x2, matrix products: 98.1 us -> 10.2 us  [the longest x1 5.63 us: kernel_pass(): lax.dot_general(tok.reshape(-1, fan), tap_grads, (((0,), (0,)), ((), ()))...]
    reduce_scatter x2 -> x0, waiting for transfers between devices: 68.6 us -> none  [the longest x1 43.9 us: per_device(): lax.psum_scatter(object_part, ('plane', 'tile'), scatter_dimension=0, til...]
    unnamed x184 -> x34, local copies, waits for them, and re-layouts: 71.8 us -> 10.2 us
    ppermute x32 -> x13, starting transfers between devices: 83 us -> 28.2 us  [the longest x8 22 us: shifted(): return lax.ppermute(array, axis, pairs)]
    psum x1 -> x0, blocking collectives: 41.2 us -> none  [per_device(): lax.psum((kernel_sum, conv_bias_sum, bias_grad), ('obj', 'plane', 'tile'))]
    all_to_all x0 -> x8, starting transfers between devices: none -> 37.7 us  [the longest x6 28.4 us: sent_to_all(): return lax.all_to_all(copies, axes, 0, 0, tiled=True)]
  transfers between devices with their start and end apart: 39 -> 21, of which waited for: 6 -> 10; matrix products, arithmetic and copies ran while one was open for 32% -> 14% of each run, Pallas kernels for 0% -> 25%
where the time goes in v1:
time: 344 us; the launch traced here: 342 us
  Pallas kernels  137 us (40%)
  waiting for transfers between devices  68.7 us (20%)
  starting transfers between devices  65.9 us (19%)
  local copies, waits for them, and re-layouts  43.3 us (13%)
  other arithmetic  15.8 us (5%)
  matrix products  10.2 us (3%)
    pallas_call x8, Pallas kernels, call(): pl.pallas_call(kernel, grid=(planes,), in_specs=[spec(a.shape, shared) fo...  128 us
    all_to_all x6, starting transfers between devices, sent_to_all(): return lax.all_to_all(copies, axes, 0, 0, tiled=True)  28.4 us
    ppermute x5, waiting for transfers between devices, halved(): other = lax.ppermute(theirs, axis, [(i, i ^ step) for i in range(size)])  23.9 us
    ppermute x8, starting transfers between devices, shifted(): return lax.ppermute(array, axis, pairs)  22 us
    all_to_all x2, waiting for transfers between devices, scattered(): return jnp.sum(lax.all_to_all(parts, axes, 0, 0, tiled=True).astype(F32), 0)  20.7 us
    ppermute x8, waiting for transfers between devices, shifted(): return lax.ppermute(array, axis, pairs)  12.8 us
    all_to_all x6, waiting for transfers between devices, sent_to_all(): return lax.all_to_all(copies, axes, 0, 0, tiled=True)  11.2 us
    unnamed x34, local copies, waits for them, and re-layouts  10.2 us
  transfers between devices with their start and end apart: 21, of which 10 were waited for; matrix products, arithmetic and copies ran while one was open for 14% of the time, Pallas kernels for 25%

profile of v1, /device:TPU:0, one launch (start us, length us, event | category | flops | bytes accessed | tf_op | source)
XLA Modules:
  0.0 341.9 jit_solution(16006867140430507091)
XLA Ops:
  3.7 3.8 %collective-permute-start.4 = (bf16[6,2,64,128]{3,2,1,0:T(8,128)(2,1)}, bf16[6,2,64,128]{3,2,1,0:T(8,128)(2,1)}, u32[]{:S(2)}, u32[]{:S(2)}) collective-permute-start(bf16[6,2,64,128]{3,2,1,0:T(8,128)(2,1)} %get-tuple-element.66), channel_id=1, source_target_pairs={{0,2},{2,4},{4,6},{1,3},{3,5},{5,7},{8,10},{10,12},{12,14},{9,11},... | collective-permute-start | bytes 589832 | tf_op jit(solution)/shard_map/ppermute | solution.py:20
  11.2 3.9 %collective-permute-start = (bf16[6,1,16,1024]{3,1,0,2:T(2,128)(2,1)}, bf16[6,1,16,1024]{3,1,0,2:T(2,128)(2,1)S(1)}, u32[]{:S(2)}, u32[]{:S(2)}) collective-permute-start(bf16[6,1,16,1024]{3,1,0,2:T(2,128)(2,1)} %get-tuple-element.71), channel_id=1, source_target_pairs={{0,2},{2,4},{4,6},{1,3},{3,5},{5,7},{8,10},{10,12},{12,14},{9,11},... | collective-permute-start | bytes 589832 | tf_op jit(solution)/shard_map/ppermute | solution.py:20
  22.1 4.6 %collective-permute-start.2 = (bf16[6,10,1,1024]{3,1,0,2:T(8,128)(2,1)S(1)}, bf16[6,10,1,1024]{3,1,0,2:T(8,128)(2,1)S(1)}, u32[]{:S(2)}, u32[]{:S(2)}) collective-permute-start(bf16[6,10,1,1024]{3,1,0,2:T(8,128)(2,1)S(1)} %pad_maximum_fusion), channel_id=1, source_target_pairs={{0,1},{2,3},{4,5},{6,7},{8,9},{10,11},{12,13},{14,15},{16,17},{18,... | collective-permute-start | bytes 368648 | tf_op jit(solution)/shard_map/ppermute | solution.py:20
  30.9 14.6 %shard_map.101 = (f32[6,2880,128]{2,1,0:T(8,128)}, f32[6,96,128]{2,1,0:T(8,128)}) custom-call(bf16[6,128,1024]{2,1,0:T(8,128)(2,1)} %bitcast.86, bf16[6,64,1024]{2,1,0:T(8,128)(2,1)} %fusion.6.ring_ref, bf16[1024,2048]{1,0:T(8,128)(2,1)} %weight_ref.1), custom_call_target="tpu_custom_call" | custom-call | flops 4831838208 | bytes 13107200 | tf_op jit(solution)/shard_map/pallas_call | solution.py:146
  47.7 8.8 %all-to-all-start = ((bf16[8,6,96,128]{3,2,1,0:T(8,128)(2,1)}), bf16[8,6,96,128]{3,2,1,0:T(8,128)(2,1)S(1)}, u32[]{:S(2)}, u32[]{:S(2)}) async-start(bf16[8,6,96,128]{3,2,1,0:T(8,128)(2,1)} %broadcast_in_dim.23), calls=%async_computation | async-start | bytes 2359296 | tf_op jit(solution)/shard_map/all_to_all | solution.py:548
  61.5 11.2 %all-to-all-done.parts_ref = bf16[8,6,96,128]{3,2,1,0:T(8,128)(2,1)S(1)} async-done(((bf16[8,6,96,128]{3,2,1,0:T(8,128)(2,1)}), bf16[8,6,96,128]{3,2,1,0:T(8,128)(2,1)S(1)}, u32[]{:S(2)}, u32[]{:S(2)}) %all-to-all-start) | async-done | bytes 1179680 | tf_op jit(solution)/shard_map/all_to_all | solution.py:548
  77.3 25.2 %shard_map.103 = (bf16[6,2880,128]{2,1,0:T(8,128)(2,1)}, bf16[6,2880,128]{2,1,0:T(8,128)(2,1)}, f32[6,2720,128]{2,1,0:T(8,128)}, f32[6,96,128]{2,1,0:T(8,128)}) custom-call(f32[6,2880,128]{2,1,0:T(8,128)} %get-tuple-element.34.raw_ref, f32[6,36,128]{2,1,0:T(8,128)} %get-tuple-element.36.row_ref, f32[6,80,128]{2,1,0:T(8,128)} %get-tuple-element.37.col_ref, ...), custom_call_target="tpu_custom_call" | custom-call | flops 4812963840 | bytes 19116032 | tf_op jit(solution)/shard_map/pallas_call | solution.py:146
  110.7 4.6 %collective-permute-start.6 = (bf16[6,36,2,128]{3,2,1,0:T(2,128)(2,1)S(1)}, bf16[6,36,2,128]{3,2,1,0:T(2,128)(2,1)S(1)}, u32[]{:S(2)}, u32[]{:S(2)}) collective-permute-start(bf16[6,36,2,128]{3,2,1,0:T(2,128)(2,1)S(1)} %pad_maximum_fusion.2), channel_id=1, source_target_pairs={{0,1},{2,3},{4,5},{6,7},{8,9},{10,11},{12,13},{14,15},{16,17},{18,... | collective-permute-start | bytes 331784 | tf_op jit(solution)/shard_map/ppermute | solution.py:20
  115.3 11.2 %collective-permute-done.7 = bf16[6,36,2,128]{3,2,1,0:T(2,128)(2,1)S(1)} collective-permute-done((bf16[6,36,2,128]{3,2,1,0:T(2,128)(2,1)S(1)}, bf16[6,36,2,128]{3,2,1,0:T(2,128)(2,1)S(1)}, u32[]{:S(2)}, u32[]{:S(2)}) %collective-permute-start.7) | collective-permute-done | bytes 110624 | tf_op jit(solution)/shard_map/ppermute | solution.py:20
  128.5 16.9 %shard_map.104 = (bf16[6,2880,128]{2,1,0:T(8,128)(2,1)}, f32[6,2720,128]{2,1,0:T(8,128)}) custom-call(bf16[6,2048,128]{2,1,0:T(8,128)(2,1)} %bitcast.80, bf16[6,128,128]{2,1,0:T(8,128)(2,1)} %bitcast.13.above_ref, bf16[6,128,128]{2,1,0:T(8,128)(2,1)} %bitcast.14.below_ref, f32[6,288,128]{2,1,0:T(8,128)} %bitcast_convert_fusion.2.left_ref, ...), custom_call_target="tpu_custom_call" | custom-call | flops 4812963840 | bytes 11206656 | tf_op jit(solution)/shard_map/pallas_call | solution.py:146
  149.9 16.9 %shard_map.106 = (bf16[6,2720,128]{2,1,0:T(8,128)(2,1)}, f32[6,2720,128]{2,1,0:T(8,128)}, f32[6,96,128]{2,1,0:T(8,128)}) custom-call(f32[6,2720,128]{2,1,0:T(8,128)} %get-tuple-element.38.hid_ref, f32[6,2720,128]{2,1,0:T(8,128)} %get-tuple-element.39.adj_ref, bf16[6,2880,128]{2,1,0:T(8,128)(2,1)} %get-tuple-element.40.grad_ref, ...), custom_call_target="tpu_custom_call" | custom-call | bytes 43087872 | tf_op jit(solution)/shard_map/pallas_call | solution.py:146
  173.4 13.9 %shard_map.107 = f32[384,384]{1,0:T(8,128)} custom-call(bf16[6,2720,128]{2,1,0:T(8,128)(2,1)} %get-tuple-element.47.act_ref, bf16[6,2880,128]{2,1,0:T(8,128)(2,1)} %get-tuple-element.40.grad_ref), custom_call_target="tpu_custom_call" | custom-call | flops 4529848320 | bytes 17203200 | tf_op jit(solution)/shard_map/pallas_call | solution.py:146
  192.0 19.8 %shard_map.109 = (bf16[6,2720,128]{2,1,0:T(8,128)(2,1)}, f32[6,2048,128]{2,1,0:T(8,128)}, f32[6,96,128]{2,1,0:T(8,128)}, f32[6,1,128]{2,1,0:T(1,128)}) custom-call(f32[6,2720,128]{2,1,0:T(8,128)} %get-tuple-element.44.part_ref, bf16[6,2880,128]{2,1,0:T(8,128)(2,1)} %get-tuple-element.45.slope_ref, f32[6,34,128]{2,1,0:T(8,128)} %get-tuple-element.49.row_ref, ...), custom_call_target="tpu_custom_call" | custom-call | flops 4529848320 | bytes 26966016 | tf_op jit(solution)/shard_map/pallas_call | solution.py:146
  214.0 4.1 %all-to-all-start.3 = ((bf16[8,6,96,128]{3,2,1,0:T(8,128)(2,1)}), bf16[8,6,96,128]{3,2,1,0:T(8,128)(2,1)S(1)}, u32[]{:S(2)}, u32[]{:S(2)}) async-start(bf16[8,6,96,128]{3,2,1,0:T(8,128)(2,1)} %broadcast_in_dim.30), calls=%async_computation.3 | async-start | bytes 2359296 | tf_op jit(solution)/shard_map/all_to_all | solution.py:548
  218.1 14.0 %shard_map.110 = f32[384,384]{1,0:T(8,128)} custom-call(bf16[6,2880,128]{2,1,0:T(8,128)(2,1)} %get-tuple-element.53.act_ref, bf16[6,2720,128]{2,1,0:T(8,128)(2,1)} %get-tuple-element.54.grad_ref), custom_call_target="tpu_custom_call" | custom-call | flops 4529848320 | bytes 17203200 | tf_op jit(solution)/shard_map/pallas_call | solution.py:146
  237.5 6.8 %shard_map.112 = (bf16[6,128,2048]{2,1,0:T(8,128)(2,1)}, f32[6,1,128]{2,1,0:T(1,128)}) custom-call(f32[6,2048,128]{2,1,0:T(8,128)} %get-tuple-element.51.part_ref, f32[6,32,128]{2,1,0:T(8,128)} %get-tuple-element.56.row_ref, f32[6,64,128]{2,1,0:T(8,128)} %get-tuple-element.57.col_ref), custom_call_target="tpu_custom_call" | custom-call | bytes 13172736 | tf_op jit(solution)/shard_map/pallas_call | solution.py:146
  244.3 5.6 %convolution_convert_fusion = bf16[2048,1024]{0,1:T(8,128)(2,1)S(1)} fusion(bf16[768,2048]{1,0:T(8,128)(2,1)} %bitcast.109, bf16[768,1024]{1,0:T(8,128)(2,1)S(1)} %bitcast.87), kind=kOutput, calls=%fused_computation.1 | convolution fusion | flops 3223322624 | bytes 8912896 | tf_op jit(solution)/shard_map/dot_general | solution.py:752
  258.6 4.1 %all-to-all-start.5 = ((bf16[8,304,128]{2,1,0:T(8,128)(2,1)}), bf16[8,304,128]{2,1,0:T(8,128)(2,1)S(1)}, u32[]{:S(2)}, u32[]{:S(2)}) async-start(bf16[8,304,128]{2,1,0:T(8,128)(2,1)} %bitcast.35), calls=%async_computation.5 | async-start | bytes 1245184 | tf_op jit(solution)/shard_map/all_to_all | solution.py:128
  262.8 10.2 %all-to-all-done.5 = bf16[8,304,128]{2,1,0:T(8,128)(2,1)S(1)} async-done(((bf16[8,304,128]{2,1,0:T(8,128)(2,1)}), bf16[8,304,128]{2,1,0:T(8,128)(2,1)S(1)}, u32[]{:S(2)}, u32[]{:S(2)}) %all-to-all-start.5) | async-done | bytes 622624 | tf_op jit(solution)/shard_map/all_to_all | solution.py:128
  273.8 4.9 %all-to-all-start.6 = ((bf16[4,304,128]{2,1,0:T(8,128)(2,1)}), bf16[4,304,128]{2,1,0:T(8,128)(2,1)S(1)}, u32[]{:S(2)}, u32[]{:S(2)}) async-start(bf16[4,304,128]{2,1,0:T(8,128)(2,1)} %broadcast_in_dim.32), calls=%async_computation.6 | async-start | bytes 622592 | tf_op jit(solution)/shard_map/all_to_all | solution.py:548
  284.2 4.5 %convolution_convert_fusion.1 = bf16[768,1024]{1,0:T(8,128)(2,1)} fusion(bf16[768,2048]{1,0:T(8,128)(2,1)S(1)} %bitcast.110, bf16[1024,2048]{1,0:T(8,128)(2,1)S(1)} %copy-done.12), kind=kOutput, calls=%fused_computation.2 | convolution fusion | flops 3222011904 | bytes 8912896 | tf_op jit(solution)/shard_map/dot_general | solution.py:756
  297.9 17.0 %collective-permute-done.9 = bf16[2,1,1,2,32,2048]{5,4,3,2,1,0:T(8,128)(2,1)S(1)} collective-permute-done((bf16[2,1,1,2,32,2048]{5,4,3,2,1,0:T(8,128)(2,1)S(1)}, bf16[2,1,1,2,32,2048]{5,4,3,2,1,0:T(8,128)(2,1)S(1)}, u32[]{:S(2)}, u32[]{:S(2)}) %collective-permute-start.9) | collective-permute-done | bytes 524320 | tf_op jit(solution)/shard_map/ppermute | solution.py:578
  323.2 5.1 %all-to-all-start.4 = ((bf16[4,32,2048]{2,1,0:T(8,128)(2,1)}), bf16[4,32,2048]{2,1,0:T(8,128)(2,1)S(1)}, u32[]{:S(2)}, u32[]{:S(2)}) async-start(bf16[4,32,2048]{2,1,0:T(8,128)(2,1)} %maximum_bitcast_fusion), calls=%async_computation.4 | async-start | bytes 1048576 | tf_op jit(solution)/shard_map/all_to_all | solution.py:128
  330.6 10.5 %all-to-all-done.4 = bf16[4,32,2048]{2,1,0:T(8,128)(2,1)S(1)} async-done(((bf16[4,32,2048]{2,1,0:T(8,128)(2,1)}), bf16[4,32,2048]{2,1,0:T(8,128)(2,1)S(1)}, u32[]{:S(2)}, u32[]{:S(2)}) %all-to-all-start.4) | async-done | bytes 524320 | tf_op jit(solution)/shard_map/all_to_all | solution.py:128
  (137 shorter events, 98.5 us)
Async XLA Ops:
  2.4 58.3 %collective-permute-start.5 = (bf16[6,2,64,128]{3,2,1,0:T(8,128)(2,1)}, bf16[6,2,64,128]{3,2,1,0:T(8,128)(2,1)}, u32[]{:S(2)}, u32[]{:S(2)}) collective-permute-start(bf16[6,2,64,128]{3,2,1,0:T(8,128)(2,1)} %get-tuple-element.65), channel_id=1, source_target_pairs={{2,0},{4,2},{6,4},{3,1},{5,3},{7,5},{10,8},{12,10},{14,12},{11,9},... | collective-permute-start | bytes 589832 | tf_op jit(solution)/shard_map/ppermute | solution.py:20
  3.7 12.7 %copy-start.7 = (bf16[2,1152,128]{2,1,0:T(8,128)(2,1)S(1)}, bf16[2,1152,128]{2,1,0:T(8,128)(2,1)}, u32[]{:S(2)}) copy-start(bf16[2,1152,128]{2,1,0:T(8,128)(2,1)} %param.10) | copy-start | bytes 1769476
  3.7 104.6 %collective-permute-start.4 = (bf16[6,2,64,128]{3,2,1,0:T(8,128)(2,1)}, bf16[6,2,64,128]{3,2,1,0:T(8,128)(2,1)}, u32[]{:S(2)}, u32[]{:S(2)}) collective-permute-start(bf16[6,2,64,128]{3,2,1,0:T(8,128)(2,1)} %get-tuple-element.66), channel_id=1, source_target_pairs={{0,2},{2,4},{4,6},{1,3},{3,5},{5,7},{8,10},{10,12},{12,14},{9,11},... | collective-permute-start | bytes 589832 | tf_op jit(solution)/shard_map/ppermute | solution.py:20
  11.2 8.5 %collective-permute-start = (bf16[6,1,16,1024]{3,1,0,2:T(2,128)(2,1)}, bf16[6,1,16,1024]{3,1,0,2:T(2,128)(2,1)S(1)}, u32[]{:S(2)}, u32[]{:S(2)}) collective-permute-start(bf16[6,1,16,1024]{3,1,0,2:T(2,128)(2,1)} %get-tuple-element.71), channel_id=1, source_target_pairs={{0,2},{2,4},{4,6},{1,3},{3,5},{5,7},{8,10},{10,12},{12,14},{9,11},... | collective-permute-start | bytes 589832 | tf_op jit(solution)/shard_map/ppermute | solution.py:20
  15.1 4.7 %collective-permute-start.1 = (bf16[6,1,16,1024]{3,1,0,2:T(2,128)(2,1)}, bf16[6,1,16,1024]{3,1,0,2:T(2,128)(2,1)}, u32[]{:S(2)}, u32[]{:S(2)}) collective-permute-start(bf16[6,1,16,1024]{3,1,0,2:T(2,128)(2,1)} %get-tuple-element.72), channel_id=1, source_target_pairs={{2,0},{4,2},{6,4},{3,1},{5,3},{7,5},{10,8},{12,10},{14,12},{11,9},... | collective-permute-start | bytes 589832 | tf_op jit(solution)/shard_map/ppermute | solution.py:20
  20.7 7.6 %collective-permute-start.3 = (bf16[6,10,1,1024]{3,1,0,2:T(8,128)(2,1)S(1)}, bf16[6,10,1,1024]{3,1,0,2:T(8,128)(2,1)S(1)}, u32[]{:S(2)}, u32[]{:S(2)}) collective-permute-start(bf16[6,10,1,1024]{3,1,0,2:T(8,128)(2,1)S(1)} %pad_maximum_fusion.1), channel_id=1, source_target_pairs={{1,0},{3,2},{5,4},{7,6},{9,8},{11,10},{13,12},{15,14},{17,16},{19,... | collective-permute-start | bytes 368648 | tf_op jit(solution)/shard_map/ppermute | solution.py:20
  22.1 7.7 %collective-permute-start.2 = (bf16[6,10,1,1024]{3,1,0,2:T(8,128)(2,1)S(1)}, bf16[6,10,1,1024]{3,1,0,2:T(8,128)(2,1)S(1)}, u32[]{:S(2)}, u32[]{:S(2)}) collective-permute-start(bf16[6,10,1,1024]{3,1,0,2:T(8,128)(2,1)S(1)} %pad_maximum_fusion), channel_id=1, source_target_pairs={{0,1},{2,3},{4,5},{6,7},{8,9},{10,11},{12,13},{14,15},{16,17},{18,... | collective-permute-start | bytes 368648 | tf_op jit(solution)/shard_map/ppermute | solution.py:20
  45.5 11.1 %copy-start.8 = (bf16[2,1152,128]{2,1,0:T(8,128)(2,1)S(1)}, bf16[2,1152,128]{2,1,0:T(8,128)(2,1)}, u32[]{:S(2)}) copy-start(bf16[2,1152,128]{2,1,0:T(8,128)(2,1)} %param.10) | copy-start | bytes 1769476
  47.7 25.0 %all-to-all-start = ((bf16[8,6,96,128]{3,2,1,0:T(8,128)(2,1)}), bf16[8,6,96,128]{3,2,1,0:T(8,128)(2,1)S(1)}, u32[]{:S(2)}, u32[]{:S(2)}) async-start(bf16[8,6,96,128]{3,2,1,0:T(8,128)(2,1)} %broadcast_in_dim.23), calls=%async_computation | async-start | bytes 2359296 | tf_op jit(solution)/shard_map/all_to_all | solution.py:548
  104.7 40.6 %all-to-all-start.1 = ((bf16[8,6,96,128]{3,2,1,0:T(8,128)(2,1)}), bf16[8,6,96,128]{3,2,1,0:T(8,128)(2,1)S(1)}, u32[]{:S(2)}, u32[]{:S(2)}) async-start(bf16[8,6,96,128]{3,2,1,0:T(8,128)(2,1)} %broadcast_in_dim.26), calls=%async_computation.1 | async-start | bytes 2359296 | tf_op jit(solution)/shard_map/all_to_all | solution.py:548
  109.2 17.2 %collective-permute-start.7 = (bf16[6,36,2,128]{3,2,1,0:T(2,128)(2,1)S(1)}, bf16[6,36,2,128]{3,2,1,0:T(2,128)(2,1)S(1)}, u32[]{:S(2)}, u32[]{:S(2)}) collective-permute-start(bf16[6,36,2,128]{3,2,1,0:T(2,128)(2,1)S(1)} %pad_maximum_fusion.3), channel_id=1, source_target_pairs={{1,0},{3,2},{5,4},{7,6},{9,8},{11,10},{13,12},{15,14},{17,16},{19,... | collective-permute-start | bytes 331784 | tf_op jit(solution)/shard_map/ppermute | solution.py:20
  110.7 16.7 %collective-permute-start.6 = (bf16[6,36,2,128]{3,2,1,0:T(2,128)(2,1)S(1)}, bf16[6,36,2,128]{3,2,1,0:T(2,128)(2,1)S(1)}, u32[]{:S(2)}, u32[]{:S(2)}) collective-permute-start(bf16[6,36,2,128]{3,2,1,0:T(2,128)(2,1)S(1)} %pad_maximum_fusion.2), channel_id=1, source_target_pairs={{0,1},{2,3},{4,5},{6,7},{8,9},{10,11},{12,13},{14,15},{16,17},{18,... | collective-permute-start | bytes 331784 | tf_op jit(solution)/shard_map/ppermute | solution.py:20
  169.0 19.7 %all-to-all-start.2 = ((bf16[8,6,96,128]{3,2,1,0:T(8,128)(2,1)}), bf16[8,6,96,128]{3,2,1,0:T(8,128)(2,1)S(1)}, u32[]{:S(2)}, u32[]{:S(2)}) async-start(bf16[8,6,96,128]{3,2,1,0:T(8,128)(2,1)} %broadcast_in_dim.29), calls=%async_computation.2 | async-start | bytes 2359296 | tf_op jit(solution)/shard_map/all_to_all | solution.py:548
  214.0 20.3 %all-to-all-start.3 = ((bf16[8,6,96,128]{3,2,1,0:T(8,128)(2,1)}), bf16[8,6,96,128]{3,2,1,0:T(8,128)(2,1)S(1)}, u32[]{:S(2)}, u32[]{:S(2)}) async-start(bf16[8,6,96,128]{3,2,1,0:T(8,128)(2,1)} %broadcast_in_dim.30), calls=%async_computation.3 | async-start | bytes 2359296 | tf_op jit(solution)/shard_map/all_to_all | solution.py:548
  237.5 6.8 %copy-start.6 = (bf16[2,3,8,16,1024]{4,3,2,1,0:T(8,128)(2,1)S(1)}, bf16[2,3,8,16,1024]{4,3,2,1,0:T(8,128)(2,1)}, u32[]{:S(2)}) copy-start(bf16[2,3,8,16,1024]{4,3,2,1,0:T(8,128)(2,1)} %param.6) | copy-start | bytes 4718596
  253.1 25.6 %collective-permute-start.8 = (bf16[4,2,1,2,32,2048]{5,4,3,2,1,0:T(8,128)(2,1)}, bf16[4,2,1,2,32,2048]{5,4,3,2,1,0:T(8,128)(2,1)}, u32[]{:S(2)}, u32[]{:S(2)}) collective-permute-start(bf16[4,2,1,2,32,2048]{5,4,3,2,1,0:T(8,128)(2,1)} %constant_dynamic-slice_fusion.4), channel_id=1, source_target_pairs={{0,2},{2,0},{4,6},{6,4},{1,3},{3,1},{5,7},{7,5},{8,10},{10,8},{12,... | collective-permute-start | bytes 6291464 | tf_op jit(solution)/shard_map/ppermute | solution.py:578
  258.6 14.3 %all-to-all-start.5 = ((bf16[8,304,128]{2,1,0:T(8,128)(2,1)}), bf16[8,304,128]{2,1,0:T(8,128)(2,1)S(1)}, u32[]{:S(2)}, u32[]{:S(2)}) async-start(bf16[8,304,128]{2,1,0:T(8,128)(2,1)} %bitcast.35), calls=%async_computation.5 | async-start | bytes 1245184 | tf_op jit(solution)/shard_map/all_to_all | solution.py:128
  273.8 15.0 %all-to-all-start.6 = ((bf16[4,304,128]{2,1,0:T(8,128)(2,1)}), bf16[4,304,128]{2,1,0:T(8,128)(2,1)S(1)}, u32[]{:S(2)}, u32[]{:S(2)}) async-start(bf16[4,304,128]{2,1,0:T(8,128)(2,1)} %broadcast_in_dim.32), calls=%async_computation.6 | async-start | bytes 622592 | tf_op jit(solution)/shard_map/all_to_all | solution.py:548
  283.0 13.7 %collective-permute-start.11 = (bf16[2,2,1,1,32,2048]{5,4,3,2,1,0:T(8,128)(2,1)}, bf16[2,2,1,1,32,2048]{5,4,3,2,1,0:T(8,128)(2,1)S(1)}, u32[]{:S(2)}, u32[]{:S(2)}) collective-permute-start(bf16[2,2,1,1,32,2048]{5,4,3,2,1,0:T(8,128)(2,1)} %constant_dynamic-slice_fusion.1), channel_id=1, source_target_pairs={{0,1},{1,0},{2,3},{3,2},{4,5},{5,4},{6,7},{7,6},{8,9},{9,8},{10,11... | collective-permute-start | bytes 1572872 | tf_op jit(solution)/shard_map/ppermute | solution.py:578
  289.7 33.5 %all-to-all-start.7 = ((bf16[8,304,128]{2,1,0:T(8,128)(2,1)}), bf16[8,304,128]{2,1,0:T(8,128)(2,1)S(1)}, u32[]{:S(2)}, u32[]{:S(2)}) async-start(bf16[8,304,128]{2,1,0:T(8,128)(2,1)} %broadcast_in_dim.33), calls=%async_computation.7 | async-start | bytes 1245184 | tf_op jit(solution)/shard_map/all_to_all | solution.py:548
  293.3 21.5 %collective-permute-start.9 = (bf16[2,1,1,2,32,2048]{5,4,3,2,1,0:T(8,128)(2,1)S(1)}, bf16[2,1,1,2,32,2048]{5,4,3,2,1,0:T(8,128)(2,1)S(1)}, u32[]{:S(2)}, u32[]{:S(2)}) collective-permute-start(bf16[2,1,1,2,32,2048]{5,4,3,2,1,0:T(8,128)(2,1)S(1)} %constant_dynamic-slice_fusion.3), channel_id=1, source_target_pairs={{0,4},{2,6},{4,0},{6,2},{1,5},{3,7},{5,1},{7,3},{8,12},{10,14},{12... | collective-permute-start | bytes 1572872 | tf_op jit(solution)/shard_map/ppermute | solution.py:578
  296.8 23.2 %collective-permute-start.12 = (bf16[2,1,1,1,32,2048]{5,4,3,2,1,0:T(8,128)(2,1)S(1)}, bf16[2,1,1,1,32,2048]{5,4,3,2,1,0:T(8,128)(2,1)S(1)}, u32[]{:S(2)}, u32[]{:S(2)}) collective-permute-start(bf16[2,1,1,1,32,2048]{5,4,3,2,1,0:T(8,128)(2,1)S(1)} %constant_dynamic-slice_fusion), channel_id=1, source_target_pairs={{0,4},{2,6},{4,0},{6,2},{1,5},{3,7},{5,1},{7,3},{8,12},{10,14},{12... | collective-permute-start | bytes 786440 | tf_op jit(solution)/shard_map/ppermute | solution.py:578
  315.1 7.3 %collective-permute-start.10 = (bf16[2,1,1,1,32,2048]{5,4,3,2,1,0:T(8,128)(2,1)S(1)}, bf16[2,1,1,1,32,2048]{5,4,3,2,1,0:T(8,128)(2,1)S(1)}, u32[]{:S(2)}, u32[]{:S(2)}) collective-permute-start(bf16[2,1,1,1,32,2048]{5,4,3,2,1,0:T(8,128)(2,1)S(1)} %constant_dynamic-slice_fusion.2), channel_id=1, source_target_pairs={{0,1},{1,0},{2,3},{3,2},{4,5},{5,4},{6,7},{7,6},{8,9},{9,8},{10,11... | collective-permute-start | bytes 786440 | tf_op jit(solution)/shard_map/ppermute | solution.py:578
  323.2 17.9 %all-to-all-start.4 = ((bf16[4,32,2048]{2,1,0:T(8,128)(2,1)}), bf16[4,32,2048]{2,1,0:T(8,128)(2,1)S(1)}, u32[]{:S(2)}, u32[]{:S(2)}) async-start(bf16[4,32,2048]{2,1,0:T(8,128)(2,1)} %maximum_bitcast_fusion), calls=%async_computation.4 | async-start | bytes 1048576 | tf_op jit(solution)/shard_map/all_to_all | solution.py:128
  (12 other events, 31.8 us)

commit v2 on v1

--- a/solution.py
+++ b/solution.py
@@ -137,17 +137,29 @@
 
 
 def call(kernel, planes, ins, outs, scratch=(), flops=0):
-    def spec(shape, shared):
-        if shared:
-            return pl.BlockSpec(shape, lambda p: (0,) * len(shape))
-        return pl.BlockSpec((None,) + shape[1:], lambda p: (p,) + (0,) * (len(shape) - 1))
+    def spec(shape, kind):
+        rest = (0,) * (len(shape) - 1)
+        if kind is True:
+            return pl.BlockSpec(shape, lambda p: (0,) + rest)
+        if kind == "copies":
+            return pl.BlockSpec(
+                (shape[0], None) + shape[2:], lambda p: (0, p) + (0,) * (len(shape) - 2)
+            )
+        if kind is False:
+            return pl.BlockSpec((None,) + shape[1:], lambda p: (p,) + rest)
+        first, count = kind
+        if count < 0:
+            return pl.BlockSpec((None,) + shape[1:], lambda p: (p + first,) + rest)
+        return pl.BlockSpec(
+            (None,) + shape[1:], lambda p: (jnp.clip(p - first, 0, count - 1),) + rest
+        )
 
     moved = sum(a.size * a.dtype.itemsize for a, _ in ins)
     return pl.pallas_call(
         kernel,
         grid=(planes,),
-        in_specs=[spec(a.shape, shared) for a, shared in ins],
-        out_specs=[spec(shape, shared) for shape, _, shared in outs],
+        in_specs=[spec(a.shape, kind) for a, kind in ins],
+        out_specs=[spec(shape, kind) for shape, _, kind in outs],
         out_shape=[jax.ShapeDtypeStruct(shape, dtype) for shape, dtype, _ in outs],
         scratch_shapes=list(scratch),
         compiler_params=pltpu.CompilerParams(
@@ -159,6 +171,22 @@
     )(*[a for a, _ in ins])
 
 
+def inside_limits(ring, extent, height, breadth, width):
+    row_start = lax.axis_index("plane") * height
+    col_start = lax.axis_index("tile") * breadth
+    edge = (width - breadth) // 2
+    column = lax.broadcasted_iota(jnp.int32, (width, 128), 0) - edge
+    ok = (column >= -ring) & (column < breadth + ring)
+    ok = ok & (col_start + column >= 0) & (col_start + column < extent)
+    ones = jnp.where(ok, 1.0, 0.0)
+
+    def limit(r):
+        row = row_start + r - ring
+        return jnp.where((row >= 0) & (row < extent), 0.5, 2.0)
+
+    return ones, limit
+
+
 def span(row, width, rows=1):
     return pl.ds(pl.multiple_of(row * width, 16), rows * width)
 
@@ -167,26 +195,30 @@
     return pl.ds(pl.multiple_of(start, 8), size)
 
 
-def loop(rows, body, carry=None, unroll=2):
+def loop(rows, body, carry=None, unroll=4):
     return lax.fori_loop(0, rows, body, carry, unroll=unroll)
 
 
-def convolve_rows(src, base, kernel_ref, prod, rows_out, width, chunks, finish, carry):
+def convolve_rows(
+    src, base, kernel_ref, prod, rows_out, width, chunks, finish, carry, flipped=False
+):
     step = rows_out // chunks
     size = step * width
+    order = (2, 1, 0) if flipped else (0, 1, 2)
 
     def chunk(index, carry):
         start = base + index * step
-        lhs = jnp.concatenate([src[span(start + dy, width, step), :] for dy in range(3)], 1)
+        lhs = jnp.concatenate([src[span(start + dy, width, step), :] for dy in order], 1)
         prod[pl.ds(8, size), :] = jnp.dot(lhs, kernel_ref[...], preferred_element_type=F32)
         channels = prod.shape[1] // 3
 
         def row(r, carry):
             view = prod.at[span8(r * width, width + 16), :]
+            first, _, last = order
             value = (
-                view[7 : 7 + width, :channels]
+                view[7 + first : 7 + first + width, :channels]
                 + view[8 : 8 + width, channels : 2 * channels]
-                + view[9 : 9 + width, 2 * channels :]
+                + view[7 + last : 7 + last + width, 2 * channels :]
             )
             return finish(index * step + r, value, carry)
 
@@ -195,67 +227,93 @@
     return lax.fori_loop(0, chunks, chunk, carry)
 
 
-def upsample_kernel(dims, tok_ref, ring_ref, weight_ref, raw_ref, sums_ref):
-    tok_rows, tok_cols, up, height, breadth, width, channels = dims
-    edge = (width - breadth) // 2
+def send_sums(sums, copies_ref):
+    for copy in range(copies_ref.shape[0]):
+        copies_ref[copy] = sums[...].astype(BF)
+
+
+def place_row(rows, r, slot, center, left_ref, right_ref):
+    side = left_ref.shape[0] // rows // 2
+    at = span8((2 * r + slot) * side, side)
+    return jnp.concatenate([left_ref[at, :], center, right_ref[at, :]], 0)
+
+
+def place_rows(rows, breadth, slot, refs, put):
+    own_ref, above_ref, below_ref, left_ref, right_ref = refs
+
+    def one(r, ref, at):
+        center = ref[at, :].astype(F32)
+        put(r, place_row(rows, r, slot, center, left_ref, right_ref))
+
+    for r in range(2):
+        at = (2 * slot + r) * breadth
+        one(r, above_ref, slice(at, at + breadth))
+        one(rows - 2 + r, below_ref, slice(at, at + breadth))
+
+    def inner(r, carry):
+        one(r + 2, own_ref, span(r, breadth))
+        return carry
+
+    loop(rows - 4, inner, 0)
+
+
+def upsample_kernel(
+    dims, tok_ref, grad_ref, weight_ref,
+    raw_ref, copies_ref, first_ref, last_ref, bias_ref, sums,
+):
+    tok_rows, tok_cols, up, height, breadth, channels = dims
     cut = up * channels
     for a in range(up):
         weight = weight_ref[:, a * cut : (a + 1) * cut]
         prod = jnp.dot(tok_ref[...], weight, preferred_element_type=F32)
-        rim = jnp.dot(ring_ref[...], weight, preferred_element_type=F32)
         for b in range(up):
-            lanes = slice(b * channels, (b + 1) * channels)
             for i in range(tok_rows):
-                at = (2 + up * i + a) * width + edge + b
-                raw_ref[pl.ds(at, tok_cols, stride=up), :] = prod[
-                    i * tok_cols : (i + 1) * tok_cols, lanes
+                raw_ref[pl.ds((up * i + a) * breadth + b, tok_cols, stride=up), :] = prod[
+                    i * tok_cols : (i + 1) * tok_cols, b * channels : (b + 1) * channels
                 ]
-            if a >= up - 2:
-                at = (a - up + 2) * width + edge + b
-                raw_ref[pl.ds(at, tok_cols, stride=up), :] = rim[:tok_cols, lanes]
-            if a < 2:
-                at = (2 + height + a) * width + edge + b
-                raw_ref[pl.ds(at, tok_cols, stride=up), :] = rim[tok_cols : 2 * tok_cols, lanes]
-            first = 0 if a >= up - 2 else 1
-            row = up * first + a - up + 2
-            count = tok_rows + 1 if a >= up - 2 or a < 2 else tok_rows
-            for side in range(2):
-                at = 2 * tok_cols + side * (tok_rows + 2) + first
-                column = edge - up + b if side == 0 else edge + breadth + b
-                if (b >= up - 2) if side == 0 else (b < 2):
-                    raw_ref[pl.ds(row * width + column, count, stride=up * width), :] = rim[
-                        at : at + count, lanes
-                    ]
 
     def add(r, total):
-        own = raw_ref[span8((r + 2) * width + edge, breadth), :]
-        sums_ref[pl.ds(r, 1), :] = jnp.sum(own, 0, keepdims=True)
-        return total + own
-
-    sums_ref[pl.ds(height, breadth), :] = loop(height, add, jnp.zeros((breadth, channels), F32))
+        own = raw_ref[span(r, breadth), :]
+        sums[pl.ds(r, 1), :] = jnp.sum(own, 0, keepdims=True)
+        total, bias = total
+        return total + own, bias + grad_ref[span(r, breadth), :].astype(F32)
+
+    zero = jnp.zeros((breadth, channels), F32)
+    total, bias = loop(height, add, (zero, zero))
+    sums[pl.ds(height, breadth), :] = total
+    bias_ref[...] = jnp.sum(bias, 0, keepdims=True)
+    send_sums(sums, copies_ref)
+    rim = 2 * breadth
+    tail = slice((height - 2) * breadth, height * breadth)
+    for ref, at in ((first_ref, slice(0, rim)), (last_ref, tail)):
+        ref[:rim, :] = grad_ref[at, :]
+        ref[rim:, :] = raw_ref[at, :].astype(BF)
 
 
 def forward_kernel(
-    dims, raw_ref, row_ref, col_ref, rok_ref, cok_ref, kernel_ref,
-    act_ref, slope_ref, next_ref, sums_ref, prod,
+    dims, extent, own_ref, above_ref, below_ref, left_ref, right_ref,
+    row_ref, col_ref, kernel_ref,
+    act_ref, slope_ref, next_ref, copies_ref, raw_ref, prod, sums_ref, mask,
 ):
     height, breadth, width = dims
+    mask[...], limit = inside_limits(2, extent, height, breadth, width)
     edge = (width - breadth) // 2
 
-    def activate(r, carry):
-        pre = raw_ref[span(r, width), :] + row_ref[pl.ds(r, 1), :] + col_ref[...]
+    def activate(r, value):
+        raw_ref[span(r, width), :] = value
+        pre = value + row_ref[pl.ds(r, 1), :] + col_ref[...]
         sig = 0.5 * jnp.tanh(0.5 * pre) + 0.5
-        ok = cok_ref[...] * rok_ref[pl.ds(r, 1), :] > 0.5
+        ok = mask[...] > limit(r)
         act_ref[span(r, width), :] = jnp.where(ok, pre * sig, 0.0).astype(BF)
         slope_ref[span(r, width), :] = (sig * (1.0 + pre * (1.0 - sig))).astype(BF)
-        return carry
-
-    loop(height + 4, activate, 0)
+
+    refs = (own_ref, above_ref, below_ref, left_ref, right_ref)
+    place_rows(height + 4, breadth, 1, refs, activate)
     zero = jnp.zeros((breadth, sums_ref.shape[1]), F32)
 
     def finish(r, value, total):
         value = raw_ref[span(r + 1, width), :] + value
-        next_ref[span(r, width), :] = value
+        next_ref[span(r, width), :] = value.astype(BF)
         own = value[edge : edge + breadth]
         inner = (r >= 1) & (r <= height)
 
@@ -268,36 +326,28 @@
     sums_ref[pl.ds(height, breadth), :] = convolve_rows(
         act_ref, 0, kernel_ref, prod, height + 2, width, 2, finish, zero
     )
+    send_sums(sums_ref, copies_ref)
 
 
 def adjoint_kernel(
     dims, own_ref, above_ref, below_ref, left_ref, right_ref, kernel_ref, wide_ref, out_ref, prod
 ):
     height, breadth, width = dims
-    edge = (width - breadth) // 2
-
-    def place(r, center):
-        row = [left_ref[span8(r * edge, edge), :], center, right_ref[span8(r * edge, edge), :]]
-        wide_ref[span(r, width), :] = jnp.concatenate(row, 0).astype(BF)
-
-    for r in range(2):
-        place(r, above_ref[r * breadth : (r + 1) * breadth, :].astype(F32))
-        place(r + 2 + height, below_ref[r * breadth : (r + 1) * breadth, :].astype(F32))
-
-    def fill(r, carry):
-        place(r + 2, own_ref[span(r, breadth), :].astype(F32))
+
+    def put(r, row):
+        wide_ref[span(r, width), :] = row.astype(BF)
+
+    refs = (own_ref, above_ref, below_ref, left_ref, right_ref)
+    place_rows(height + 4, breadth, 0, refs, put)
+
+    def finish(r, value, carry):
+        out_ref[span(r, width), :] = value.astype(BF)
         return carry
 
-    loop(height, fill, 0)
-
-    def finish(r, value, carry):
-        out_ref[span(r, width), :] = value
-        return carry
-
-    convolve_rows(wide_ref, 0, kernel_ref, prod, height + 2, width, 2, finish, 0)
-
-
-def context_kernel(dims, ring, side, start_ref, parts_ref, bias_ref, row_ref, col_ref, rows, cols):
+    convolve_rows(wide_ref, 0, kernel_ref, prod, height + 2, width, 2, finish, 0, True)
+
+
+def context_kernel(dims, ring, side, parts_ref, bias_ref, row_ref, col_ref, rows, cols):
     height, breadth, _ = dims
     bands, planes = parts_ref.shape[:2]
     extent = rows.shape[1] - 16
@@ -314,8 +364,8 @@
             for t in range(across):
                 pieces = [part(p, t, height, breadth) for p in range(down)]
                 cols[q, 8 + t * breadth : 8 + (t + 1) * breadth, :] = scale * sum(pieces)
-        row_at = span8(start_ref[0], height + 16)
-        col_at = span8(start_ref[1], breadth + 16)
+        row_at = span8(lax.axis_index("plane") * height, height + 16)
+        col_at = span8(lax.axis_index("tile") * breadth, breadth + 16)
         for q, (ref, other) in enumerate(((rows, 1), (rows, 0), (cols, 0))):
             view = ref.at[other, row_at, :]
             row_ref[first + q] = view[8 - ring : 8 + height + ring, :] + 2.0 * bias_ref[...]
@@ -325,19 +375,24 @@
 
 
 def middle_kernel(
-    dims, hid_ref, adj_ref, grad_ref, row_ref, col_ref, rok_ref, cok_ref,
-    act_ref, next_ref, sums_ref,
+    dims, extent, half, hid_ref, adj_low, adj_high, grad_low, grad_high,
+    row_ref, col_ref, act_ref, next_ref, copies_ref, sums_ref, mask,
 ):
     height, breadth, width = dims
+    mask[...], limit = inside_limits(1, extent, height, breadth, width)
+    low = pl.program_id(0) < half
     edge = (width - breadth) // 2
 
     def one(r, total):
-        pre = hid_ref[span(r, width), :] + row_ref[pl.ds(r, 1), :] + col_ref[...]
+        pre = hid_ref[span(r, width), :].astype(F32) + row_ref[pl.ds(r, 1), :] + col_ref[...]
         sig = 0.5 * jnp.tanh(0.5 * pre) + 0.5
-        ok = cok_ref[...] * rok_ref[pl.ds(r, 1), :] > 0.5
+        ok = mask[...] > limit(r)
         act_ref[span(r, width), :] = jnp.where(ok, pre * sig, 0.0).astype(BF)
-        dz = adj_ref[span(r, width), :] * (sig * (1.0 + pre * (1.0 - sig)))
-        next_ref[span(r, width), :] = grad_ref[span(r + 1, width), :].astype(F32) + dz
+        here, after = span(r, width), span(r + 1, width)
+        adj = jnp.where(low, adj_low[here, :].astype(F32), adj_high[here, :].astype(F32))
+        grad = jnp.where(low, grad_low[after, :].astype(F32), grad_high[after, :].astype(F32))
+        dz = adj * (sig * (1.0 + pre * (1.0 - sig)))
+        next_ref[here, :] = (grad + dz).astype(BF)
         own = dz[edge : edge + breadth]
         inner = (r >= 1) & (r <= height)
 
@@ -348,20 +403,22 @@
         return total + jnp.where(inner, own, 0.0)
 
     sums_ref[pl.ds(height, breadth), :] = loop(height + 2, one, jnp.zeros((breadth, sums_ref.shape[1]), F32))
+    send_sums(sums_ref, copies_ref)
 
 
 def backward_kernel(
-    dims, part_ref, slope_ref, row_ref, col_ref, rok_ref, cok_ref, kernel_ref,
-    grad_ref, next_ref, sums_ref, bias_ref, prod,
+    dims, extent, part_ref, slope_ref, row_ref, col_ref, kernel_ref,
+    grad_ref, next_ref, copies_ref, bias_ref, prod, sums_ref, mask,
 ):
     height, breadth, width = dims
+    mask[...], limit = inside_limits(1, extent, height, breadth, width)
     edge = (width - breadth) // 2
 
     def full(r):
-        return part_ref[span(r, width), :] + row_ref[pl.ds(r, 1), :] + col_ref[...]
+        return part_ref[span(r, width), :].astype(F32) + row_ref[pl.ds(r, 1), :] + col_ref[...]
 
     def round_row(r, carry):
-        ok = cok_ref[...] * rok_ref[pl.ds(r, 1), :] > 0.5
+        ok = mask[...] > limit(r)
         grad_ref[span(r, width), :] = jnp.where(ok, full(r), 0.0).astype(BF)
         return carry
 
@@ -374,13 +431,14 @@
         own = dz[edge : edge + breadth]
         grad = full(r + 1)[edge : edge + breadth]
         sums_ref[pl.ds(r, 1), :] = jnp.sum(own, 0, keepdims=True)
-        next_ref[pl.ds(pl.multiple_of(r * breadth, 16), breadth), :] = grad + own
+        next_ref[pl.ds(pl.multiple_of(r * breadth, 16), breadth), :] = (grad + own).astype(BF)
         return total + own, bias + grad
 
     total, bias = convolve_rows(
-        grad_ref, 0, kernel_ref, prod, height, width, 2, finish, (zero, zero)
+        grad_ref, 0, kernel_ref, prod, height, width, 2, finish, (zero, zero), True
     )
     sums_ref[pl.ds(height, breadth), :] = total
+    send_sums(sums_ref, copies_ref)
     bias_ref[...] = jnp.sum(bias, 0, keepdims=True)
 
 
@@ -389,7 +447,7 @@
 
     def one(r, total):
         at = pl.ds(pl.multiple_of(r * breadth, 16), breadth)
-        value = part_ref[at, :] + row_ref[pl.ds(r, 1), :] + col_ref[...]
+        value = part_ref[at, :].astype(F32) + row_ref[pl.ds(r, 1), :] + col_ref[...]
         full[at, :] = value
         return total + value
 
@@ -406,7 +464,7 @@
                 ] = piece.astype(BF)
 
 
-def kernel_grad_kernel(dims, act_base, grad_base, act_ref, grad_ref, out_ref, wide, moved):
+def kernel_grad_kernel(dims, act_base, grad_base, act_ref, grad_ref, rounded_ref, wide, moved, out_ref):
     height, breadth, width = dims
     edge = (width - breadth) // 2
     channels = act_ref.shape[1]
@@ -416,8 +474,13 @@
     wide[pl.ds(8 + height * width, 8), :] = jnp.zeros((8, channels), F32)
 
     def fill(r, carry):
-        value = grad_ref[span(r + grad_base, width), :].astype(F32)
-        wide[span8(r * width + 8, width), :] = jnp.where(ok, value, 0.0)
+        if grad_base is None:
+            value = grad_ref[span(r, breadth), :].astype(F32)
+            rim = jnp.zeros((edge, channels), F32)
+            value = jnp.concatenate([rim, value, rim], 0)
+        else:
+            value = jnp.where(ok, grad_ref[span(r + grad_base, width), :].astype(F32), 0.0)
+        wide[span8(r * width + 8, width), :] = value
         return carry
 
     loop(height, fill, 0)
@@ -444,15 +507,24 @@
         lhs = jnp.concatenate(
             [act_ref[span(start + act_base + dy, width, step), :] for dy in range(3)], 1
         )
-        out_ref[...] += lax.dot_general(
+        result = lax.dot_general(
             lhs,
             moved[span(start, width, step), :],
             (((0,), (0,)), ((), ())),
             preferred_element_type=F32,
         )
+        for tap in range(9):
+            dy, dx = divmod(tap, 3)
+            out_ref[tap * channels : (tap + 1) * channels, :] += result[
+                dy * channels : (dy + 1) * channels, dx * channels : (dx + 1) * channels
+            ]
         return carry
 
     lax.fori_loop(0, chunks, chunk, 0)
+
+    @pl.when(pl.program_id(0) == pl.num_programs(0) - 1)
+    def _():
+        rounded_ref[...] = out_ref[...].astype(BF)
 
 
 def plain_pass(tokens, gout, deconv_weight, deconv_bias, conv_kernels, conv_biases):
@@ -525,22 +597,16 @@
     )
     small = jnp.concatenate(
         [kernel0.reshape(-1, channels), kernel1.reshape(-1, channels)]
-        + [v.reshape(1, channels) for v in (cbias0, cbias1, bias_part)],
+        + [v.reshape(1, channels) for v in (cbias0, cbias1)],
         0,
     )
+    small = small_whole(small_summed(small_parts(small), bias_part))
     bands = lax.axis_size("plane") * lax.axis_size("tile")
     total = lax.axis_size("obj") * bands
     weight_grad = scatter_all(
         weight_part.reshape(total, fan // total, -1), (lax.axis_size("obj"), bands)
     )
-    return (tok_grad, weight_grad) + finish_small(small, conv_kernels.shape[1])
-
-
-def edges(ring, extent, start, length, side, channels):
-    place = lax.iota(jnp.int32, length + 2 * side) - side
-    ok = (place >= -ring) & (place < length + ring)
-    ok = ok & (start + place >= 0) & (start + place < extent)
-    return jnp.broadcast_to(ok[:, None].astype(F32), (length + 2 * side, channels))
+    return (tok_grad, weight_grad) + small_results(small, conv_kernels.shape[1])
 
 
 def sent_to_all(array, axes):
@@ -548,18 +614,31 @@
     return lax.all_to_all(copies, axes, 0, 0, tiled=True)
 
 
-def finish_small(small, per_kernel):
+def small_parts(small):
     rows, channels = small.shape
-    bands = lax.axis_size("plane") * lax.axis_size("tile")
+    bands = lax.axis_size(BANDS)
     piece = -(-rows // bands)
     piece += -piece % 16
     parts = jnp.pad(small, ((0, piece * bands - rows), (0, 0))).astype(BF)
-    part = scattered(parts.reshape(bands, piece, channels), BANDS).astype(BF)
-    part = jnp.sum(sent_to_all(part, "obj").astype(F32), 0).astype(BF)
-    small = sent_to_all(part, BANDS).reshape(-1, channels).astype(F32)
+    return lax.all_to_all(parts.reshape(bands, piece, channels), BANDS, 0, 0, tiled=True)
+
+
+def small_summed(parts, bias_part):
+    piece = jnp.sum(parts.astype(F32), 0)
+    tail = jnp.pad(bias_part[None], ((0, 15), (0, 0)))
+    return sent_to_all(jnp.concatenate([piece, tail], 0).astype(BF), "obj")
+
+
+def small_whole(parts):
+    return sent_to_all(jnp.sum(parts.astype(F32), 0).astype(BF), BANDS)
+
+
+def small_results(parts, per_kernel):
+    channels = parts.shape[-1]
+    small = parts[:, :-16].reshape(-1, channels).astype(F32)
+    bias = jnp.sum(parts[:, -16].astype(F32), 0)
     kernel_grads = small[: 2 * per_kernel].reshape(2, per_kernel, channels)
-    cbias_grads = small[2 * per_kernel : 2 * per_kernel + 2]
-    return (small[2 * per_kernel + 2], kernel_grads, cbias_grads)
+    return (bias, kernel_grads, small[2 * per_kernel : 2 * per_kernel + 2])
 
 
 def bits_of(size):
@@ -579,23 +658,29 @@
     return (mine.astype(F32) + other.astype(F32)).astype(BF)
 
 
-def scatter_weight(product, fan, columns):
+def near_step():
+    return ("plane", 1), 1 + len(bits_of(lax.axis_size("plane"))) - 1
+
+
+def weight_parts(product):
+    fan, columns = product.shape
     objs = lax.axis_size("obj")
+    bits = len(bits_of(lax.axis_size("plane"))) + len(bits_of(lax.axis_size("tile")))
+    shape = (objs,) + (2,) * bits + (fan // (objs * 2**bits), columns)
+    step, dim = near_step()
+    return halved(product.astype(BF).reshape(shape), dim, *step)
+
+
+def weight_scattered(parts):
+    objs = parts.shape[0]
     steps = [("plane", s) for s in bits_of(lax.axis_size("plane"))]
     steps += [("tile", s) for s in bits_of(lax.axis_size("tile"))]
-    block = fan // (objs * 2 ** len(steps))
-    shape = (objs,) + (2,) * len(steps) + (block, columns)
-    parts = product.astype(BF).reshape(shape)
-    order = list(range(len(steps)))
-    near = order.index(len(bits_of(lax.axis_size("plane"))) - 1)
-    parts = halved(parts, 1 + near, *steps[near])
-    rest = [i for i in order if i != near]
+    rest = [(i + 1, step) for i, step in enumerate(steps) if i + 1 != near_step()[1]]
     streams = [parts[: objs // 2], parts[objs // 2 :]]
     for one, two in zip(rest, reversed(rest)):
-        streams[0] = halved(streams[0], 1 + one, *steps[one])
-        streams[1] = halved(streams[1], 1 + two, *steps[two])
-    parts = jnp.concatenate(streams, 0).reshape(objs, block, columns)
-    return scattered(parts, "obj")
+        streams[0] = halved(streams[0], one[0], *one[1])
+        streams[1] = halved(streams[1], two[0], *two[1])
+    return jnp.concatenate(streams, 0).reshape(objs, *parts.shape[-2:])
 
 
 def kernel_pass(tokens, gout, deconv_weight, deconv_bias, conv_kernels, conv_biases):
@@ -612,45 +697,34 @@
 
     tok = tokens.reshape(planes, tok_rows, tok_cols, fan)
     grad_top = gout.reshape(planes, height, breadth, channels)
-    tok_above, tok_below = shifted(tok[:, -1:], "plane", 1), shifted(tok[:, :1], "plane", -1)
-    above, below = shifted(grad_top[:, -2:], "plane", 1), shifted(grad_top[:, :2], "plane", -1)
-
-    def column(parts, last, rim):
-        cut = lambda part: part[:, :, -rim:] if last else part[:, :, :rim]
-        return jnp.concatenate([cut(part) for part in parts], 1)
-
-    tok_parts, grad_parts = (tok_above, tok, tok_below), (above, grad_top, below)
-    tok_left = shifted(column(tok_parts, True, 1), "tile", 1)
-    tok_right = shifted(column(tok_parts, False, 1), "tile", -1)
-    left = shifted(column(grad_parts, True, 2), "tile", 1)
-    right = shifted(column(grad_parts, False, 2), "tile", -1)
     flat_tok = lambda array: array.reshape(planes, -1, fan)
-    ring = jnp.concatenate([flat_tok(a) for a in (tok_above, tok_below, tok_left, tok_right)], 1)
-    ring = jnp.pad(ring, ((0, 0), (0, -ring.shape[1] % 16), (0, 0)))
     flat_grad = lambda array: array.reshape(planes, -1, channels)
-    left = flat_grad(jnp.pad(left, ((0, 0), (0, 0), (edge - 2, 0), (0, 0))).astype(F32))
-    right = flat_grad(jnp.pad(right, ((0, 0), (0, 0), (0, edge - 2), (0, 0))).astype(F32))
+
+    def columns_beside(bands_of, last):
+        def cut(parts):
+            cells = [p[:, :, -2:] if last else p[:, :, :2] for p in parts]
+            return jnp.concatenate([c.astype(BF) for c in cells], 1)
+
+        rim = shifted(jnp.stack([cut(parts) for parts in bands_of], 2), "tile", 1 if last else -1)
+        room = (edge - 2, 0) if last else (0, edge - 2)
+        return flat_grad(jnp.pad(rim, ((0, 0),) * 3 + (room, (0, 0))).astype(F32))
 
     taps = conv_kernels.reshape(2, 3, 3, channels, channels)
     side = 3 * channels
     ahead = taps[0].transpose(0, 2, 1, 3).reshape(side, side)
-    back = taps[:, ::-1, ::-1].transpose(0, 1, 4, 2, 3).reshape(2, side, side)
-
-    def oks(rim):
-        return (
-            edges(rim, extent, row_start, height, rim, channels),
-            edges(rim, extent, col_start, breadth, edge, channels),
-        )
+    back = taps.transpose(0, 1, 4, 2, 3).reshape(2, side, side)
 
     flat = lambda rows: (planes, rows * width, channels)
-    sums = ((planes, height + breadth, channels), F32, False)
+    bands = lax.axis_size(BANDS)
+    copies = ((bands, planes, height + breadth, channels), BF, "copies")
+    sums = pltpu.VMEM((height + breadth, channels), F32)
     one = ((planes, 1, channels), F32, False)
     prod = lambda rows: pltpu.VMEM((rows * width + 16, side), F32)
     conv_flops = lambda rows: 2 * rows * width * side * side
-    starts = jnp.stack([row_start, col_start]).astype(jnp.int32)
+    mask = pltpu.VMEM((width, channels), F32)
 
     def contexts(parts, rim, pad, bias, beside=None):
-        parts = sent_to_all(parts.astype(BF), BANDS)
+        parts = lax.all_to_all(parts, BANDS, 0, 0, tiled=True)
         if beside is not None:
             parts, beside = lax.optimization_barrier((parts, beside))
         whole = lambda array: pl.BlockSpec(memory_space=pltpu.VMEM)
@@ -660,7 +734,7 @@
         ]
         terms = pl.pallas_call(
             functools.partial(context_kernel, dims, rim, pad),
-            in_specs=[pl.BlockSpec(memory_space=pltpu.SMEM), whole(parts), whole(bias)],
+            in_specs=[whole(parts), whole(bias)],
             out_specs=[whole(shape) for shape in shapes],
             out_shape=shapes,
             scratch_shapes=[pltpu.VMEM((3, extent + 16, channels), F32)] * 2,
@@ -668,46 +742,68 @@
             cost_estimate=pl.CostEstimate(
                 flops=4 * parts.size, bytes_accessed=2 * parts.size, transcendentals=0
             ),
-        )(starts, parts, bias.reshape(1, channels))
+        )(parts, bias.reshape(1, channels))
         return tuple(terms) if beside is None else tuple(terms) + (beside,)
 
-    raw, parts = call(
-        functools.partial(
-            upsample_kernel, (tok_rows, tok_cols, up, height, breadth, width, channels)
-        ),
+    rim_rows = ((planes, 4 * breadth, channels), BF, False)
+    raw, parts, first, last, cbias1 = call(
+        functools.partial(upsample_kernel, (tok_rows, tok_cols, up, height, breadth, channels)),
         planes,
-        [(flat_tok(tok), False), (ring, False), (deconv_weight, True)],
-        [(flat(height + 4), F32, False), sums],
-        flops=2 * 192 * fan * up * up * channels,
-    )
-    row_ctx, col_ctx = contexts(parts, 2, edge, deconv_bias)
-    grad_wide, adjoint = call(
-        functools.partial(adjoint_kernel, dims),
+        [(flat_tok(tok), False), (flat_grad(grad_top), False), (deconv_weight, True)],
+        [((planes, height * breadth, channels), F32, False), copies, rim_rows, rim_rows, one],
+        [sums],
+        flops=2 * tok_rows * tok_cols * fan * up * up * channels,
+    )
+    half = planes // 2
+    above, below = shifted(last, "plane", 1), shifted(first, "plane", -1)
+    slots = lambda array: array.reshape(planes, 2, 2, breadth, channels)
+    beyond = (slots(above), slots(below))
+    both = [
+        (beyond[0][:, slot], cells, beyond[1][:, slot])
+        for slot, cells in enumerate((grad_top, raw.reshape(grad_top.shape)))
+    ]
+    left, right = columns_beside(both, True), columns_beside(both, False)
+
+    def adjoint_of(first, count):
+        kind = (first, -count)
+        return call(
+            functools.partial(adjoint_kernel, dims),
+            count,
+            [(flat_grad(grad_top), kind)]
+            + [(array, kind) for array in (above, below, left, right)]
+            + [(back[1], True)],
+            [
+                ((count, (height + 4) * width, channels), BF, False),
+                ((count, (height + 2) * width, channels), BF, False),
+            ],
+            [prod(height // 2 + 1)],
+            conv_flops(height + 2),
+        )
+
+    low = adjoint_of(0, half)
+    row_ctx, col_ctx, low = contexts(parts, 2, edge, deconv_bias, low)
+    act0, slope0, hidden, parts = call(
+        functools.partial(forward_kernel, dims, extent),
         planes,
-        [(flat_grad(a), False) for a in (grad_top, above, below)]
-        + [(left, False), (right, False), (back[1], True)],
-        [(flat(height + 4), BF, False), (flat(height + 2), F32, False)],
-        [prod(height // 2 + 1)],
+        [(raw, False)]
+        + [(array, False) for array in (above, below, left, right)]
+        + [(row_ctx, False), (col_ctx, False)]
+        + [(ahead, True)],
+        [(flat(height + 4), BF, False)] * 2 + [(flat(height + 2), BF, False), copies],
+        [pltpu.VMEM(flat(height + 4)[1:], F32), prod(height // 2 + 1), sums, mask],
         conv_flops(height + 2),
     )
-    row_ok2, col_ok2 = oks(2)
-    act0, slope0, hidden, parts = call(
-        functools.partial(forward_kernel, dims),
+    high = adjoint_of(half, planes - half)
+    row_ctx, col_ctx, high = contexts(parts, 1, edge, deconv_bias + conv_biases[0], high)
+    act1, part1, parts = call(
+        functools.partial(middle_kernel, dims, extent, half),
         planes,
-        [(raw, False), (row_ctx, False), (col_ctx, False)]
-        + [(row_ok2, True), (col_ok2, True), (ahead, True)],
-        [(flat(height + 4), BF, False)] * 2 + [(flat(height + 2), F32, False), sums],
-        [prod(height // 2 + 1)],
-        conv_flops(height + 2),
-    )
-    row_ctx, col_ctx = contexts(parts, 1, edge, deconv_bias + conv_biases[0])
-    row_ok1, col_ok1 = oks(1)
-    act1, part1, parts = call(
-        functools.partial(middle_kernel, dims),
-        planes,
-        [(hidden, False), (adjoint, False), (grad_wide, False)]
-        + [(row_ctx, False), (col_ctx, False), (row_ok1, True), (col_ok1, True)],
-        [(flat(height + 2), BF, False), (flat(height + 2), F32, False), sums],
+        [(hidden, False)]
+        + [(low[1], (0, half)), (high[1], (half, planes - half))]
+        + [(low[0], (0, half)), (high[0], (half, planes - half))]
+        + [(row_ctx, False), (col_ctx, False)],
+        [(flat(height + 2), BF, False), (flat(height + 2), BF, False), copies],
+        [sums, mask],
     )
 
     def kernel_gradient_of(act, grad, act_base, grad_base):
@@ -715,32 +811,36 @@
             functools.partial(kernel_grad_kernel, dims, act_base, grad_base),
             planes,
             [(act, False), (grad, False)],
-            [((side, side), F32, True)],
+            [((9 * channels, channels), BF, True)],
             [
                 pltpu.VMEM((height * width + 16, channels), F32),
                 pltpu.VMEM((height * width, side), BF),
+                pltpu.VMEM((9 * channels, channels), F32),
             ],
             2 * height * width * side * side,
         )
-        result = result.reshape(3, channels, 3, channels).transpose(0, 2, 1, 3)
-        return result.reshape(-1, channels)
+        return result
 
     none = jnp.zeros((channels,), F32)
-    kernel1 = kernel_gradient_of(act1, grad_wide, 0, 2)
+    kernel1 = kernel_gradient_of(act1, flat_grad(grad_top), 0, None)
     row_ctx, col_ctx, kernel1 = contexts(parts, 1, edge, none, kernel1)
-    cbias1 = jnp.sum(grad_top.astype(F32), (0, 1, 2))
     gb1, part0, parts, cbias0 = call(
-        functools.partial(backward_kernel, dims),
+        functools.partial(backward_kernel, dims, extent),
         planes,
         [(part1, False), (slope0, False), (row_ctx, False), (col_ctx, False)]
-        + [(row_ok1, True), (col_ok1, True), (back[0], True)],
-        [(flat(height + 2), BF, False), ((planes, height * breadth, channels), F32, False)]
-        + [sums, one],
-        [prod(height // 2)],
+        + [(back[0], True)],
+        [(flat(height + 2), BF, False), ((planes, height * breadth, channels), BF, False)]
+        + [copies, one],
+        [prod(height // 2), sums, mask],
         conv_flops(height),
     )
     kernel0 = kernel_gradient_of(act0, gb1, 1, 1)
     row_ctx, col_ctx, kernel0 = contexts(parts, 0, 0, none, kernel0)
+    small = small_parts(
+        jnp.concatenate(
+            [kernel0, kernel1] + [jnp.sum(v, 0).astype(BF) for v in (cbias0, cbias1)], 0
+        )
+    )
     tap_grads, bias_part = call(
         functools.partial(taps_kernel, (height, breadth, up, channels)),
         planes,
@@ -749,18 +849,21 @@
         [pltpu.VMEM((height * breadth, channels), F32)],
     )
     tap_grads = tap_grads.reshape(-1, up * up * channels)
+    tap_grads, small = lax.optimization_barrier((tap_grads, small))
     product = lax.dot_general(
         tok.reshape(-1, fan), tap_grads, (((0,), (0,)), ((), ())), preferred_element_type=F32
     )
-    weight_grad = scatter_weight(product, fan, up * up * channels)
+    small = small_summed(small, jnp.sum(bias_part, (0, 1)))
+    parts = weight_parts(product)
     tok_grad = lax.dot_general(
         tap_grads, deconv_weight, (((1,), (1,)), ((), ())), preferred_element_type=F32
     )
     tok_grad = tok_grad.astype(BF).reshape(tokens.shape)
-    small = jnp.concatenate(
-        [kernel0, kernel1, jnp.sum(cbias0, 0), cbias1[None], jnp.sum(bias_part, 0)], 0
-    )
-    return (tok_grad, weight_grad) + finish_small(small, conv_kernels.shape[1])
+    parts, small, tok_grad = lax.optimization_barrier((parts, small, tok_grad))
+    small = small_whole(small)
+    parts, small = lax.optimization_barrier((weight_scattered(parts), small))
+    weight_grad = scattered(parts, "obj")
+    return (tok_grad, weight_grad) + small_results(small, conv_kernels.shape[1])
 
 
 def per_device(tokens, gout, deconv_weight, deconv_bias, conv_kernels, conv_biases):

time: 344 us -> 282 us (0.82)
  waiting for transfers between devices: 68.7 us -> 42.3 us
  local copies, waits for them, and re-layouts: 43.3 us -> 24.3 us
  starting transfers between devices: 65.9 us -> 49.2 us
    all_to_all x0 -> x5, starting transfers between devices: none -> 22.8 us  [the longest x4 19.2 us: contexts(): parts = lax.all_to_all(parts, BANDS, 0, 0, tiled=True)]
    all_to_all x6 -> x2, starting transfers between devices: 28.4 us -> 8.41 us  [sent_to_all(): return lax.all_to_all(copies, axes, 0, 0, tiled=True)]
    ppermute x8 -> x4, starting transfers between devices: 22 us -> 9.56 us  [shifted(): return lax.ppermute(array, axis, pairs)]
    all_to_all x0 -> x5, waiting for transfers between devices: none -> 11.4 us  [the longest x4 9.55 us: contexts(): parts = lax.all_to_all(parts, BANDS, 0, 0, tiled=True)]
    all_to_all x6 -> x2, waiting for transfers between devices: 11.2 us -> 0.7 us  [sent_to_all(): return lax.all_to_all(copies, axes, 0, 0, tiled=True)]
    ppermute x8 -> x4, waiting for transfers between devices: 12.8 us -> 2.95 us  [shifted(): return lax.ppermute(array, axis, pairs)]
    all_to_all x2 -> x1, waiting for transfers between devices: 20.7 us -> 11.2 us  [scattered(): return jnp.sum(lax.all_to_all(parts, axes, 0, 0, tiled=True).astype(F32), 0)]
    ppermute x5, waiting for transfers between devices: 23.9 us -> 16 us  [halved(): other = lax.ppermute(theirs, axis, [(i, i ^ step) for i in range(size)])]
  transfers between devices with their start and end apart: 21 -> 17, of which waited for: 10 -> 9; matrix products, arithmetic and copies ran while one was open for 14% -> 12% of each run, Pallas kernels for 25% -> 20%
where the time goes in v2:
time: 282 us; the launch traced here: 280 us
  Pallas kernels  134 us (48%)
  starting transfers between devices  49.2 us (17%)
  waiting for transfers between devices  42.3 us (15%)
  local copies, waits for them, and re-layouts  24.3 us (9%)
  other arithmetic  15.7 us (6%)
  matrix products  13.5 us (5%)
    pallas_call x9, Pallas kernels, call(): pl.pallas_call(kernel, grid=(planes,), in_specs=[spec(a.shape, kind) for...  125 us
    all_to_all x4, starting transfers between devices, contexts(): parts = lax.all_to_all(parts, BANDS, 0, 0, tiled=True)  19.2 us
    ppermute x5, waiting for transfers between devices, halved(): other = lax.ppermute(theirs, axis, [(i, i ^ step) for i in range(size)])  16 us
    all_to_all x1, waiting for transfers between devices, scattered(): return jnp.sum(lax.all_to_all(parts, axes, 0, 0, tiled=True).astype(F32), 0)  11.2 us
    ppermute x4, starting transfers between devices, shifted(): return lax.ppermute(array, axis, pairs)  9.56 us
    all_to_all x4, waiting for transfers between devices, contexts(): parts = lax.all_to_all(parts, BANDS, 0, 0, tiled=True)  9.55 us
    pallas_call x4, Pallas kernels, contexts(): pl.pallas_call(functools.partial(context_kernel, dims, rim, pad), in_spec...  8.82 us
    unnamed x39, local copies, waits for them, and re-layouts  8.42 us
  transfers between devices with their start and end apart: 17, of which 9 were waited for; matrix products, arithmetic and copies ran while one was open for 12% of the time, Pallas kernels for 20%

profile of v2, /device:TPU:0, one launch (start us, length us, event | category | flops | bytes accessed | tf_op | source)
XLA Modules:
  0.0 280.0 jit_solution(12565219043805043238)
XLA Ops:
  0.6 10.9 %shard_map.101 = (f32[6,2048,128]{2,1,0:T(8,128)}, bf16[8,6,96,128]{3,2,1,0:T(8,128)(2,1)}, bf16[6,256,128]{2,1,0:T(8,128)(2,1)}, bf16[6,256,128]{2,1,0:T(8,128)(2,1)}, f32[6,1,128]{2,1,0:T(1,128)}) custom-call(bf16[6,128,1024]{2,1,0:T(8,128)(2,1)} %bitcast.118, bf16[6,2048,128]{2,1,0:T(8,128)(2,1)} %bitcast.107, bf16[1024,2048]{1,0:T(8,128)(2,1)} %weight_ref.1), custom_call_target="tpu_custom_call" | custom-call | flops 3221225472 | bytes 17825792 | tf_op jit(solution)/shard_map/pallas_call | solution.py:158
  15.3 7.1 %all-to-all-start = ((bf16[8,6,96,128]{3,2,1,0:T(8,128)(2,1)}), bf16[8,6,96,128]{3,2,1,0:T(8,128)(2,1)S(1)}, u32[]{:S(2)}, u32[]{:S(2)}) async-start(bf16[8,6,96,128]{3,2,1,0:T(8,128)(2,1)} %get-tuple-element.55), calls=%async_computation | async-start | bytes 2359296 | tf_op jit(solution)/shard_map/all_to_all | solution.py:727
  22.3 4.9 %convert.21 = bf16[6,2048,128]{2,1,0:T(8,128)(2,1)} convert(f32[6,2048,128]{2,1,0:T(8,128)} %get-tuple-element.52.own_ref) | non-fusion elementwise | flops 1572864 | bytes 9437184 | tf_op jit(solution)/shard_map/convert.10
  33.9 4.6 %collective-permute-start.2 = (bf16[6,36,2,2,128]{4,3,1,0,2:T(2,128)(2,1)S(1)}, bf16[6,36,2,2,128]{4,3,1,0,2:T(2,128)(2,1)S(1)}, u32[]{:S(2)}, u32[]{:S(2)}) collective-permute-start(bf16[6,36,2,2,128]{4,3,1,0,2:T(2,128)(2,1)S(1)} %pad_maximum_fusion), channel_id=1, source_target_pairs={{0,1},{2,3},{4,5},{6,7},{8,9},{10,11},{12,13},{14,15},{16,17},{18,... | collective-permute-start | bytes 663560 | tf_op jit(solution)/shard_map/ppermute | solution.py:20
  46.8 10.8 %shard_map.102 = (bf16[3,2880,128]{2,1,0:T(8,128)(2,1)}, bf16[3,2720,128]{2,1,0:T(8,128)(2,1)}) custom-call(bf16[6,2048,128]{2,1,0:T(8,128)(2,1)} %bitcast.109, bf16[6,256,128]{2,1,0:T(8,128)(2,1)} %copy-done.9, bf16[6,256,128]{2,1,0:T(8,128)(2,1)} %copy-done.10, f32[6,576,128]{2,1,0:T(8,128)} %bitcast.92, f32[6,576,128]{2,1,0:T(8,128)} %bitcast_convert_fusion.right_ref, ...), custom_call_target="tpu_custom_call" | custom-call | flops 2406481920 | bytes 15532032 | tf_op jit(solution)/shard_map/pallas_call | solution.py:158
  60.8 25.4 %shard_map.104 = (bf16[6,2880,128]{2,1,0:T(8,128)(2,1)}, bf16[6,2880,128]{2,1,0:T(8,128)(2,1)}, bf16[6,2720,128]{2,1,0:T(8,128)(2,1)}, bf16[8,6,96,128]{3,2,1,0:T(8,128)(2,1)}) custom-call(f32[6,2048,128]{2,1,0:T(8,128)} %get-tuple-element.52.own_ref, bf16[6,256,128]{2,1,0:T(8,128)(2,1)} %copy-done.9, bf16[6,256,128]{2,1,0:T(8,128)(2,1)} %copy-done.10, ...), custom_call_target="tpu_custom_call" | custom-call | flops 4812963840 | bytes 22536192 | tf_op jit(solution)/shard_map/pallas_call | solution.py:158
  86.2 4.8 %all-to-all-start.1 = ((bf16[8,6,96,128]{3,2,1,0:T(8,128)(2,1)}), bf16[8,6,96,128]{3,2,1,0:T(8,128)(2,1)S(1)}, u32[]{:S(2)}, u32[]{:S(2)}) async-start(bf16[8,6,96,128]{3,2,1,0:T(8,128)(2,1)} %get-tuple-element.63), calls=%async_computation.1 | async-start | bytes 2359296 | tf_op jit(solution)/shard_map/all_to_all | solution.py:727
  91.6 10.8 %shard_map.105 = (bf16[3,2880,128]{2,1,0:T(8,128)(2,1)}, bf16[3,2720,128]{2,1,0:T(8,128)(2,1)}) custom-call(bf16[6,2048,128]{2,1,0:T(8,128)(2,1)} %bitcast.110, bf16[6,256,128]{2,1,0:T(8,128)(2,1)} %copy-done.9, bf16[6,256,128]{2,1,0:T(8,128)(2,1)} %copy-done.10, f32[6,576,128]{2,1,0:T(8,128)} %bitcast.94, f32[6,576,128]{2,1,0:T(8,128)} %bitcast_convert_fusion.right_ref, ...), custom_call_target="tpu_custom_call" | custom-call | flops 2406481920 | bytes 15532032 | tf_op jit(solution)/shard_map/pallas_call | solution.py:158
  102.4 4.9 %all-to-all-done.1.parts_ref = bf16[8,6,96,128]{3,2,1,0:T(8,128)(2,1)S(1)} async-done(((bf16[8,6,96,128]{3,2,1,0:T(8,128)(2,1)}), bf16[8,6,96,128]{3,2,1,0:T(8,128)(2,1)S(1)}, u32[]{:S(2)}, u32[]{:S(2)}) %all-to-all-start.1) | async-done | bytes 1179680 | tf_op jit(solution)/shard_map/all_to_all | solution.py:727
  110.5 14.5 %shard_map.107 = (bf16[6,2720,128]{2,1,0:T(8,128)(2,1)}, bf16[6,2720,128]{2,1,0:T(8,128)(2,1)}, bf16[8,6,96,128]{3,2,1,0:T(8,128)(2,1)}) custom-call(bf16[6,2720,128]{2,1,0:T(8,128)(2,1)} %get-tuple-element.61.hid_ref, bf16[3,2720,128]{2,1,0:T(8,128)(2,1)} %get-tuple-element.62.adj_low, bf16[3,2720,128]{2,1,0:T(8,128)(2,1)} %get-tuple-element.66.adj_high, ...), custom_call_target="tpu_custom_call" | custom-call | bytes 26259456 | tf_op jit(solution)/shard_map/pallas_call | solution.py:158
  125.0 3.6 %all-to-all-start.2 = ((bf16[8,6,96,128]{3,2,1,0:T(8,128)(2,1)}), bf16[8,6,96,128]{3,2,1,0:T(8,128)(2,1)S(1)}, u32[]{:S(2)}, u32[]{:S(2)}) async-start(bf16[8,6,96,128]{3,2,1,0:T(8,128)(2,1)} %get-tuple-element.74), calls=%async_computation.2 | async-start | bytes 2359296 | tf_op jit(solution)/shard_map/all_to_all | solution.py:727
  129.3 13.2 %shard_map.108 = bf16[1152,128]{1,0:T(8,128)(2,1)} custom-call(bf16[6,2720,128]{2,1,0:T(8,128)(2,1)} %get-tuple-element.75.act_ref, bf16[6,2048,128]{2,1,0:T(8,128)(2,1)} %bitcast.111), custom_call_target="tpu_custom_call" | custom-call | flops 4529848320 | bytes 14647296 | tf_op jit(solution)/shard_map/pallas_call | solution.py:158
  147.9 20.2 %shard_map.110 = (bf16[6,2720,128]{2,1,0:T(8,128)(2,1)}, bf16[6,2048,128]{2,1,0:T(8,128)(2,1)}, bf16[8,6,96,128]{3,2,1,0:T(8,128)(2,1)}, f32[6,1,128]{2,1,0:T(1,128)}) custom-call(bf16[6,2720,128]{2,1,0:T(8,128)(2,1)} %get-tuple-element.72.part_ref, bf16[6,2880,128]{2,1,0:T(8,128)(2,1)} %get-tuple-element.73.slope_ref, ...), custom_call_target="tpu_custom_call" | custom-call | flops 4529848320 | bytes 18493440 | tf_op jit(solution)/shard_map/pallas_call | solution.py:158
  168.2 3.8 %all-to-all-start.3 = ((bf16[8,6,96,128]{3,2,1,0:T(8,128)(2,1)}), bf16[8,6,96,128]{3,2,1,0:T(8,128)(2,1)S(1)}, u32[]{:S(2)}, u32[]{:S(2)}) async-start(bf16[8,6,96,128]{3,2,1,0:T(8,128)(2,1)} %get-tuple-element.80), calls=%async_computation.3 | async-start | bytes 2359296 | tf_op jit(solution)/shard_map/all_to_all | solution.py:727
  172.0 13.4 %shard_map.111 = bf16[1152,128]{1,0:T(8,128)(2,1)} custom-call(bf16[6,2880,128]{2,1,0:T(8,128)(2,1)} %get-tuple-element.81.act_ref, bf16[6,2720,128]{2,1,0:T(8,128)(2,1)} %get-tuple-element.82.grad_ref), custom_call_target="tpu_custom_call" | custom-call | flops 4529848320 | bytes 17203200 | tf_op jit(solution)/shard_map/pallas_call | solution.py:158
  190.9 3.5 %all-to-all-start.4 = ((bf16[8,304,128]{2,1,0:T(8,128)(2,1)}), bf16[8,304,128]{2,1,0:T(8,128)(2,1)S(1)}, u32[]{:S(2)}, u32[]{:S(2)}) async-start(bf16[8,304,128]{2,1,0:T(8,128)(2,1)} %bitcast.28), calls=%async_computation.4 | async-start | bytes 1245184 | tf_op jit(solution)/shard_map/all_to_all | solution.py:623
  196.7 6.0 %shard_map.113 = (bf16[6,128,2048]{2,1,0:T(8,128)(2,1)}, f32[6,1,128]{2,1,0:T(1,128)}) custom-call(bf16[6,2048,128]{2,1,0:T(8,128)(2,1)} %get-tuple-element.79.part_ref, f32[6,32,128]{2,1,0:T(8,128)} %get-tuple-element.84.row_ref, f32[6,64,128]{2,1,0:T(8,128)} %get-tuple-element.85.col_ref), custom_call_target="tpu_custom_call" | custom-call | bytes 6881280 | tf_op jit(solution)/shard_map/pallas_call | solution.py:158
  204.5 5.6 %convolution_convert_fusion = bf16[2048,1024]{0,1:T(8,128)(2,1)S(1)} fusion(bf16[768,2048]{1,0:T(8,128)(2,1)} %bitcast.116, bf16[768,1024]{1,0:T(8,128)(2,1)S(1)} %bitcast.119), kind=kOutput, calls=%fused_computation.1 | convolution fusion | flops 3223322624 | bytes 8912896 | tf_op jit(solution)/shard_map/dot_general | solution.py:853
  214.6 4.9 %all-to-all-start.5 = ((bf16[4,320,128]{2,1,0:T(8,128)(2,1)}), bf16[4,320,128]{2,1,0:T(8,128)(2,1)S(1)}, u32[]{:S(2)}, u32[]{:S(2)}) async-start(bf16[4,320,128]{2,1,0:T(8,128)(2,1)} %broadcast_in_dim.8), calls=%async_computation.5 | async-start | bytes 655360 | tf_op jit(solution)/shard_map/all_to_all | solution.py:614
  219.5 7.9 %convolution_convert_fusion.1 = bf16[768,1024]{1,0:T(8,128)(2,1)} fusion(bf16[768,2048]{1,0:T(8,128)(2,1)} %bitcast.117, bf16[1024,2048]{1,0:T(8,128)(2,1)} %weight_ref.1), kind=kOutput, calls=%fused_computation.2 | convolution fusion | flops 3222011904 | bytes 8912896 | tf_op jit(solution)/shard_map/dot_general | solution.py:858
  239.6 8.0 %collective-permute-done.5 = bf16[2,1,1,2,32,2048]{5,4,3,2,1,0:T(8,128)(2,1)} collective-permute-done((bf16[2,1,1,2,32,2048]{5,4,3,2,1,0:T(8,128)(2,1)}, bf16[2,1,1,2,32,2048]{5,4,3,2,1,0:T(8,128)(2,1)}, u32[]{:S(2)}, u32[]{:S(2)}) %collective-permute-start.5) | collective-permute-done | bytes 524320 | tf_op jit(solution)/shard_map/ppermute | solution.py:657
  251.8 8.0 %collective-permute-done.6 = bf16[2,1,1,1,32,2048]{5,4,3,2,1,0:T(8,128)(2,1)S(1)} collective-permute-done((bf16[2,1,1,1,32,2048]{5,4,3,2,1,0:T(8,128)(2,1)S(1)}, bf16[2,1,1,1,32,2048]{5,4,3,2,1,0:T(8,128)(2,1)S(1)}, u32[]{:S(2)}, u32[]{:S(2)}) %collective-permute-start.6) | collective-permute-done | bytes 262176 | tf_op jit(solution)/shard_map/ppermute | solution.py:657
  260.9 4.8 %all-to-all-start.7 = ((bf16[4,32,2048]{2,1,0:T(8,128)(2,1)}), bf16[4,32,2048]{2,1,0:T(8,128)(2,1)S(1)}, u32[]{:S(2)}, u32[]{:S(2)}) async-start(bf16[4,32,2048]{2,1,0:T(8,128)(2,1)} %maximum_bitcast_fusion), calls=%async_computation.7 | async-start | bytes 1048576 | tf_op jit(solution)/shard_map/all_to_all | solution.py:128
  268.0 11.2 %all-to-all-done.7 = bf16[4,32,2048]{2,1,0:T(8,128)(2,1)S(1)} async-done(((bf16[4,32,2048]{2,1,0:T(8,128)(2,1)}), bf16[4,32,2048]{2,1,0:T(8,128)(2,1)S(1)}, u32[]{:S(2)}, u32[]{:S(2)}) %all-to-all-start.7) | async-done | bytes 524320 | tf_op jit(solution)/shard_map/all_to_all | solution.py:128
  (115 shorter events, 66.2 us)
Async XLA Ops:
  11.6 18.9 %collective-permute-start = (bf16[6,256,128]{2,1,0:T(8,128)(2,1)}, bf16[6,256,128]{2,1,0:T(8,128)(2,1)S(1)}, u32[]{:S(2)}, u32[]{:S(2)}) collective-permute-start(bf16[6,256,128]{2,1,0:T(8,128)(2,1)} %get-tuple-element.53), channel_id=1, source_target_pairs={{0,2},{2,4},{4,6},{1,3},{3,5},{5,7},{8,10},{10,12},{12,14},{9,11},... | collective-permute-start | bytes 1179656 | tf_op jit(solution)/shard_map/ppermute | solution.py:20
  14.0 16.5 %collective-permute-start.1 = (bf16[6,256,128]{2,1,0:T(8,128)(2,1)}, bf16[6,256,128]{2,1,0:T(8,128)(2,1)S(1)}, u32[]{:S(2)}, u32[]{:S(2)}) collective-permute-start(bf16[6,256,128]{2,1,0:T(8,128)(2,1)} %get-tuple-element.54), channel_id=1, source_target_pairs={{2,0},{4,2},{6,4},{3,1},{5,3},{7,5},{10,8},{12,10},{14,12},{11,9},... | collective-permute-start | bytes 1179656 | tf_op jit(solution)/shard_map/ppermute | solution.py:20
  15.3 42.3 %all-to-all-start = ((bf16[8,6,96,128]{3,2,1,0:T(8,128)(2,1)}), bf16[8,6,96,128]{3,2,1,0:T(8,128)(2,1)S(1)}, u32[]{:S(2)}, u32[]{:S(2)}) async-start(bf16[8,6,96,128]{3,2,1,0:T(8,128)(2,1)} %get-tuple-element.55), calls=%async_computation | async-start | bytes 2359296 | tf_op jit(solution)/shard_map/all_to_all | solution.py:727
  22.3 4.9 %copy-start.8 = (bf16[2,1152,128]{2,1,0:T(8,128)(2,1)S(1)}, bf16[2,1152,128]{2,1,0:T(8,128)(2,1)}, u32[]{:S(2)}) copy-start(bf16[2,1152,128]{2,1,0:T(8,128)(2,1)} %param.10) | copy-start | bytes 1769476
  30.4 8.3 %copy-start.9 = (bf16[6,256,128]{2,1,0:T(8,128)(2,1)}, bf16[6,256,128]{2,1,0:T(8,128)(2,1)S(1)}, u32[]{:S(2)}) copy-start(bf16[6,256,128]{2,1,0:T(8,128)(2,1)S(1)} %collective-permute-done.above_ref) | copy-start | bytes 1179652
  31.9 13.3 %collective-permute-start.3 = (bf16[6,36,2,2,128]{4,3,2,1,0:T(2,128)(2,1)S(1)}, bf16[6,36,2,2,128]{4,3,2,1,0:T(2,128)(2,1)S(1)}, u32[]{:S(2)}, u32[]{:S(2)}) collective-permute-start(bf16[6,36,2,2,128]{4,3,2,1,0:T(2,128)(2,1)S(1)} %pad_maximum_fusion.1), channel_id=1, source_target_pairs={{1,0},{3,2},{5,4},{7,6},{9,8},{11,10},{13,12},{15,14},{17,16},{19,... | collective-permute-start | bytes 663560 | tf_op jit(solution)/shard_map/ppermute | solution.py:20
  33.9 9.6 %collective-permute-start.2 = (bf16[6,36,2,2,128]{4,3,1,0,2:T(2,128)(2,1)S(1)}, bf16[6,36,2,2,128]{4,3,1,0,2:T(2,128)(2,1)S(1)}, u32[]{:S(2)}, u32[]{:S(2)}) collective-permute-start(bf16[6,36,2,2,128]{4,3,1,0,2:T(2,128)(2,1)S(1)} %pad_maximum_fusion), channel_id=1, source_target_pairs={{0,1},{2,3},{4,5},{6,7},{8,9},{10,11},{12,13},{14,15},{16,17},{18,... | collective-permute-start | bytes 663560 | tf_op jit(solution)/shard_map/ppermute | solution.py:20
  86.2 21.0 %all-to-all-start.1 = ((bf16[8,6,96,128]{3,2,1,0:T(8,128)(2,1)}), bf16[8,6,96,128]{3,2,1,0:T(8,128)(2,1)S(1)}, u32[]{:S(2)}, u32[]{:S(2)}) async-start(bf16[8,6,96,128]{3,2,1,0:T(8,128)(2,1)} %get-tuple-element.63), calls=%async_computation.1 | async-start | bytes 2359296 | tf_op jit(solution)/shard_map/all_to_all | solution.py:727
  125.0 19.7 %all-to-all-start.2 = ((bf16[8,6,96,128]{3,2,1,0:T(8,128)(2,1)}), bf16[8,6,96,128]{3,2,1,0:T(8,128)(2,1)S(1)}, u32[]{:S(2)}, u32[]{:S(2)}) async-start(bf16[8,6,96,128]{3,2,1,0:T(8,128)(2,1)} %get-tuple-element.74), calls=%async_computation.2 | async-start | bytes 2359296 | tf_op jit(solution)/shard_map/all_to_all | solution.py:727
  168.2 19.7 %all-to-all-start.3 = ((bf16[8,6,96,128]{3,2,1,0:T(8,128)(2,1)}), bf16[8,6,96,128]{3,2,1,0:T(8,128)(2,1)S(1)}, u32[]{:S(2)}, u32[]{:S(2)}) async-start(bf16[8,6,96,128]{3,2,1,0:T(8,128)(2,1)} %get-tuple-element.80), calls=%async_computation.3 | async-start | bytes 2359296 | tf_op jit(solution)/shard_map/all_to_all | solution.py:727
  172.0 15.9 %copy-start.11 = (bf16[1152,128]{1,0:T(8,128)(2,1)S(1)}, bf16[1152,128]{1,0:T(8,128)(2,1)}, u32[]{:S(2)}) copy-start(bf16[1152,128]{1,0:T(8,128)(2,1)} %shard_map.108) | copy-start | bytes 884740
  187.9 6.5 %copy-start.1 = (bf16[8,6,96,128]{3,2,1,0:T(8,128)(2,1)}, bf16[8,6,96,128]{3,2,1,0:T(8,128)(2,1)S(1)}, u32[]{:S(2)}) copy-start(bf16[8,6,96,128]{3,2,1,0:T(8,128)(2,1)S(1)} %all-to-all-done.3.parts_ref) | copy-start | bytes 3538948
  190.9 13.7 %all-to-all-start.4 = ((bf16[8,304,128]{2,1,0:T(8,128)(2,1)}), bf16[8,304,128]{2,1,0:T(8,128)(2,1)S(1)}, u32[]{:S(2)}, u32[]{:S(2)}) async-start(bf16[8,304,128]{2,1,0:T(8,128)(2,1)} %bitcast.28), calls=%async_computation.4 | async-start | bytes 1245184 | tf_op jit(solution)/shard_map/all_to_all | solution.py:623
  194.4 10.1 %copy-start.16 = (bf16[2,3,8,16,1024]{4,3,2,1,0:T(8,128)(2,1)S(1)}, bf16[2,3,8,16,1024]{4,3,2,1,0:T(8,128)(2,1)}, u32[]{:S(2)}) copy-start(bf16[2,3,8,16,1024]{4,3,2,1,0:T(8,128)(2,1)} %param.6) | copy-start | bytes 4718596
  213.7 13.7 %collective-permute-start.4 = (bf16[4,2,1,2,32,2048]{5,4,3,2,1,0:T(8,128)(2,1)}, bf16[4,2,1,2,32,2048]{5,4,3,2,1,0:T(8,128)(2,1)}, u32[]{:S(2)}, u32[]{:S(2)}) collective-permute-start(bf16[4,2,1,2,32,2048]{5,4,3,2,1,0:T(8,128)(2,1)} %constant_dynamic-slice_fusion.4), channel_id=1, source_target_pairs={{0,2},{2,0},{4,6},{6,4},{1,3},{3,1},{5,7},{7,5},{8,10},{10,8},{12,... | collective-permute-start | bytes 6291464 | tf_op jit(solution)/shard_map/ppermute | solution.py:657
  214.6 15.8 %all-to-all-start.5 = ((bf16[4,320,128]{2,1,0:T(8,128)(2,1)}), bf16[4,320,128]{2,1,0:T(8,128)(2,1)S(1)}, u32[]{:S(2)}, u32[]{:S(2)}) async-start(bf16[4,320,128]{2,1,0:T(8,128)(2,1)} %broadcast_in_dim.8), calls=%async_computation.5 | async-start | bytes 655360 | tf_op jit(solution)/shard_map/all_to_all | solution.py:614
  219.5 7.9 %copy-start.5 = (bf16[2048,1024]{0,1:T(8,128)(2,1)S(1)}, bf16[2048,1024]{0,1:T(8,128)(2,1)}, u32[]{:S(2)}) copy-start(bf16[2048,1024]{0,1:T(8,128)(2,1)} %copy-done.4) | copy-start | bytes 12582916
  232.4 15.1 %copy-start.7 = (bf16[2,2,1,2,32,2048]{5,4,3,2,1,0:T(8,128)(2,1)S(1)}, bf16[2,2,1,2,32,2048]{5,4,3,2,1,0:T(8,128)(2,1)}, u32[]{:S(2)}) copy-start(bf16[2,2,1,2,32,2048]{5,4,3,2,1,0:T(8,128)(2,1)} %copy-done.6) | copy-start | bytes 3145732
  232.4 15.1 %collective-permute-start.5 = (bf16[2,1,1,2,32,2048]{5,4,3,2,1,0:T(8,128)(2,1)}, bf16[2,1,1,2,32,2048]{5,4,3,2,1,0:T(8,128)(2,1)}, u32[]{:S(2)}, u32[]{:S(2)}) collective-permute-start(bf16[2,1,1,2,32,2048]{5,4,3,2,1,0:T(8,128)(2,1)} %constant_dynamic-slice_fusion.3), channel_id=1, source_target_pairs={{0,4},{2,6},{4,0},{6,2},{1,5},{3,7},{5,1},{7,3},{8,12},{10,14},{12... | collective-permute-start | bytes 1572872 | tf_op jit(solution)/shard_map/ppermute | solution.py:657
  233.9 16.1 %collective-permute-start.7 = (bf16[2,2,1,1,32,2048]{5,4,3,2,1,0:T(8,128)(2,1)}, bf16[2,2,1,1,32,2048]{5,4,3,2,1,0:T(8,128)(2,1)}, u32[]{:S(2)}, u32[]{:S(2)}) collective-permute-start(bf16[2,2,1,1,32,2048]{5,4,3,2,1,0:T(8,128)(2,1)} %constant_dynamic-slice_fusion.1), channel_id=1, source_target_pairs={{0,1},{1,0},{2,3},{3,2},{4,5},{5,4},{6,7},{7,6},{8,9},{9,8},{10,11... | collective-permute-start | bytes 1572872 | tf_op jit(solution)/shard_map/ppermute | solution.py:657
  236.0 24.8 %all-to-all-start.6 = ((bf16[8,320,128]{2,1,0:T(8,128)(2,1)}), bf16[8,320,128]{2,1,0:T(8,128)(2,1)S(1)}, u32[]{:S(2)}, u32[]{:S(2)}) async-start(bf16[8,320,128]{2,1,0:T(8,128)(2,1)} %broadcast_in_dim.18), calls=%async_computation.6 | async-start | bytes 1310720 | tf_op jit(solution)/shard_map/all_to_all | solution.py:614
  248.7 11.1 %collective-permute-start.6 = (bf16[2,1,1,1,32,2048]{5,4,3,2,1,0:T(8,128)(2,1)S(1)}, bf16[2,1,1,1,32,2048]{5,4,3,2,1,0:T(8,128)(2,1)S(1)}, u32[]{:S(2)}, u32[]{:S(2)}) collective-permute-start(bf16[2,1,1,1,32,2048]{5,4,3,2,1,0:T(8,128)(2,1)S(1)} %constant_dynamic-slice_fusion.2), channel_id=1, source_target_pairs={{0,1},{1,0},{2,3},{3,2},{4,5},{5,4},{6,7},{7,6},{8,9},{9,8},{10,11... | collective-permute-start | bytes 786440 | tf_op jit(solution)/shard_map/ppermute | solution.py:657
  251.2 8.7 %collective-permute-start.8 = (bf16[2,1,1,1,32,2048]{5,4,3,2,1,0:T(8,128)(2,1)S(1)}, bf16[2,1,1,1,32,2048]{5,4,3,2,1,0:T(8,128)(2,1)S(1)}, u32[]{:S(2)}, u32[]{:S(2)}) collective-permute-start(bf16[2,1,1,1,32,2048]{5,4,3,2,1,0:T(8,128)(2,1)S(1)} %constant_dynamic-slice_fusion), channel_id=1, source_target_pairs={{0,4},{2,6},{4,0},{6,2},{1,5},{3,7},{5,1},{7,3},{8,12},{10,14},{12... | collective-permute-start | bytes 786440 | tf_op jit(solution)/shard_map/ppermute | solution.py:657
  260.9 18.4 %all-to-all-start.7 = ((bf16[4,32,2048]{2,1,0:T(8,128)(2,1)}), bf16[4,32,2048]{2,1,0:T(8,128)(2,1)S(1)}, u32[]{:S(2)}, u32[]{:S(2)}) async-start(bf16[4,32,2048]{2,1,0:T(8,128)(2,1)} %maximum_bitcast_fusion), calls=%async_computation.7 | async-start | bytes 1048576 | tf_op jit(solution)/shard_map/all_to_all | solution.py:128
  (11 other events, 27.6 us)

commit v3 on v2

--- a/solution.py
+++ b/solution.py
@@ -291,8 +291,7 @@
 
 
 def forward_kernel(
-    dims, extent, own_ref, above_ref, below_ref, left_ref, right_ref,
-    row_ref, col_ref, kernel_ref,
+    dims, extent, row_ref, col_ref, own_ref, above_ref, below_ref, left_ref, right_ref, kernel_ref,
     act_ref, slope_ref, next_ref, copies_ref, raw_ref, prod, sums_ref, mask,
 ):
     height, breadth, width = dims
@@ -374,9 +373,24 @@
             col_ref[first + q] = view[8 - side : 8 + breadth + side, :] + bias_ref[...]
 
 
+def with_contexts(kernel, dims, ring, side):
+    def body(parts_ref, bias_ref, *refs):
+        row_all, col_all, rows, cols = refs[-4:]
+
+        @pl.when(pl.program_id(0) == 0)
+        def _():
+            context_kernel(
+                dims, ring, side, parts_ref, bias_ref, row_all, col_all, rows, cols
+            )
+
+        plane = pl.program_id(0)
+        kernel(row_all.at[plane], col_all.at[plane], *refs[:-4])
+
+    return body
+
+
 def middle_kernel(
-    dims, extent, half, hid_ref, adj_low, adj_high, grad_low, grad_high,
-    row_ref, col_ref, act_ref, next_ref, copies_ref, sums_ref, mask,
+    dims, extent, half, row_ref, col_ref, hid_ref, adj_low, adj_high, grad_low, grad_high, act_ref, next_ref, copies_ref, sums_ref, mask,
 ):
     height, breadth, width = dims
     mask[...], limit = inside_limits(1, extent, height, breadth, width)
@@ -407,7 +421,7 @@
 
 
 def backward_kernel(
-    dims, extent, part_ref, slope_ref, row_ref, col_ref, kernel_ref,
+    dims, extent, row_ref, col_ref, part_ref, slope_ref, kernel_ref,
     grad_ref, next_ref, copies_ref, bias_ref, prod, sums_ref, mask,
 ):
     height, breadth, width = dims
@@ -442,7 +456,7 @@
     bias_ref[...] = jnp.sum(bias, 0, keepdims=True)
 
 
-def taps_kernel(dims, part_ref, row_ref, col_ref, tap_ref, bias_ref, full):
+def taps_kernel(dims, row_ref, col_ref, part_ref, tap_ref, bias_ref, full):
     height, breadth, up, channels = dims
 
     def one(r, total):
@@ -464,7 +478,9 @@
                 ] = piece.astype(BF)
 
 
-def kernel_grad_kernel(dims, act_base, grad_base, act_ref, grad_ref, rounded_ref, wide, moved, out_ref):
+def kernel_grad_kernel(dims, act_base, grad_base, act_ref, grad_ref, *refs):
+    more, (rounded_ref, wide, moved, out_ref) = refs[:-4], refs[-4:]
+
     height, breadth, width = dims
     edge = (width - breadth) // 2
     channels = act_ref.shape[1]
@@ -524,7 +540,17 @@
 
     @pl.when(pl.program_id(0) == pl.num_programs(0) - 1)
     def _():
-        rounded_ref[...] = out_ref[...].astype(BF)
+        size = out_ref.shape[0]
+        rounded_ref[:size, :] = out_ref[...].astype(BF)
+        if more:
+            other_ref, bias0_ref, bias1_ref = more
+            rounded_ref[size : 2 * size, :] = other_ref[...]
+            tail = rounded_ref.shape[0] - 2 * size
+            row = lax.broadcasted_iota(jnp.int32, (tail, channels), 0)
+            bias0 = jnp.sum(bias0_ref[...], 0)
+            bias1 = jnp.sum(bias1_ref[...], 0)
+            value = jnp.where(row == 0, bias0, jnp.where(row == 1, bias1, 0.0))
+            rounded_ref[2 * size :, :] = value.astype(BF)
 
 
 def plain_pass(tokens, gout, deconv_weight, deconv_bias, conv_kernels, conv_biases):
@@ -600,7 +626,12 @@
         + [v.reshape(1, channels) for v in (cbias0, cbias1)],
         0,
     )
-    small = small_whole(small_summed(small_parts(small), bias_part))
+    bands = lax.axis_size(BANDS)
+    piece = -(-small.shape[0] // bands)
+    piece += -piece % 16
+    small = jnp.pad(small, ((0, piece * bands - small.shape[0]), (0, 0))).astype(BF)
+    small = lax.all_to_all(small.reshape(bands, piece, channels), BANDS, 0, 0, tiled=True)
+    small = small_whole(small_summed(small, bias_part))
     bands = lax.axis_size("plane") * lax.axis_size("tile")
     total = lax.axis_size("obj") * bands
     weight_grad = scatter_all(
@@ -612,15 +643,6 @@
 def sent_to_all(array, axes):
     copies = jnp.broadcast_to(array[None], (lax.axis_size(axes),) + array.shape)
     return lax.all_to_all(copies, axes, 0, 0, tiled=True)
-
-
-def small_parts(small):
-    rows, channels = small.shape
-    bands = lax.axis_size(BANDS)
-    piece = -(-rows // bands)
-    piece += -piece % 16
-    parts = jnp.pad(small, ((0, piece * bands - rows), (0, 0))).astype(BF)
-    return lax.all_to_all(parts.reshape(bands, piece, channels), BANDS, 0, 0, tiled=True)
 
 
 def small_summed(parts, bias_part):
@@ -703,6 +725,7 @@
     def columns_beside(bands_of, last):
         def cut(parts):
             cells = [p[:, :, -2:] if last else p[:, :, :2] for p in parts]
+            cells = lax.optimization_barrier(cells)
             return jnp.concatenate([c.astype(BF) for c in cells], 1)
 
         rim = shifted(jnp.stack([cut(parts) for parts in bands_of], 2), "tile", 1 if last else -1)
@@ -723,27 +746,15 @@
     conv_flops = lambda rows: 2 * rows * width * side * side
     mask = pltpu.VMEM((width, channels), F32)
 
-    def contexts(parts, rim, pad, bias, beside=None):
+    def contexts(parts, rim, pad, bias, beside):
         parts = lax.all_to_all(parts, BANDS, 0, 0, tiled=True)
-        if beside is not None:
-            parts, beside = lax.optimization_barrier((parts, beside))
-        whole = lambda array: pl.BlockSpec(memory_space=pltpu.VMEM)
-        shapes = [
-            jax.ShapeDtypeStruct((planes, height + 2 * rim, channels), F32),
-            jax.ShapeDtypeStruct((planes, breadth + 2 * pad, channels), F32),
-        ]
-        terms = pl.pallas_call(
-            functools.partial(context_kernel, dims, rim, pad),
-            in_specs=[whole(parts), whole(bias)],
-            out_specs=[whole(shape) for shape in shapes],
-            out_shape=shapes,
-            scratch_shapes=[pltpu.VMEM((3, extent + 16, channels), F32)] * 2,
-            compiler_params=pltpu.CompilerParams(vmem_limit_bytes=60 << 20),
-            cost_estimate=pl.CostEstimate(
-                flops=4 * parts.size, bytes_accessed=2 * parts.size, transcendentals=0
-            ),
-        )(parts, bias.reshape(1, channels))
-        return tuple(terms) if beside is None else tuple(terms) + (beside,)
+        parts, beside = lax.optimization_barrier((parts, beside))
+        room = [
+            pltpu.VMEM((planes, height + 2 * rim, channels), F32),
+            pltpu.VMEM((planes, breadth + 2 * pad, channels), F32),
+        ] + [pltpu.VMEM((3, extent + 16, channels), F32)] * 2
+        given = [(parts, True), (bias.reshape(1, channels), True)]
+        return given, room, lambda kernel: with_contexts(kernel, dims, rim, pad), beside
 
     rim_rows = ((planes, 4 * breadth, channels), BF, False)
     raw, parts, first, last, cbias1 = call(
@@ -763,6 +774,7 @@
         for slot, cells in enumerate((grad_top, raw.reshape(grad_top.shape)))
     ]
     left, right = columns_beside(both, True), columns_beside(both, False)
+    parts, left, right = lax.optimization_barrier((parts, left, right))
 
     def adjoint_of(first, count):
         kind = (first, -count)
@@ -781,37 +793,38 @@
         )
 
     low = adjoint_of(0, half)
-    row_ctx, col_ctx, low = contexts(parts, 2, edge, deconv_bias, low)
+    given, room, wrap, low = contexts(parts, 2, edge, deconv_bias, low)
     act0, slope0, hidden, parts = call(
-        functools.partial(forward_kernel, dims, extent),
+        wrap(functools.partial(forward_kernel, dims, extent)),
         planes,
-        [(raw, False)]
+        given
+        + [(raw, False)]
         + [(array, False) for array in (above, below, left, right)]
-        + [(row_ctx, False), (col_ctx, False)]
         + [(ahead, True)],
         [(flat(height + 4), BF, False)] * 2 + [(flat(height + 2), BF, False), copies],
-        [pltpu.VMEM(flat(height + 4)[1:], F32), prod(height // 2 + 1), sums, mask],
+        [pltpu.VMEM(flat(height + 4)[1:], F32), prod(height // 2 + 1), sums, mask]
+        + room,
         conv_flops(height + 2),
     )
     high = adjoint_of(half, planes - half)
-    row_ctx, col_ctx, high = contexts(parts, 1, edge, deconv_bias + conv_biases[0], high)
+    given, room, wrap, high = contexts(parts, 1, edge, deconv_bias + conv_biases[0], high)
     act1, part1, parts = call(
-        functools.partial(middle_kernel, dims, extent, half),
+        wrap(functools.partial(middle_kernel, dims, extent, half)),
         planes,
-        [(hidden, False)]
+        given
+        + [(hidden, False)]
         + [(low[1], (0, half)), (high[1], (half, planes - half))]
-        + [(low[0], (0, half)), (high[0], (half, planes - half))]
-        + [(row_ctx, False), (col_ctx, False)],
+        + [(low[0], (0, half)), (high[0], (half, planes - half))],
         [(flat(height + 2), BF, False), (flat(height + 2), BF, False), copies],
-        [sums, mask],
-    )
-
-    def kernel_gradient_of(act, grad, act_base, grad_base):
+        [sums, mask] + room,
+    )
+
+    def kernel_gradient_of(act, grad, act_base, grad_base, more=(), rows=9 * channels):
         (result,) = call(
             functools.partial(kernel_grad_kernel, dims, act_base, grad_base),
             planes,
-            [(act, False), (grad, False)],
-            [((9 * channels, channels), BF, True)],
+            [(act, False), (grad, False)] + [(array, True) for array in more],
+            [((rows, channels), BF, True)],
             [
                 pltpu.VMEM((height * width + 16, channels), F32),
                 pltpu.VMEM((height * width, side), BF),
@@ -823,30 +836,28 @@
 
     none = jnp.zeros((channels,), F32)
     kernel1 = kernel_gradient_of(act1, flat_grad(grad_top), 0, None)
-    row_ctx, col_ctx, kernel1 = contexts(parts, 1, edge, none, kernel1)
+    given, room, wrap, kernel1 = contexts(parts, 1, edge, none, kernel1)
     gb1, part0, parts, cbias0 = call(
-        functools.partial(backward_kernel, dims, extent),
+        wrap(functools.partial(backward_kernel, dims, extent)),
         planes,
-        [(part1, False), (slope0, False), (row_ctx, False), (col_ctx, False)]
-        + [(back[0], True)],
+        given + [(part1, False), (slope0, False), (back[0], True)],
         [(flat(height + 2), BF, False), ((planes, height * breadth, channels), BF, False)]
         + [copies, one],
-        [prod(height // 2), sums, mask],
+        [prod(height // 2), sums, mask] + room,
         conv_flops(height),
     )
-    kernel0 = kernel_gradient_of(act0, gb1, 1, 1)
-    row_ctx, col_ctx, kernel0 = contexts(parts, 0, 0, none, kernel0)
-    small = small_parts(
-        jnp.concatenate(
-            [kernel0, kernel1] + [jnp.sum(v, 0).astype(BF) for v in (cbias0, cbias1)], 0
-        )
-    )
+    piece = -(-(18 * channels + 2) // bands)
+    piece += -piece % 16
+    more = (kernel1, cbias0, cbias1)
+    small = kernel_gradient_of(act0, gb1, 1, 1, more, piece * bands)
+    given, room, wrap, small = contexts(parts, 0, 0, none, small)
+    small = lax.all_to_all(small.reshape(bands, piece, channels), BANDS, 0, 0, tiled=True)
     tap_grads, bias_part = call(
-        functools.partial(taps_kernel, (height, breadth, up, channels)),
+        wrap(functools.partial(taps_kernel, (height, breadth, up, channels))),
         planes,
-        [(part0, False), (row_ctx, False), (col_ctx, False)],
+        given + [(part0, False)],
         [((planes, tok_rows * tok_cols, up * up * channels), BF, False), one],
-        [pltpu.VMEM((height * breadth, channels), F32)],
+        [pltpu.VMEM((height * breadth, channels), F32)] + room,
     )
     tap_grads = tap_grads.reshape(-1, up * up * channels)
     tap_grads, small = lax.optimization_barrier((tap_grads, small))

time: 282 us -> 273 us (0.968)
  waiting for transfers between devices: 42.3 us -> 51 us
  Pallas kernels: 134 us -> 128 us
  other arithmetic: 15.7 us -> 10.8 us
  local copies, waits for them, and re-layouts: 24.3 us -> 20.9 us
  starting transfers between devices: 49.2 us -> 46.3 us
    pallas_call x4 -> x0, Pallas kernels: 8.82 us -> none  [contexts(): pl.pallas_call(functools.partial(context_kernel, dims, rim, pad), in_spec...]
    another operation x1 -> x0, other arithmetic: 4.87 us -> none
    ppermute x4, waiting for transfers between devices: 2.95 us -> 6.58 us  [shifted(): return lax.ppermute(array, axis, pairs)]
    unnamed x39 -> x33, local copies, waits for them, and re-layouts: 8.42 us -> 7.79 us
  transfers between devices with their start and end apart: 17 -> 17, of which waited for: 9 -> 14; matrix products, arithmetic and copies ran while one was open for 12% -> 10% of each run, Pallas kernels for 20% -> 20%
where the time goes in v3:
time: 273 us; the launch traced here: 271 us
  Pallas kernels  128 us (47%)
  waiting for transfers between devices  51 us (19%)
  starting transfers between devices  46.3 us (17%)
  local copies, waits for them, and re-layouts  20.9 us (8%)
  matrix products  13.5 us (5%)
  other arithmetic  10.8 us (4%)
    pallas_call x9, Pallas kernels, call(): pl.pallas_call(kernel, grid=(planes,), in_specs=[spec(a.shape, kind) for...  128 us
    all_to_all x4, starting transfers between devices, contexts(): parts = lax.all_to_all(parts, BANDS, 0, 0, tiled=True)  17.9 us
    ppermute x5, waiting for transfers between devices, halved(): other = lax.ppermute(theirs, axis, [(i, i ^ step) for i in range(size)])  17.1 us
    all_to_all x4, waiting for transfers between devices, contexts(): parts = lax.all_to_all(parts, BANDS, 0, 0, tiled=True)  12.2 us
    all_to_all x1, waiting for transfers between devices, scattered(): return jnp.sum(lax.all_to_all(parts, axes, 0, 0, tiled=True).astype(F32), 0)  11.1 us
    ppermute x4, starting transfers between devices, shifted(): return lax.ppermute(array, axis, pairs)  8.41 us
    all_to_all x2, starting transfers between devices, sent_to_all(): return lax.all_to_all(copies, axes, 0, 0, tiled=True)  8.41 us
    dot_general x1, matrix products, kernel_pass(): lax.dot_general(tap_grads, deconv_weight, (((1,), (1,)), ((), ())), prefe...  7.87 us
  transfers between devices with their start and end apart: 17, of which 14 were waited for; matrix products, arithmetic and copies ran while one was open for 10% of the time, Pallas kernels for 20%

profile of v3, /device:TPU:0, one launch (start us, length us, event | category | flops | bytes accessed | tf_op | source)
XLA Modules:
  0.0 271.2 jit_solution(14529681033932834660)
XLA Ops:
  0.6 10.9 %shard_map.101 = (f32[6,2048,128]{2,1,0:T(8,128)}, bf16[8,6,96,128]{3,2,1,0:T(8,128)(2,1)}, bf16[6,256,128]{2,1,0:T(8,128)(2,1)}, bf16[6,256,128]{2,1,0:T(8,128)(2,1)}, f32[6,1,128]{2,1,0:T(1,128)}) custom-call(bf16[6,128,1024]{2,1,0:T(8,128)(2,1)} %bitcast.110, bf16[6,2048,128]{2,1,0:T(8,128)(2,1)} %bitcast.101, bf16[1024,2048]{1,0:T(8,128)(2,1)} %weight_ref.1), custom_call_target="tpu_custom_call" | custom-call | flops 3221225472 | bytes 17825792 | tf_op jit(solution)/shard_map/pallas_call | solution.py:158
  34.2 7.1 %all-to-all-start = ((bf16[8,6,96,128]{3,2,1,0:T(8,128)(2,1)}), bf16[8,6,96,128]{3,2,1,0:T(8,128)(2,1)S(1)}, u32[]{:S(2)}, u32[]{:S(2)}) async-start(bf16[8,6,96,128]{3,2,1,0:T(8,128)(2,1)} %get-tuple-element.75), calls=%async_computation | async-start | bytes 2359296 | tf_op jit(solution)/shard_map/all_to_all | solution.py:750
  43.9 10.8 %shard_map.102 = (bf16[3,2880,128]{2,1,0:T(8,128)(2,1)}, bf16[3,2720,128]{2,1,0:T(8,128)(2,1)}) custom-call(bf16[6,2048,128]{2,1,0:T(8,128)(2,1)} %bitcast.103, bf16[6,256,128]{2,1,0:T(8,128)(2,1)} %copy-done.9, bf16[6,256,128]{2,1,0:T(8,128)(2,1)} %copy-done.10, f32[6,576,128]{2,1,0:T(8,128)} %bitcast.85, ...), custom_call_target="tpu_custom_call" | custom-call | flops 2406481920 | bytes 15532032 | tf_op jit(solution)/shard_map/pallas_call | solution.py:158
  58.5 25.8 %shard_map.103 = (bf16[6,2880,128]{2,1,0:T(8,128)(2,1)}, bf16[6,2880,128]{2,1,0:T(8,128)(2,1)}, bf16[6,2720,128]{2,1,0:T(8,128)(2,1)}, bf16[8,6,96,128]{3,2,1,0:T(8,128)(2,1)}) custom-call(bf16[8,6,96,128]{3,2,1,0:T(8,128)(2,1)} %copy-done.7, f32[1,128]{1,0:T(1,128)} %bitcast.112, f32[6,2048,128]{2,1,0:T(8,128)} %get-tuple-element.65.refs_0_, ...), custom_call_target="tpu_custom_call" | custom-call | flops 4812963840 | bytes 24183808 | tf_op jit(solution)/shard_map/pallas_call | solution.py:158
  84.3 3.7 %all-to-all-start.1 = ((bf16[8,6,96,128]{3,2,1,0:T(8,128)(2,1)}), bf16[8,6,96,128]{3,2,1,0:T(8,128)(2,1)S(1)}, u32[]{:S(2)}, u32[]{:S(2)}) async-start(bf16[8,6,96,128]{3,2,1,0:T(8,128)(2,1)} %get-tuple-element.81), calls=%async_computation.1 | async-start | bytes 2359296 | tf_op jit(solution)/shard_map/all_to_all | solution.py:750
  88.5 10.8 %shard_map.104 = (bf16[3,2880,128]{2,1,0:T(8,128)(2,1)}, bf16[3,2720,128]{2,1,0:T(8,128)(2,1)}) custom-call(bf16[6,2048,128]{2,1,0:T(8,128)(2,1)} %bitcast.104, bf16[6,256,128]{2,1,0:T(8,128)(2,1)} %copy-done.9, bf16[6,256,128]{2,1,0:T(8,128)(2,1)} %copy-done.10, f32[6,576,128]{2,1,0:T(8,128)} %bitcast.87, ...), custom_call_target="tpu_custom_call" | custom-call | flops 2406481920 | bytes 15532032 | tf_op jit(solution)/shard_map/pallas_call | solution.py:158
  99.3 4.9 %all-to-all-done.1.parts_ref = bf16[8,6,96,128]{3,2,1,0:T(8,128)(2,1)S(1)} async-done(((bf16[8,6,96,128]{3,2,1,0:T(8,128)(2,1)}), bf16[8,6,96,128]{3,2,1,0:T(8,128)(2,1)S(1)}, u32[]{:S(2)}, u32[]{:S(2)}) %all-to-all-start.1) | async-done | bytes 1179680 | tf_op jit(solution)/shard_map/all_to_all | solution.py:750
  105.1 15.5 %shard_map.105 = (bf16[6,2720,128]{2,1,0:T(8,128)(2,1)}, bf16[6,2720,128]{2,1,0:T(8,128)(2,1)}, bf16[8,6,96,128]{3,2,1,0:T(8,128)(2,1)}) custom-call(bf16[8,6,96,128]{3,2,1,0:T(8,128)(2,1)} %copy-done.1, f32[1,128]{1,0:T(1,128)} %fusion.2.bias_ref, bf16[6,2720,128]{2,1,0:T(8,128)(2,1)} %get-tuple-element.85.refs_0_, ...), custom_call_target="tpu_custom_call" | custom-call | bytes 27919360 | tf_op jit(solution)/shard_map/pallas_call | solution.py:158
  120.6 3.6 %all-to-all-start.2 = ((bf16[8,6,96,128]{3,2,1,0:T(8,128)(2,1)}), bf16[8,6,96,128]{3,2,1,0:T(8,128)(2,1)S(1)}, u32[]{:S(2)}, u32[]{:S(2)}) async-start(bf16[8,6,96,128]{3,2,1,0:T(8,128)(2,1)} %get-tuple-element.90), calls=%async_computation.2 | async-start | bytes 2359296 | tf_op jit(solution)/shard_map/all_to_all | solution.py:750
  125.0 13.2 %shard_map.106.refs_0_ = bf16[1152,128]{1,0:T(8,128)(2,1)} custom-call(bf16[6,2720,128]{2,1,0:T(8,128)(2,1)} %get-tuple-element.91.act_ref, bf16[6,2048,128]{2,1,0:T(8,128)(2,1)} %bitcast.105), custom_call_target="tpu_custom_call" | custom-call | flops 4529848320 | bytes 14647296 | tf_op jit(solution)/shard_map/pallas_call | solution.py:158
  141.4 20.5 %shard_map.107 = (bf16[6,2720,128]{2,1,0:T(8,128)(2,1)}, bf16[6,2048,128]{2,1,0:T(8,128)(2,1)}, bf16[8,6,96,128]{3,2,1,0:T(8,128)(2,1)}, f32[6,1,128]{2,1,0:T(1,128)}) custom-call(bf16[8,6,96,128]{3,2,1,0:T(8,128)(2,1)} %copy-done.8, f32[1,128]{1,0:T(1,128)} %broadcast_1_bias_ref.2.bias_ref, bf16[6,2720,128]{2,1,0:T(8,128)(2,1)} %get-tuple-element.93.refs_0_, ...), custom_call_target="tpu_custom_call" | custom-call | flops 4529848320 | bytes 20153344 | tf_op jit(solution)/shard_map/pallas_call | solution.py:158
  161.9 3.6 %all-to-all-start.3 = ((bf16[8,6,96,128]{3,2,1,0:T(8,128)(2,1)}), bf16[8,6,96,128]{3,2,1,0:T(8,128)(2,1)S(1)}, u32[]{:S(2)}, u32[]{:S(2)}) async-start(bf16[8,6,96,128]{3,2,1,0:T(8,128)(2,1)} %get-tuple-element.95), calls=%async_computation.3 | async-start | bytes 2359296 | tf_op jit(solution)/shard_map/all_to_all | solution.py:750
  165.5 13.6 %shard_map.108 = bf16[2432,128]{1,0:T(8,128)(2,1)} custom-call(bf16[6,2880,128]{2,1,0:T(8,128)(2,1)} %get-tuple-element.96.act_ref, bf16[6,2720,128]{2,1,0:T(8,128)(2,1)} %get-tuple-element.97.grad_ref, bf16[1152,128]{1,0:T(8,128)(2,1)} %shard_map.106.refs_0_, f32[6,1,128]{2,1,0:T(1,128)} %get-tuple-element.99.refs_1_, f32[6,1,128]{2,1,0:T(1,128)} %get-tuple-element.100.refs_2_), custom_call_target="tpu_custom_call" | custom-call | flops 4529848320 | bytes 17805312 | tf_op jit(solution)/shard_map/pallas_call | solution.py:158
  181.6 3.7 %all-to-all-start.4 = ((bf16[8,304,128]{2,1,0:T(8,128)(2,1)}), bf16[8,304,128]{2,1,0:T(8,128)(2,1)S(1)}, u32[]{:S(2)}, u32[]{:S(2)}) async-start(bf16[8,304,128]{2,1,0:T(8,128)(2,1)} %bitcast.94), calls=%async_computation.4 | async-start | bytes 1245184 | tf_op jit(solution)/shard_map/all_to_all | solution.py:854
  185.4 6.7 %shard_map.109 = (bf16[6,128,2048]{2,1,0:T(8,128)(2,1)}, f32[6,1,128]{2,1,0:T(1,128)}) custom-call(bf16[8,6,96,128]{3,2,1,0:T(8,128)(2,1)} %copy-done, f32[1,128]{1,0:T(1,128)} %broadcast_1_bias_ref.2.bias_ref, bf16[6,2048,128]{2,1,0:T(8,128)(2,1)} %get-tuple-element.102.refs_0_), custom_call_target="tpu_custom_call" | custom-call | bytes 8651776 | tf_op jit(solution)/shard_map/pallas_call | solution.py:158
  195.3 5.6 %convolution_convert_fusion = bf16[2048,1024]{0,1:T(8,128)(2,1)S(1)} fusion(bf16[768,2048]{1,0:T(8,128)(2,1)} %bitcast.108, bf16[768,1024]{1,0:T(8,128)(2,1)S(1)} %bitcast.111), kind=kOutput, calls=%fused_computation.1 | convolution fusion | flops 3223322624 | bytes 8912896 | tf_op jit(solution)/shard_map/dot_general | solution.py:864
  205.4 4.9 %all-to-all-start.5 = ((bf16[4,320,128]{2,1,0:T(8,128)(2,1)}), bf16[4,320,128]{2,1,0:T(8,128)(2,1)S(1)}, u32[]{:S(2)}, u32[]{:S(2)}) async-start(bf16[4,320,128]{2,1,0:T(8,128)(2,1)} %broadcast_in_dim.8), calls=%async_computation.5 | async-start | bytes 655360 | tf_op jit(solution)/shard_map/all_to_all | solution.py:645
  210.3 7.9 %convolution_convert_fusion.1 = bf16[768,1024]{1,0:T(8,128)(2,1)} fusion(bf16[768,2048]{1,0:T(8,128)(2,1)} %bitcast.109, bf16[1024,2048]{1,0:T(8,128)(2,1)} %weight_ref.1), kind=kOutput, calls=%fused_computation.2 | convolution fusion | flops 3222011904 | bytes 8912896 | tf_op jit(solution)/shard_map/dot_general | solution.py:869
  226.8 3.5 %all-to-all-start.6 = ((bf16[8,320,128]{2,1,0:T(8,128)(2,1)}), bf16[8,320,128]{2,1,0:T(8,128)(2,1)S(1)}, u32[]{:S(2)}, u32[]{:S(2)}) async-start(bf16[8,320,128]{2,1,0:T(8,128)(2,1)} %broadcast_in_dim.18), calls=%async_computation.6 | async-start | bytes 1310720 | tf_op jit(solution)/shard_map/all_to_all | solution.py:645
  230.4 8.0 %collective-permute-done.7 = bf16[2,2,1,1,32,2048]{5,4,3,2,1,0:T(8,128)(2,1)} collective-permute-done((bf16[2,2,1,1,32,2048]{5,4,3,2,1,0:T(8,128)(2,1)}, bf16[2,2,1,1,32,2048]{5,4,3,2,1,0:T(8,128)(2,1)}, u32[]{:S(2)}, u32[]{:S(2)}) %collective-permute-start.7) | collective-permute-done | bytes 524320 | tf_op jit(solution)/shard_map/ppermute | solution.py:679
  240.2 3.6 %collective-permute-done.5 = bf16[2,1,1,2,32,2048]{5,4,3,2,1,0:T(8,128)(2,1)} collective-permute-done((bf16[2,1,1,2,32,2048]{5,4,3,2,1,0:T(8,128)(2,1)}, bf16[2,1,1,2,32,2048]{5,4,3,2,1,0:T(8,128)(2,1)}, u32[]{:S(2)}, u32[]{:S(2)}) %collective-permute-start.5) | collective-permute-done | bytes 524320 | tf_op jit(solution)/shard_map/ppermute | solution.py:679
  245.9 5.2 %collective-permute-done.8 = bf16[2,1,1,1,32,2048]{5,4,3,2,1,0:T(8,128)(2,1)S(1)} collective-permute-done((bf16[2,1,1,1,32,2048]{5,4,3,2,1,0:T(8,128)(2,1)S(1)}, bf16[2,1,1,1,32,2048]{5,4,3,2,1,0:T(8,128)(2,1)S(1)}, u32[]{:S(2)}, u32[]{:S(2)}) %collective-permute-start.8) | collective-permute-done | bytes 262176 | tf_op jit(solution)/shard_map/ppermute | solution.py:679
  252.4 4.6 %all-to-all-start.7 = ((bf16[4,32,2048]{2,1,0:T(8,128)(2,1)}), bf16[4,32,2048]{2,1,0:T(8,128)(2,1)S(1)}, u32[]{:S(2)}, u32[]{:S(2)}) async-start(bf16[4,32,2048]{2,1,0:T(8,128)(2,1)} %maximum_bitcast_fusion), calls=%async_computation.7 | async-start | bytes 1048576 | tf_op jit(solution)/shard_map/all_to_all | solution.py:128
  259.4 11.1 %all-to-all-done.7 = bf16[4,32,2048]{2,1,0:T(8,128)(2,1)S(1)} async-done(((bf16[4,32,2048]{2,1,0:T(8,128)(2,1)}), bf16[4,32,2048]{2,1,0:T(8,128)(2,1)S(1)}, u32[]{:S(2)}, u32[]{:S(2)}) %all-to-all-start.7) | async-done | bytes 524320 | tf_op jit(solution)/shard_map/all_to_all | solution.py:128
  (100 shorter events, 61.5 us)
Async XLA Ops:
  11.6 6.6 %collective-permute-start = (bf16[6,256,128]{2,1,0:T(8,128)(2,1)}, bf16[6,256,128]{2,1,0:T(8,128)(2,1)S(1)}, u32[]{:S(2)}, u32[]{:S(2)}) collective-permute-start(bf16[6,256,128]{2,1,0:T(8,128)(2,1)} %get-tuple-element.60), channel_id=1, source_target_pairs={{0,2},{2,4},{4,6},{1,3},{3,5},{5,7},{8,10},{10,12},{12,14},{9,11},... | collective-permute-start | bytes 1179656 | tf_op jit(solution)/shard_map/ppermute | solution.py:20
  14.0 5.9 %collective-permute-start.1 = (bf16[6,256,128]{2,1,0:T(8,128)(2,1)}, bf16[6,256,128]{2,1,0:T(8,128)(2,1)S(1)}, u32[]{:S(2)}, u32[]{:S(2)}) collective-permute-start(bf16[6,256,128]{2,1,0:T(8,128)(2,1)} %get-tuple-element.61), channel_id=1, source_target_pairs={{2,0},{4,2},{6,4},{3,1},{5,3},{7,5},{10,8},{12,10},{14,12},{11,9},... | collective-permute-start | bytes 1179656 | tf_op jit(solution)/shard_map/ppermute | solution.py:20
  18.1 7.9 %copy-start.9 = (bf16[6,256,128]{2,1,0:T(8,128)(2,1)}, bf16[6,256,128]{2,1,0:T(8,128)(2,1)S(1)}, u32[]{:S(2)}) copy-start(bf16[6,256,128]{2,1,0:T(8,128)(2,1)S(1)} %collective-permute-done.above_ref.refs_1_) | copy-start | bytes 1179652
  19.9 7.6 %copy-start.10 = (bf16[6,256,128]{2,1,0:T(8,128)(2,1)}, bf16[6,256,128]{2,1,0:T(8,128)(2,1)S(1)}, u32[]{:S(2)}) copy-start(bf16[6,256,128]{2,1,0:T(8,128)(2,1)S(1)} %collective-permute-done.1.below_ref.refs_2_) | copy-start | bytes 1179652
  20.7 6.8 %collective-permute-start.2 = (bf16[6,36,2,2,128]{4,3,1,0,2:T(2,128)(2,1)S(1)}, bf16[6,36,2,2,128]{4,3,1,0,2:T(2,128)(2,1)S(1)}, u32[]{:S(2)}, u32[]{:S(2)}) collective-permute-start(bf16[6,36,2,2,128]{4,3,1,0,2:T(2,128)(2,1)S(1)} %pad_maximum_fusion), channel_id=1, source_target_pairs={{0,1},{2,3},{4,5},{6,7},{8,9},{10,11},{12,13},{14,15},{16,17},{18,... | collective-permute-start | bytes 663560 | tf_op jit(solution)/shard_map/ppermute | solution.py:20
  24.7 7.8 %collective-permute-start.3 = (bf16[6,36,2,2,128]{4,3,2,1,0:T(2,128)(2,1)S(1)}, bf16[6,36,2,2,128]{4,3,2,1,0:T(2,128)(2,1)S(1)}, u32[]{:S(2)}, u32[]{:S(2)}) collective-permute-start(bf16[6,36,2,2,128]{4,3,2,1,0:T(2,128)(2,1)S(1)} %pad_maximum_fusion.1), channel_id=1, source_target_pairs={{1,0},{3,2},{5,4},{7,6},{9,8},{11,10},{13,12},{15,14},{17,16},{19,... | collective-permute-start | bytes 663560 | tf_op jit(solution)/shard_map/ppermute | solution.py:20
  32.7 8.5 %copy-start.6 = (bf16[2,1152,128]{2,1,0:T(8,128)(2,1)S(1)}, bf16[2,1152,128]{2,1,0:T(8,128)(2,1)}, u32[]{:S(2)}) copy-start(bf16[2,1152,128]{2,1,0:T(8,128)(2,1)} %param.10) | copy-start | bytes 1769476
  34.2 23.3 %all-to-all-start = ((bf16[8,6,96,128]{3,2,1,0:T(8,128)(2,1)}), bf16[8,6,96,128]{3,2,1,0:T(8,128)(2,1)S(1)}, u32[]{:S(2)}, u32[]{:S(2)}) async-start(bf16[8,6,96,128]{3,2,1,0:T(8,128)(2,1)} %get-tuple-element.75), calls=%async_computation | async-start | bytes 2359296 | tf_op jit(solution)/shard_map/all_to_all | solution.py:750
  84.3 19.9 %all-to-all-start.1 = ((bf16[8,6,96,128]{3,2,1,0:T(8,128)(2,1)}), bf16[8,6,96,128]{3,2,1,0:T(8,128)(2,1)S(1)}, u32[]{:S(2)}, u32[]{:S(2)}) async-start(bf16[8,6,96,128]{3,2,1,0:T(8,128)(2,1)} %get-tuple-element.81), calls=%async_computation.1 | async-start | bytes 2359296 | tf_op jit(solution)/shard_map/all_to_all | solution.py:750
  120.6 19.7 %all-to-all-start.2 = ((bf16[8,6,96,128]{3,2,1,0:T(8,128)(2,1)}), bf16[8,6,96,128]{3,2,1,0:T(8,128)(2,1)S(1)}, u32[]{:S(2)}, u32[]{:S(2)}) async-start(bf16[8,6,96,128]{3,2,1,0:T(8,128)(2,1)} %get-tuple-element.90), calls=%async_computation.2 | async-start | bytes 2359296 | tf_op jit(solution)/shard_map/all_to_all | solution.py:750
  161.9 19.7 %all-to-all-start.3 = ((bf16[8,6,96,128]{3,2,1,0:T(8,128)(2,1)}), bf16[8,6,96,128]{3,2,1,0:T(8,128)(2,1)S(1)}, u32[]{:S(2)}, u32[]{:S(2)}) async-start(bf16[8,6,96,128]{3,2,1,0:T(8,128)(2,1)} %get-tuple-element.95), calls=%async_computation.3 | async-start | bytes 2359296 | tf_op jit(solution)/shard_map/all_to_all | solution.py:750
  181.6 3.8 %copy-start = (bf16[8,6,96,128]{3,2,1,0:T(8,128)(2,1)}, bf16[8,6,96,128]{3,2,1,0:T(8,128)(2,1)S(1)}, u32[]{:S(2)}) copy-start(bf16[8,6,96,128]{3,2,1,0:T(8,128)(2,1)S(1)} %all-to-all-done.3.parts_ref) | copy-start | bytes 3538948
  181.6 13.7 %all-to-all-start.4 = ((bf16[8,304,128]{2,1,0:T(8,128)(2,1)}), bf16[8,304,128]{2,1,0:T(8,128)(2,1)S(1)}, u32[]{:S(2)}, u32[]{:S(2)}) async-start(bf16[8,304,128]{2,1,0:T(8,128)(2,1)} %bitcast.94), calls=%async_computation.4 | async-start | bytes 1245184 | tf_op jit(solution)/shard_map/all_to_all | solution.py:854
  185.3 10.0 %copy-start.12 = (bf16[2,3,8,16,1024]{4,3,2,1,0:T(8,128)(2,1)S(1)}, bf16[2,3,8,16,1024]{4,3,2,1,0:T(8,128)(2,1)}, u32[]{:S(2)}) copy-start(bf16[2,3,8,16,1024]{4,3,2,1,0:T(8,128)(2,1)} %param.6) | copy-start | bytes 4718596
  204.5 13.6 %collective-permute-start.4 = (bf16[4,2,1,2,32,2048]{5,4,3,2,1,0:T(8,128)(2,1)}, bf16[4,2,1,2,32,2048]{5,4,3,2,1,0:T(8,128)(2,1)}, u32[]{:S(2)}, u32[]{:S(2)}) collective-permute-start(bf16[4,2,1,2,32,2048]{5,4,3,2,1,0:T(8,128)(2,1)} %constant_dynamic-slice_fusion.4), channel_id=1, source_target_pairs={{0,2},{2,0},{4,6},{6,4},{1,3},{3,1},{5,7},{7,5},{8,10},{10,8},{12,... | collective-permute-start | bytes 6291464 | tf_op jit(solution)/shard_map/ppermute | solution.py:679
  205.4 15.8 %all-to-all-start.5 = ((bf16[4,320,128]{2,1,0:T(8,128)(2,1)}), bf16[4,320,128]{2,1,0:T(8,128)(2,1)S(1)}, u32[]{:S(2)}, u32[]{:S(2)}) async-start(bf16[4,320,128]{2,1,0:T(8,128)(2,1)} %broadcast_in_dim.8), calls=%async_computation.5 | async-start | bytes 655360 | tf_op jit(solution)/shard_map/all_to_all | solution.py:645
  210.3 7.9 %copy-start.3 = (bf16[2048,1024]{0,1:T(8,128)(2,1)S(1)}, bf16[2048,1024]{0,1:T(8,128)(2,1)}, u32[]{:S(2)}) copy-start(bf16[2048,1024]{0,1:T(8,128)(2,1)} %copy-done.2) | copy-start | bytes 12582916
  223.2 15.1 %copy-start.5 = (bf16[2,2,1,2,32,2048]{5,4,3,2,1,0:T(8,128)(2,1)S(1)}, bf16[2,2,1,2,32,2048]{5,4,3,2,1,0:T(8,128)(2,1)}, u32[]{:S(2)}) copy-start(bf16[2,2,1,2,32,2048]{5,4,3,2,1,0:T(8,128)(2,1)} %copy-done.4) | copy-start | bytes 3145732
  223.2 15.1 %collective-permute-start.7 = (bf16[2,2,1,1,32,2048]{5,4,3,2,1,0:T(8,128)(2,1)}, bf16[2,2,1,1,32,2048]{5,4,3,2,1,0:T(8,128)(2,1)}, u32[]{:S(2)}, u32[]{:S(2)}) collective-permute-start(bf16[2,2,1,1,32,2048]{5,4,3,2,1,0:T(8,128)(2,1)} %constant_dynamic-slice_fusion.1), channel_id=1, source_target_pairs={{0,1},{1,0},{2,3},{3,2},{4,5},{5,4},{6,7},{7,6},{8,9},{9,8},{10,11... | collective-permute-start | bytes 1572872 | tf_op jit(solution)/shard_map/ppermute | solution.py:679
  225.2 18.6 %collective-permute-start.5 = (bf16[2,1,1,2,32,2048]{5,4,3,2,1,0:T(8,128)(2,1)}, bf16[2,1,1,2,32,2048]{5,4,3,2,1,0:T(8,128)(2,1)}, u32[]{:S(2)}, u32[]{:S(2)}) collective-permute-start(bf16[2,1,1,2,32,2048]{5,4,3,2,1,0:T(8,128)(2,1)} %constant_dynamic-slice_fusion.3), channel_id=1, source_target_pairs={{0,4},{2,6},{4,0},{6,2},{1,5},{3,7},{5,1},{7,3},{8,12},{10,14},{12... | collective-permute-start | bytes 1572872 | tf_op jit(solution)/shard_map/ppermute | solution.py:679
  226.8 25.6 %all-to-all-start.6 = ((bf16[8,320,128]{2,1,0:T(8,128)(2,1)}), bf16[8,320,128]{2,1,0:T(8,128)(2,1)S(1)}, u32[]{:S(2)}, u32[]{:S(2)}) async-start(bf16[8,320,128]{2,1,0:T(8,128)(2,1)} %broadcast_in_dim.18), calls=%async_computation.6 | async-start | bytes 1310720 | tf_op jit(solution)/shard_map/all_to_all | solution.py:645
  239.6 11.6 %collective-permute-start.8 = (bf16[2,1,1,1,32,2048]{5,4,3,2,1,0:T(8,128)(2,1)S(1)}, bf16[2,1,1,1,32,2048]{5,4,3,2,1,0:T(8,128)(2,1)S(1)}, u32[]{:S(2)}, u32[]{:S(2)}) collective-permute-start(bf16[2,1,1,1,32,2048]{5,4,3,2,1,0:T(8,128)(2,1)S(1)} %constant_dynamic-slice_fusion), channel_id=1, source_target_pairs={{0,4},{2,6},{4,0},{6,2},{1,5},{3,7},{5,1},{7,3},{8,12},{10,14},{12... | collective-permute-start | bytes 786440 | tf_op jit(solution)/shard_map/ppermute | solution.py:679
  245.1 6.4 %collective-permute-start.6 = (bf16[2,1,1,1,32,2048]{5,4,3,2,1,0:T(8,128)(2,1)S(1)}, bf16[2,1,1,1,32,2048]{5,4,3,2,1,0:T(8,128)(2,1)S(1)}, u32[]{:S(2)}, u32[]{:S(2)}) collective-permute-start(bf16[2,1,1,1,32,2048]{5,4,3,2,1,0:T(8,128)(2,1)S(1)} %constant_dynamic-slice_fusion.2), channel_id=1, source_target_pairs={{0,1},{1,0},{2,3},{3,2},{4,5},{5,4},{6,7},{7,6},{8,9},{9,8},{10,11... | collective-permute-start | bytes 786440 | tf_op jit(solution)/shard_map/ppermute | solution.py:679
  252.4 18.0 %all-to-all-start.7 = ((bf16[4,32,2048]{2,1,0:T(8,128)(2,1)}), bf16[4,32,2048]{2,1,0:T(8,128)(2,1)S(1)}, u32[]{:S(2)}, u32[]{:S(2)}) async-start(bf16[4,32,2048]{2,1,0:T(8,128)(2,1)} %maximum_bitcast_fusion), calls=%async_computation.7 | async-start | bytes 1048576 | tf_op jit(solution)/shard_map/all_to_all | solution.py:128
  (8 other events, 17.0 us)

commit v4 on v3

--- a/solution.py
+++ b/solution.py
@@ -200,29 +200,50 @@
 
 
 def convolve_rows(
-    src, base, kernel_ref, prod, rows_out, width, chunks, finish, carry, flipped=False
+    src, base, kernel_ref, prod, pair, rows_out, width, chunks, finish, carry, flipped=False
 ):
     step = rows_out // chunks
-    size = step * width
+    pairs = step // 2
+    size = pairs * width
     order = (2, 1, 0) if flipped else (0, 1, 2)
+    channels = kernel_ref.shape[0] // 3
+    side = 3 * channels
+
+    @pl.when(pl.program_id(0) == 0)
+    def _():
+        pair[...] = jnp.zeros(pair.shape, BF)
+        for row in range(2):
+            for tap, dy in enumerate(order):
+                at = (row + dy) * channels
+                pair[at : at + channels, row * side : (row + 1) * side] = kernel_ref[
+                    tap * channels : (tap + 1) * channels, :
+                ]
 
     def chunk(index, carry):
         start = base + index * step
-        lhs = jnp.concatenate([src[span(start + dy, width, step), :] for dy in order], 1)
-        prod[pl.ds(8, size), :] = jnp.dot(lhs, kernel_ref[...], preferred_element_type=F32)
-        channels = prod.shape[1] // 3
-
-        def row(r, carry):
-            view = prod.at[span8(r * width, width + 16), :]
-            first, _, last = order
-            value = (
-                view[7 + first : 7 + first + width, :channels]
-                + view[8 : 8 + width, channels : 2 * channels]
-                + view[7 + last : 7 + last + width, 2 * channels :]
-            )
-            return finish(index * step + r, value, carry)
-
-        return loop(step, row, carry)
+
+        def lane(j):
+            block = src[span(start + j // 2 * 2, width, step), :]
+            block = block.reshape(pairs, 2 * width, channels)
+            return block[:, j % 2 * width : (j % 2 + 1) * width].reshape(size, channels)
+
+        lhs = jnp.concatenate([lane(j) for j in range(4)], 1)
+        prod[pl.ds(8, size), :] = jnp.dot(lhs, pair[...], preferred_element_type=F32)
+        first, _, last = order
+
+        def rows(q, carry):
+            view = prod.at[span8(q * width, width + 16), :]
+            for row in range(2):
+                at = row * side
+                value = (
+                    view[7 + first : 7 + first + width, at : at + channels]
+                    + view[8 : 8 + width, at + channels : at + 2 * channels]
+                    + view[7 + last : 7 + last + width, at + 2 * channels : at + side]
+                )
+                carry = finish(index * step + 2 * q + row, value, carry)
+            return carry
+
+        return loop(pairs, rows, carry, unroll=2)
 
     return lax.fori_loop(0, chunks, chunk, carry)
 
@@ -292,7 +313,7 @@
 
 def forward_kernel(
     dims, extent, row_ref, col_ref, own_ref, above_ref, below_ref, left_ref, right_ref, kernel_ref,
-    act_ref, slope_ref, next_ref, copies_ref, raw_ref, prod, sums_ref, mask,
+    act_ref, slope_ref, next_ref, copies_ref, raw_ref, prod, pair, sums_ref, mask,
 ):
     height, breadth, width = dims
     mask[...], limit = inside_limits(2, extent, height, breadth, width)
@@ -303,8 +324,9 @@
         pre = value + row_ref[pl.ds(r, 1), :] + col_ref[...]
         sig = 0.5 * jnp.tanh(0.5 * pre) + 0.5
         ok = mask[...] > limit(r)
-        act_ref[span(r, width), :] = jnp.where(ok, pre * sig, 0.0).astype(BF)
-        slope_ref[span(r, width), :] = (sig * (1.0 + pre * (1.0 - sig))).astype(BF)
+        act = pre * sig
+        act_ref[span(r, width), :] = jnp.where(ok, act, 0.0).astype(BF)
+        slope_ref[span(r, width), :] = (sig + act * (1.0 - sig)).astype(BF)
 
     refs = (own_ref, above_ref, below_ref, left_ref, right_ref)
     place_rows(height + 4, breadth, 1, refs, activate)
@@ -323,13 +345,13 @@
         return total + jnp.where(inner, own, 0.0)
 
     sums_ref[pl.ds(height, breadth), :] = convolve_rows(
-        act_ref, 0, kernel_ref, prod, height + 2, width, 2, finish, zero
+        act_ref, 0, kernel_ref, prod, pair, height + 2, width, 1, finish, zero
     )
     send_sums(sums_ref, copies_ref)
 
 
 def adjoint_kernel(
-    dims, own_ref, above_ref, below_ref, left_ref, right_ref, kernel_ref, wide_ref, out_ref, prod
+    dims, own_ref, above_ref, below_ref, left_ref, right_ref, kernel_ref, wide_ref, out_ref, prod, pair
 ):
     height, breadth, width = dims
 
@@ -343,7 +365,7 @@
         out_ref[span(r, width), :] = value.astype(BF)
         return carry
 
-    convolve_rows(wide_ref, 0, kernel_ref, prod, height + 2, width, 2, finish, 0, True)
+    convolve_rows(wide_ref, 0, kernel_ref, prod, pair, height + 2, width, 1, finish, 0, True)
 
 
 def context_kernel(dims, ring, side, parts_ref, bias_ref, row_ref, col_ref, rows, cols):
@@ -401,11 +423,12 @@
         pre = hid_ref[span(r, width), :].astype(F32) + row_ref[pl.ds(r, 1), :] + col_ref[...]
         sig = 0.5 * jnp.tanh(0.5 * pre) + 0.5
         ok = mask[...] > limit(r)
-        act_ref[span(r, width), :] = jnp.where(ok, pre * sig, 0.0).astype(BF)
+        act = pre * sig
+        act_ref[span(r, width), :] = jnp.where(ok, act, 0.0).astype(BF)
         here, after = span(r, width), span(r + 1, width)
         adj = jnp.where(low, adj_low[here, :].astype(F32), adj_high[here, :].astype(F32))
         grad = jnp.where(low, grad_low[after, :].astype(F32), grad_high[after, :].astype(F32))
-        dz = adj * (sig * (1.0 + pre * (1.0 - sig)))
+        dz = adj * (sig + act * (1.0 - sig))
         next_ref[here, :] = (grad + dz).astype(BF)
         own = dz[edge : edge + breadth]
         inner = (r >= 1) & (r <= height)
@@ -422,7 +445,7 @@
 
 def backward_kernel(
     dims, extent, row_ref, col_ref, part_ref, slope_ref, kernel_ref,
-    grad_ref, next_ref, copies_ref, bias_ref, prod, sums_ref, mask,
+    grad_ref, next_ref, copies_ref, bias_ref, prod, pair, sums_ref, mask,
 ):
     height, breadth, width = dims
     mask[...], limit = inside_limits(1, extent, height, breadth, width)
@@ -449,7 +472,7 @@
         return total + own, bias + grad
 
     total, bias = convolve_rows(
-        grad_ref, 0, kernel_ref, prod, height, width, 2, finish, (zero, zero), True
+        grad_ref, 0, kernel_ref, prod, pair, height, width, 1, finish, (zero, zero), True
     )
     sums_ref[pl.ds(height, breadth), :] = total
     send_sums(sums_ref, copies_ref)
@@ -742,7 +765,10 @@
     copies = ((bands, planes, height + breadth, channels), BF, "copies")
     sums = pltpu.VMEM((height + breadth, channels), F32)
     one = ((planes, 1, channels), F32, False)
-    prod = lambda rows: pltpu.VMEM((rows * width + 16, side), F32)
+    prod = lambda rows: [
+        pltpu.VMEM((rows // 2 * width + 16, 2 * side), F32),
+        pltpu.VMEM((4 * channels, 2 * side), BF),
+    ]
     conv_flops = lambda rows: 2 * rows * width * side * side
     mask = pltpu.VMEM((width, channels), F32)
 
@@ -788,7 +814,7 @@
                 ((count, (height + 4) * width, channels), BF, False),
                 ((count, (height + 2) * width, channels), BF, False),
             ],
-            [prod(height // 2 + 1)],
+            prod(height + 2),
             conv_flops(height + 2),
         )
 
@@ -802,7 +828,7 @@
         + [(array, False) for array in (above, below, left, right)]
         + [(ahead, True)],
         [(flat(height + 4), BF, False)] * 2 + [(flat(height + 2), BF, False), copies],
-        [pltpu.VMEM(flat(height + 4)[1:], F32), prod(height // 2 + 1), sums, mask]
+        [pltpu.VMEM(flat(height + 4)[1:], F32), *prod(height + 2), sums, mask]
         + room,
         conv_flops(height + 2),
     )
@@ -843,7 +869,7 @@
         given + [(part1, False), (slope0, False), (back[0], True)],
         [(flat(height + 2), BF, False), ((planes, height * breadth, channels), BF, False)]
         + [copies, one],
-        [prod(height // 2), sums, mask] + room,
+        [*prod(height), sums, mask] + room,
         conv_flops(height),
     )
     piece = -(-(18 * channels + 2) // bands)

time: 273 us -> 267 us (0.978)
  Pallas kernels: 128 us -> 119 us
  waiting for transfers between devices: 51 us -> 54 us
    pallas_call x9, Pallas kernels: 128 us -> 119 us  [call(): pl.pallas_call(kernel, grid=(planes,), in_specs=[spec(a.shape, kind) for...]
    all_to_all x4, waiting for transfers between devices: 12.2 us -> 15.1 us  [contexts(): parts = lax.all_to_all(parts, BANDS, 0, 0, tiled=True)]
where the time goes in v4:
time: 267 us; the launch traced here: 265 us
  Pallas kernels  119 us (45%)
  waiting for transfers between devices  54 us (20%)
  starting transfers between devices  46.3 us (17%)
  local copies, waits for them, and re-layouts  20.9 us (8%)
  matrix products  13.5 us (5%)
  other arithmetic  10.8 us (4%)
    pallas_call x9, Pallas kernels, call(): pl.pallas_call(kernel, grid=(planes,), in_specs=[spec(a.shape, kind) for...  119 us
    all_to_all x4, starting transfers between devices, contexts(): parts = lax.all_to_all(parts, BANDS, 0, 0, tiled=True)  18.1 us
    ppermute x5, waiting for transfers between devices, halved(): other = lax.ppermute(theirs, axis, [(i, i ^ step) for i in range(size)])  17.1 us
    all_to_all x4, waiting for transfers between devices, contexts(): parts = lax.all_to_all(parts, BANDS, 0, 0, tiled=True)  15.1 us
    all_to_all x1, waiting for transfers between devices, scattered(): return jnp.sum(lax.all_to_all(parts, axes, 0, 0, tiled=True).astype(F32), 0)  11.1 us
    ppermute x4, starting transfers between devices, shifted(): return lax.ppermute(array, axis, pairs)  8.41 us
    all_to_all x2, starting transfers between devices, sent_to_all(): return lax.all_to_all(copies, axes, 0, 0, tiled=True)  8.41 us
    dot_general x1, matrix products, kernel_pass(): lax.dot_general(tap_grads, deconv_weight, (((1,), (1,)), ((), ())), prefe...  7.87 us
  transfers between devices with their start and end apart: 17, of which 14 were waited for; matrix products, arithmetic and copies ran while one was open for 10% of the time, Pallas kernels for 20%

profile of v4, /device:TPU:0, one launch (start us, length us, event | category | flops | bytes accessed | tf_op | source)
XLA Modules:
  0.0 265.2 jit_solution(10976351090160593650)
XLA Ops:
  0.6 10.9 %shard_map.101 = (f32[6,2048,128]{2,1,0:T(8,128)}, bf16[8,6,96,128]{3,2,1,0:T(8,128)(2,1)}, bf16[6,256,128]{2,1,0:T(8,128)(2,1)}, bf16[6,256,128]{2,1,0:T(8,128)(2,1)}, f32[6,1,128]{2,1,0:T(1,128)}) custom-call(bf16[6,128,1024]{2,1,0:T(8,128)(2,1)} %bitcast.110, bf16[6,2048,128]{2,1,0:T(8,128)(2,1)} %bitcast.101, bf16[1024,2048]{1,0:T(8,128)(2,1)} %weight_ref.1), custom_call_target="tpu_custom_call" | custom-call | flops 3221225472 | bytes 17825792 | tf_op jit(solution)/shard_map/pallas_call | solution.py:158
  34.2 7.1 %all-to-all-start = ((bf16[8,6,96,128]{3,2,1,0:T(8,128)(2,1)}), bf16[8,6,96,128]{3,2,1,0:T(8,128)(2,1)S(1)}, u32[]{:S(2)}, u32[]{:S(2)}) async-start(bf16[8,6,96,128]{3,2,1,0:T(8,128)(2,1)} %get-tuple-element.75), calls=%async_computation | async-start | bytes 2359296 | tf_op jit(solution)/shard_map/all_to_all | solution.py:776
  43.9 9.2 %shard_map.102 = (bf16[3,2880,128]{2,1,0:T(8,128)(2,1)}, bf16[3,2720,128]{2,1,0:T(8,128)(2,1)}) custom-call(bf16[6,2048,128]{2,1,0:T(8,128)(2,1)} %bitcast.103, bf16[6,256,128]{2,1,0:T(8,128)(2,1)} %copy-done.9, bf16[6,256,128]{2,1,0:T(8,128)(2,1)} %copy-done.10, f32[6,576,128]{2,1,0:T(8,128)} %bitcast.85, ...), custom_call_target="tpu_custom_call" | custom-call | flops 2406481920 | bytes 15532032 | tf_op jit(solution)/shard_map/pallas_call | solution.py:158
  53.2 4.3 %all-to-all-done.parts_ref = bf16[8,6,96,128]{3,2,1,0:T(8,128)(2,1)S(1)} async-done(((bf16[8,6,96,128]{3,2,1,0:T(8,128)(2,1)}), bf16[8,6,96,128]{3,2,1,0:T(8,128)(2,1)S(1)}, u32[]{:S(2)}, u32[]{:S(2)}) %all-to-all-start) | async-done | bytes 1179680 | tf_op jit(solution)/shard_map/all_to_all | solution.py:776
  58.5 21.9 %shard_map.103 = (bf16[6,2880,128]{2,1,0:T(8,128)(2,1)}, bf16[6,2880,128]{2,1,0:T(8,128)(2,1)}, bf16[6,2720,128]{2,1,0:T(8,128)(2,1)}, bf16[8,6,96,128]{3,2,1,0:T(8,128)(2,1)}) custom-call(bf16[8,6,96,128]{3,2,1,0:T(8,128)(2,1)} %copy-done.7, f32[1,128]{1,0:T(1,128)} %bitcast.112, f32[6,2048,128]{2,1,0:T(8,128)} %get-tuple-element.65.refs_0_, ...), custom_call_target="tpu_custom_call" | custom-call | flops 4812963840 | bytes 24183808 | tf_op jit(solution)/shard_map/pallas_call | solution.py:158
  80.4 3.7 %all-to-all-start.1 = ((bf16[8,6,96,128]{3,2,1,0:T(8,128)(2,1)}), bf16[8,6,96,128]{3,2,1,0:T(8,128)(2,1)S(1)}, u32[]{:S(2)}, u32[]{:S(2)}) async-start(bf16[8,6,96,128]{3,2,1,0:T(8,128)(2,1)} %get-tuple-element.81), calls=%async_computation.1 | async-start | bytes 2359296 | tf_op jit(solution)/shard_map/all_to_all | solution.py:776
  84.7 9.2 %shard_map.104 = (bf16[3,2880,128]{2,1,0:T(8,128)(2,1)}, bf16[3,2720,128]{2,1,0:T(8,128)(2,1)}) custom-call(bf16[6,2048,128]{2,1,0:T(8,128)(2,1)} %bitcast.104, bf16[6,256,128]{2,1,0:T(8,128)(2,1)} %copy-done.9, bf16[6,256,128]{2,1,0:T(8,128)(2,1)} %copy-done.10, f32[6,576,128]{2,1,0:T(8,128)} %bitcast.87, ...), custom_call_target="tpu_custom_call" | custom-call | flops 2406481920 | bytes 15532032 | tf_op jit(solution)/shard_map/pallas_call | solution.py:158
  93.9 6.4 %all-to-all-done.1.parts_ref = bf16[8,6,96,128]{3,2,1,0:T(8,128)(2,1)S(1)} async-done(((bf16[8,6,96,128]{3,2,1,0:T(8,128)(2,1)}), bf16[8,6,96,128]{3,2,1,0:T(8,128)(2,1)S(1)}, u32[]{:S(2)}, u32[]{:S(2)}) %all-to-all-start.1) | async-done | bytes 1179680 | tf_op jit(solution)/shard_map/all_to_all | solution.py:776
  101.3 15.1 %shard_map.105 = (bf16[6,2720,128]{2,1,0:T(8,128)(2,1)}, bf16[6,2720,128]{2,1,0:T(8,128)(2,1)}, bf16[8,6,96,128]{3,2,1,0:T(8,128)(2,1)}) custom-call(bf16[8,6,96,128]{3,2,1,0:T(8,128)(2,1)} %copy-done.1, f32[1,128]{1,0:T(1,128)} %fusion.2.bias_ref, bf16[6,2720,128]{2,1,0:T(8,128)(2,1)} %get-tuple-element.85.refs_0_, ...), custom_call_target="tpu_custom_call" | custom-call | bytes 27919360 | tf_op jit(solution)/shard_map/pallas_call | solution.py:158
  116.4 3.7 %all-to-all-start.2 = ((bf16[8,6,96,128]{3,2,1,0:T(8,128)(2,1)}), bf16[8,6,96,128]{3,2,1,0:T(8,128)(2,1)S(1)}, u32[]{:S(2)}, u32[]{:S(2)}) async-start(bf16[8,6,96,128]{3,2,1,0:T(8,128)(2,1)} %get-tuple-element.90), calls=%async_computation.2 | async-start | bytes 2359296 | tf_op jit(solution)/shard_map/all_to_all | solution.py:776
  121.0 13.2 %shard_map.106.refs_0_ = bf16[1152,128]{1,0:T(8,128)(2,1)} custom-call(bf16[6,2720,128]{2,1,0:T(8,128)(2,1)} %get-tuple-element.91.act_ref, bf16[6,2048,128]{2,1,0:T(8,128)(2,1)} %bitcast.105), custom_call_target="tpu_custom_call" | custom-call | flops 4529848320 | bytes 14647296 | tf_op jit(solution)/shard_map/pallas_call | solution.py:158
  137.2 18.6 %shard_map.107 = (bf16[6,2720,128]{2,1,0:T(8,128)(2,1)}, bf16[6,2048,128]{2,1,0:T(8,128)(2,1)}, bf16[8,6,96,128]{3,2,1,0:T(8,128)(2,1)}, f32[6,1,128]{2,1,0:T(1,128)}) custom-call(bf16[8,6,96,128]{3,2,1,0:T(8,128)(2,1)} %copy-done.8, f32[1,128]{1,0:T(1,128)} %broadcast_1_bias_ref.2.bias_ref, bf16[6,2720,128]{2,1,0:T(8,128)(2,1)} %get-tuple-element.93.refs_0_, ...), custom_call_target="tpu_custom_call" | custom-call | flops 4529848320 | bytes 20153344 | tf_op jit(solution)/shard_map/pallas_call | solution.py:158
  155.8 3.6 %all-to-all-start.3 = ((bf16[8,6,96,128]{3,2,1,0:T(8,128)(2,1)}), bf16[8,6,96,128]{3,2,1,0:T(8,128)(2,1)S(1)}, u32[]{:S(2)}, u32[]{:S(2)}) async-start(bf16[8,6,96,128]{3,2,1,0:T(8,128)(2,1)} %get-tuple-element.95), calls=%async_computation.3 | async-start | bytes 2359296 | tf_op jit(solution)/shard_map/all_to_all | solution.py:776
  159.4 13.6 %shard_map.108 = bf16[2432,128]{1,0:T(8,128)(2,1)} custom-call(bf16[6,2880,128]{2,1,0:T(8,128)(2,1)} %get-tuple-element.96.act_ref, bf16[6,2720,128]{2,1,0:T(8,128)(2,1)} %get-tuple-element.97.grad_ref, bf16[1152,128]{1,0:T(8,128)(2,1)} %shard_map.106.refs_0_, f32[6,1,128]{2,1,0:T(1,128)} %get-tuple-element.99.refs_1_, f32[6,1,128]{2,1,0:T(1,128)} %get-tuple-element.100.refs_2_), custom_call_target="tpu_custom_call" | custom-call | flops 4529848320 | bytes 17805312 | tf_op jit(solution)/shard_map/pallas_call | solution.py:158
  179.1 6.7 %shard_map.109 = (bf16[6,128,2048]{2,1,0:T(8,128)(2,1)}, f32[6,1,128]{2,1,0:T(1,128)}) custom-call(bf16[8,6,96,128]{3,2,1,0:T(8,128)(2,1)} %copy-done, f32[1,128]{1,0:T(1,128)} %broadcast_1_bias_ref.2.bias_ref, bf16[6,2048,128]{2,1,0:T(8,128)(2,1)} %get-tuple-element.102.refs_0_), custom_call_target="tpu_custom_call" | custom-call | bytes 8651776 | tf_op jit(solution)/shard_map/pallas_call | solution.py:158
  189.2 5.6 %convolution_convert_fusion = bf16[2048,1024]{0,1:T(8,128)(2,1)S(1)} fusion(bf16[768,2048]{1,0:T(8,128)(2,1)} %bitcast.108, bf16[768,1024]{1,0:T(8,128)(2,1)S(1)} %bitcast.111), kind=kOutput, calls=%fused_computation.1 | convolution fusion | flops 3223322624 | bytes 8912896 | tf_op jit(solution)/shard_map/dot_general | solution.py:890
  199.3 4.9 %all-to-all-start.5 = ((bf16[4,320,128]{2,1,0:T(8,128)(2,1)}), bf16[4,320,128]{2,1,0:T(8,128)(2,1)S(1)}, u32[]{:S(2)}, u32[]{:S(2)}) async-start(bf16[4,320,128]{2,1,0:T(8,128)(2,1)} %broadcast_in_dim.8), calls=%async_computation.5 | async-start | bytes 655360 | tf_op jit(solution)/shard_map/all_to_all | solution.py:668
  204.2 7.9 %convolution_convert_fusion.1 = bf16[768,1024]{1,0:T(8,128)(2,1)} fusion(bf16[768,2048]{1,0:T(8,128)(2,1)} %bitcast.109, bf16[1024,2048]{1,0:T(8,128)(2,1)} %weight_ref.1), kind=kOutput, calls=%fused_computation.2 | convolution fusion | flops 3222011904 | bytes 8912896 | tf_op jit(solution)/shard_map/dot_general | solution.py:895
  220.7 3.5 %all-to-all-start.6 = ((bf16[8,320,128]{2,1,0:T(8,128)(2,1)}), bf16[8,320,128]{2,1,0:T(8,128)(2,1)S(1)}, u32[]{:S(2)}, u32[]{:S(2)}) async-start(bf16[8,320,128]{2,1,0:T(8,128)(2,1)} %broadcast_in_dim.18), calls=%async_computation.6 | async-start | bytes 1310720 | tf_op jit(solution)/shard_map/all_to_all | solution.py:668
  224.3 8.0 %collective-permute-done.7 = bf16[2,2,1,1,32,2048]{5,4,3,2,1,0:T(8,128)(2,1)} collective-permute-done((bf16[2,2,1,1,32,2048]{5,4,3,2,1,0:T(8,128)(2,1)}, bf16[2,2,1,1,32,2048]{5,4,3,2,1,0:T(8,128)(2,1)}, u32[]{:S(2)}, u32[]{:S(2)}) %collective-permute-start.7) | collective-permute-done | bytes 524320 | tf_op jit(solution)/shard_map/ppermute | solution.py:702
  234.1 3.6 %collective-permute-done.5 = bf16[2,1,1,2,32,2048]{5,4,3,2,1,0:T(8,128)(2,1)} collective-permute-done((bf16[2,1,1,2,32,2048]{5,4,3,2,1,0:T(8,128)(2,1)}, bf16[2,1,1,2,32,2048]{5,4,3,2,1,0:T(8,128)(2,1)}, u32[]{:S(2)}, u32[]{:S(2)}) %collective-permute-start.5) | collective-permute-done | bytes 524320 | tf_op jit(solution)/shard_map/ppermute | solution.py:702
  239.8 5.2 %collective-permute-done.8 = bf16[2,1,1,1,32,2048]{5,4,3,2,1,0:T(8,128)(2,1)S(1)} collective-permute-done((bf16[2,1,1,1,32,2048]{5,4,3,2,1,0:T(8,128)(2,1)S(1)}, bf16[2,1,1,1,32,2048]{5,4,3,2,1,0:T(8,128)(2,1)S(1)}, u32[]{:S(2)}, u32[]{:S(2)}) %collective-permute-start.8) | collective-permute-done | bytes 262176 | tf_op jit(solution)/shard_map/ppermute | solution.py:702
  246.4 4.6 %all-to-all-start.7 = ((bf16[4,32,2048]{2,1,0:T(8,128)(2,1)}), bf16[4,32,2048]{2,1,0:T(8,128)(2,1)S(1)}, u32[]{:S(2)}, u32[]{:S(2)}) async-start(bf16[4,32,2048]{2,1,0:T(8,128)(2,1)} %maximum_bitcast_fusion), calls=%async_computation.7 | async-start | bytes 1048576 | tf_op jit(solution)/shard_map/all_to_all | solution.py:128
  253.3 11.1 %all-to-all-done.7 = bf16[4,32,2048]{2,1,0:T(8,128)(2,1)S(1)} async-done(((bf16[4,32,2048]{2,1,0:T(8,128)(2,1)}), bf16[4,32,2048]{2,1,0:T(8,128)(2,1)S(1)}, u32[]{:S(2)}, u32[]{:S(2)}) %all-to-all-start.7) | async-done | bytes 524320 | tf_op jit(solution)/shard_map/all_to_all | solution.py:128
  (100 shorter events, 62.3 us)
Async XLA Ops:
  11.6 6.6 %collective-permute-start = (bf16[6,256,128]{2,1,0:T(8,128)(2,1)}, bf16[6,256,128]{2,1,0:T(8,128)(2,1)S(1)}, u32[]{:S(2)}, u32[]{:S(2)}) collective-permute-start(bf16[6,256,128]{2,1,0:T(8,128)(2,1)} %get-tuple-element.60), channel_id=1, source_target_pairs={{0,2},{2,4},{4,6},{1,3},{3,5},{5,7},{8,10},{10,12},{12,14},{9,11},... | collective-permute-start | bytes 1179656 | tf_op jit(solution)/shard_map/ppermute | solution.py:20
  14.0 5.9 %collective-permute-start.1 = (bf16[6,256,128]{2,1,0:T(8,128)(2,1)}, bf16[6,256,128]{2,1,0:T(8,128)(2,1)S(1)}, u32[]{:S(2)}, u32[]{:S(2)}) collective-permute-start(bf16[6,256,128]{2,1,0:T(8,128)(2,1)} %get-tuple-element.61), channel_id=1, source_target_pairs={{2,0},{4,2},{6,4},{3,1},{5,3},{7,5},{10,8},{12,10},{14,12},{11,9},... | collective-permute-start | bytes 1179656 | tf_op jit(solution)/shard_map/ppermute | solution.py:20
  18.1 7.9 %copy-start.9 = (bf16[6,256,128]{2,1,0:T(8,128)(2,1)}, bf16[6,256,128]{2,1,0:T(8,128)(2,1)S(1)}, u32[]{:S(2)}) copy-start(bf16[6,256,128]{2,1,0:T(8,128)(2,1)S(1)} %collective-permute-done.above_ref.refs_1_) | copy-start | bytes 1179652
  19.9 7.6 %copy-start.10 = (bf16[6,256,128]{2,1,0:T(8,128)(2,1)}, bf16[6,256,128]{2,1,0:T(8,128)(2,1)S(1)}, u32[]{:S(2)}) copy-start(bf16[6,256,128]{2,1,0:T(8,128)(2,1)S(1)} %collective-permute-done.1.below_ref.refs_2_) | copy-start | bytes 1179652
  20.7 6.8 %collective-permute-start.2 = (bf16[6,36,2,2,128]{4,3,1,0,2:T(2,128)(2,1)S(1)}, bf16[6,36,2,2,128]{4,3,1,0,2:T(2,128)(2,1)S(1)}, u32[]{:S(2)}, u32[]{:S(2)}) collective-permute-start(bf16[6,36,2,2,128]{4,3,1,0,2:T(2,128)(2,1)S(1)} %pad_maximum_fusion), channel_id=1, source_target_pairs={{0,1},{2,3},{4,5},{6,7},{8,9},{10,11},{12,13},{14,15},{16,17},{18,... | collective-permute-start | bytes 663560 | tf_op jit(solution)/shard_map/ppermute | solution.py:20
  24.7 7.8 %collective-permute-start.3 = (bf16[6,36,2,2,128]{4,3,2,1,0:T(2,128)(2,1)S(1)}, bf16[6,36,2,2,128]{4,3,2,1,0:T(2,128)(2,1)S(1)}, u32[]{:S(2)}, u32[]{:S(2)}) collective-permute-start(bf16[6,36,2,2,128]{4,3,2,1,0:T(2,128)(2,1)S(1)} %pad_maximum_fusion.1), channel_id=1, source_target_pairs={{1,0},{3,2},{5,4},{7,6},{9,8},{11,10},{13,12},{15,14},{17,16},{19,... | collective-permute-start | bytes 663560 | tf_op jit(solution)/shard_map/ppermute | solution.py:20
  32.7 8.5 %copy-start.6 = (bf16[2,1152,128]{2,1,0:T(8,128)(2,1)S(1)}, bf16[2,1152,128]{2,1,0:T(8,128)(2,1)}, u32[]{:S(2)}) copy-start(bf16[2,1152,128]{2,1,0:T(8,128)(2,1)} %param.10) | copy-start | bytes 1769476
  34.2 23.3 %all-to-all-start = ((bf16[8,6,96,128]{3,2,1,0:T(8,128)(2,1)}), bf16[8,6,96,128]{3,2,1,0:T(8,128)(2,1)S(1)}, u32[]{:S(2)}, u32[]{:S(2)}) async-start(bf16[8,6,96,128]{3,2,1,0:T(8,128)(2,1)} %get-tuple-element.75), calls=%async_computation | async-start | bytes 2359296 | tf_op jit(solution)/shard_map/all_to_all | solution.py:776
  80.4 3.7 %copy-start.14 = (f32[128]{0:T(128)S(1)}, f32[128]{0:T(128)}, u32[]{:S(2)}) copy-start(f32[128]{0:T(128)} %param.9) | copy-start | bytes 1540
  80.4 19.9 %all-to-all-start.1 = ((bf16[8,6,96,128]{3,2,1,0:T(8,128)(2,1)}), bf16[8,6,96,128]{3,2,1,0:T(8,128)(2,1)S(1)}, u32[]{:S(2)}, u32[]{:S(2)}) async-start(bf16[8,6,96,128]{3,2,1,0:T(8,128)(2,1)} %get-tuple-element.81), calls=%async_computation.1 | async-start | bytes 2359296 | tf_op jit(solution)/shard_map/all_to_all | solution.py:776
  116.4 19.7 %all-to-all-start.2 = ((bf16[8,6,96,128]{3,2,1,0:T(8,128)(2,1)}), bf16[8,6,96,128]{3,2,1,0:T(8,128)(2,1)S(1)}, u32[]{:S(2)}, u32[]{:S(2)}) async-start(bf16[8,6,96,128]{3,2,1,0:T(8,128)(2,1)} %get-tuple-element.90), calls=%async_computation.2 | async-start | bytes 2359296 | tf_op jit(solution)/shard_map/all_to_all | solution.py:776
  155.8 19.7 %all-to-all-start.3 = ((bf16[8,6,96,128]{3,2,1,0:T(8,128)(2,1)}), bf16[8,6,96,128]{3,2,1,0:T(8,128)(2,1)S(1)}, u32[]{:S(2)}, u32[]{:S(2)}) async-start(bf16[8,6,96,128]{3,2,1,0:T(8,128)(2,1)} %get-tuple-element.95), calls=%async_computation.3 | async-start | bytes 2359296 | tf_op jit(solution)/shard_map/all_to_all | solution.py:776
  175.5 13.7 %all-to-all-start.4 = ((bf16[8,304,128]{2,1,0:T(8,128)(2,1)}), bf16[8,304,128]{2,1,0:T(8,128)(2,1)S(1)}, u32[]{:S(2)}, u32[]{:S(2)}) async-start(bf16[8,304,128]{2,1,0:T(8,128)(2,1)} %bitcast.94), calls=%async_computation.4 | async-start | bytes 1245184 | tf_op jit(solution)/shard_map/all_to_all | solution.py:880
  179.1 10.1 %copy-start.12 = (bf16[2,3,8,16,1024]{4,3,2,1,0:T(8,128)(2,1)S(1)}, bf16[2,3,8,16,1024]{4,3,2,1,0:T(8,128)(2,1)}, u32[]{:S(2)}) copy-start(bf16[2,3,8,16,1024]{4,3,2,1,0:T(8,128)(2,1)} %param.6) | copy-start | bytes 4718596
  198.4 13.6 %collective-permute-start.4 = (bf16[4,2,1,2,32,2048]{5,4,3,2,1,0:T(8,128)(2,1)}, bf16[4,2,1,2,32,2048]{5,4,3,2,1,0:T(8,128)(2,1)}, u32[]{:S(2)}, u32[]{:S(2)}) collective-permute-start(bf16[4,2,1,2,32,2048]{5,4,3,2,1,0:T(8,128)(2,1)} %constant_dynamic-slice_fusion.4), channel_id=1, source_target_pairs={{0,2},{2,0},{4,6},{6,4},{1,3},{3,1},{5,7},{7,5},{8,10},{10,8},{12,... | collective-permute-start | bytes 6291464 | tf_op jit(solution)/shard_map/ppermute | solution.py:702
  199.3 15.8 %all-to-all-start.5 = ((bf16[4,320,128]{2,1,0:T(8,128)(2,1)}), bf16[4,320,128]{2,1,0:T(8,128)(2,1)S(1)}, u32[]{:S(2)}, u32[]{:S(2)}) async-start(bf16[4,320,128]{2,1,0:T(8,128)(2,1)} %broadcast_in_dim.8), calls=%async_computation.5 | async-start | bytes 655360 | tf_op jit(solution)/shard_map/all_to_all | solution.py:668
  204.2 7.9 %copy-start.3 = (bf16[2048,1024]{0,1:T(8,128)(2,1)S(1)}, bf16[2048,1024]{0,1:T(8,128)(2,1)}, u32[]{:S(2)}) copy-start(bf16[2048,1024]{0,1:T(8,128)(2,1)} %copy-done.2) | copy-start | bytes 12582916
  217.2 15.1 %copy-start.5 = (bf16[2,2,1,2,32,2048]{5,4,3,2,1,0:T(8,128)(2,1)S(1)}, bf16[2,2,1,2,32,2048]{5,4,3,2,1,0:T(8,128)(2,1)}, u32[]{:S(2)}) copy-start(bf16[2,2,1,2,32,2048]{5,4,3,2,1,0:T(8,128)(2,1)} %copy-done.4) | copy-start | bytes 3145732
  217.2 15.1 %collective-permute-start.7 = (bf16[2,2,1,1,32,2048]{5,4,3,2,1,0:T(8,128)(2,1)}, bf16[2,2,1,1,32,2048]{5,4,3,2,1,0:T(8,128)(2,1)}, u32[]{:S(2)}, u32[]{:S(2)}) collective-permute-start(bf16[2,2,1,1,32,2048]{5,4,3,2,1,0:T(8,128)(2,1)} %constant_dynamic-slice_fusion.1), channel_id=1, source_target_pairs={{0,1},{1,0},{2,3},{3,2},{4,5},{5,4},{6,7},{7,6},{8,9},{9,8},{10,11... | collective-permute-start | bytes 1572872 | tf_op jit(solution)/shard_map/ppermute | solution.py:702
  219.1 18.6 %collective-permute-start.5 = (bf16[2,1,1,2,32,2048]{5,4,3,2,1,0:T(8,128)(2,1)}, bf16[2,1,1,2,32,2048]{5,4,3,2,1,0:T(8,128)(2,1)}, u32[]{:S(2)}, u32[]{:S(2)}) collective-permute-start(bf16[2,1,1,2,32,2048]{5,4,3,2,1,0:T(8,128)(2,1)} %constant_dynamic-slice_fusion.3), channel_id=1, source_target_pairs={{0,4},{2,6},{4,0},{6,2},{1,5},{3,7},{5,1},{7,3},{8,12},{10,14},{12... | collective-permute-start | bytes 1572872 | tf_op jit(solution)/shard_map/ppermute | solution.py:702
  220.7 25.6 %all-to-all-start.6 = ((bf16[8,320,128]{2,1,0:T(8,128)(2,1)}), bf16[8,320,128]{2,1,0:T(8,128)(2,1)S(1)}, u32[]{:S(2)}, u32[]{:S(2)}) async-start(bf16[8,320,128]{2,1,0:T(8,128)(2,1)} %broadcast_in_dim.18), calls=%async_computation.6 | async-start | bytes 1310720 | tf_op jit(solution)/shard_map/all_to_all | solution.py:668
  233.5 11.6 %collective-permute-start.8 = (bf16[2,1,1,1,32,2048]{5,4,3,2,1,0:T(8,128)(2,1)S(1)}, bf16[2,1,1,1,32,2048]{5,4,3,2,1,0:T(8,128)(2,1)S(1)}, u32[]{:S(2)}, u32[]{:S(2)}) collective-permute-start(bf16[2,1,1,1,32,2048]{5,4,3,2,1,0:T(8,128)(2,1)S(1)} %constant_dynamic-slice_fusion), channel_id=1, source_target_pairs={{0,4},{2,6},{4,0},{6,2},{1,5},{3,7},{5,1},{7,3},{8,12},{10,14},{12... | collective-permute-start | bytes 786440 | tf_op jit(solution)/shard_map/ppermute | solution.py:702
  239.0 6.4 %collective-permute-start.6 = (bf16[2,1,1,1,32,2048]{5,4,3,2,1,0:T(8,128)(2,1)S(1)}, bf16[2,1,1,1,32,2048]{5,4,3,2,1,0:T(8,128)(2,1)S(1)}, u32[]{:S(2)}, u32[]{:S(2)}) collective-permute-start(bf16[2,1,1,1,32,2048]{5,4,3,2,1,0:T(8,128)(2,1)S(1)} %constant_dynamic-slice_fusion.2), channel_id=1, source_target_pairs={{0,1},{1,0},{2,3},{3,2},{4,5},{5,4},{6,7},{7,6},{8,9},{9,8},{10,11... | collective-permute-start | bytes 786440 | tf_op jit(solution)/shard_map/ppermute | solution.py:702
  246.4 18.0 %all-to-all-start.7 = ((bf16[4,32,2048]{2,1,0:T(8,128)(2,1)}), bf16[4,32,2048]{2,1,0:T(8,128)(2,1)S(1)}, u32[]{:S(2)}, u32[]{:S(2)}) async-start(bf16[4,32,2048]{2,1,0:T(8,128)(2,1)} %maximum_bitcast_fusion), calls=%async_computation.7 | async-start | bytes 1048576 | tf_op jit(solution)/shard_map/all_to_all | solution.py:128
  (8 other events, 16.9 us)

commit v5 on v4

--- a/solution.py
+++ b/solution.py
@@ -654,7 +654,8 @@
     piece += -piece % 16
     small = jnp.pad(small, ((0, piece * bands - small.shape[0]), (0, 0))).astype(BF)
     small = lax.all_to_all(small.reshape(bands, piece, channels), BANDS, 0, 0, tiled=True)
-    small = small_whole(small_summed(small, bias_part))
+    small = lax.all_to_all(small_copies(small, bias_part), "obj", 0, 0, tiled=True)
+    small = small_whole(small)
     bands = lax.axis_size("plane") * lax.axis_size("tile")
     total = lax.axis_size("obj") * bands
     weight_grad = scatter_all(
@@ -668,10 +669,11 @@
     return lax.all_to_all(copies, axes, 0, 0, tiled=True)
 
 
-def small_summed(parts, bias_part):
+def small_copies(parts, bias_part):
     piece = jnp.sum(parts.astype(F32), 0)
     tail = jnp.pad(bias_part[None], ((0, 15), (0, 0)))
-    return sent_to_all(jnp.concatenate([piece, tail], 0).astype(BF), "obj")
+    piece = jnp.concatenate([piece, tail], 0).astype(BF)
+    return jnp.broadcast_to(piece[None], (lax.axis_size("obj"),) + piece.shape)
 
 
 def small_whole(parts):
@@ -694,13 +696,20 @@
     return steps
 
 
-def halved(parts, dim, axis, step):
+def parted(parts, dim, axis, step):
     upper = ((lax.axis_index(axis) // step) % 2).astype(jnp.int32)
+    mine = lax.dynamic_slice_in_dim(parts, upper, 1, dim)
+    return mine, lax.dynamic_slice_in_dim(parts, 1 - upper, 1, dim)
+
+
+def joined(mine, theirs, axis, step):
     size = lax.axis_size(axis)
-    mine = lax.dynamic_slice_in_dim(parts, upper, 1, dim)
-    theirs = lax.dynamic_slice_in_dim(parts, 1 - upper, 1, dim)
     other = lax.ppermute(theirs, axis, [(i, i ^ step) for i in range(size)])
     return (mine.astype(F32) + other.astype(F32)).astype(BF)
+
+
+def halved(parts, dim, axis, step):
+    return joined(*parted(parts, dim, axis, step), axis, step)
 
 
 def near_step():
@@ -716,16 +725,18 @@
     return halved(product.astype(BF).reshape(shape), dim, *step)
 
 
-def weight_scattered(parts):
+def weight_scattered(parts, beside):
     objs = parts.shape[0]
     steps = [("plane", s) for s in bits_of(lax.axis_size("plane"))]
     steps += [("tile", s) for s in bits_of(lax.axis_size("tile"))]
     rest = [(i + 1, step) for i, step in enumerate(steps) if i + 1 != near_step()[1]]
     streams = [parts[: objs // 2], parts[objs // 2 :]]
-    for one, two in zip(rest, reversed(rest)):
-        streams[0] = halved(streams[0], one[0], *one[1])
-        streams[1] = halved(streams[1], two[0], *two[1])
-    return jnp.concatenate(streams, 0).reshape(objs, *parts.shape[-2:])
+    for turn, pair in enumerate(zip(rest, reversed(rest))):
+        cut = [parted(stream, dim, *step) for stream, (dim, step) in zip(streams, pair)]
+        if turn == 0:
+            cut, beside = lax.optimization_barrier((cut, beside))
+        streams = [joined(*halves, *step) for halves, (_, step) in zip(cut, pair)]
+    return beside, jnp.concatenate(streams, 0).reshape(objs, *parts.shape[-2:])
 
 
 def kernel_pass(tokens, gout, deconv_weight, deconv_bias, conv_kernels, conv_biases):
@@ -886,19 +897,21 @@
         [pltpu.VMEM((height * breadth, channels), F32)] + room,
     )
     tap_grads = tap_grads.reshape(-1, up * up * channels)
-    tap_grads, small = lax.optimization_barrier((tap_grads, small))
+    copies = small_copies(small, jnp.sum(bias_part, (0, 1)))
+    tap_grads, copies = lax.optimization_barrier((tap_grads, copies))
+    small = lax.all_to_all(copies, "obj", 0, 0, tiled=True)
     product = lax.dot_general(
         tok.reshape(-1, fan), tap_grads, (((0,), (0,)), ((), ())), preferred_element_type=F32
     )
-    small = small_summed(small, jnp.sum(bias_part, (0, 1)))
     parts = weight_parts(product)
+    parts, small = lax.optimization_barrier((parts, small))
+    small = small_whole(small)
+    tap_grads, parts = weight_scattered(parts, tap_grads)
     tok_grad = lax.dot_general(
         tap_grads, deconv_weight, (((1,), (1,)), ((), ())), preferred_element_type=F32
     )
     tok_grad = tok_grad.astype(BF).reshape(tokens.shape)
     parts, small, tok_grad = lax.optimization_barrier((parts, small, tok_grad))
-    small = small_whole(small)
-    parts, small = lax.optimization_barrier((weight_scattered(parts), small))
     weight_grad = scattered(parts, "obj")
     return (tok_grad, weight_grad) + small_results(small, conv_kernels.shape[1])
 

time: 267 us -> 262 us (0.981)
    all_to_all x0 -> x1, waiting for transfers between devices: none -> 7.84 us  [kernel_pass(): small = lax.all_to_all(copies, 'obj', 0, 0, tiled=True)]
    ppermute x5, waiting for transfers between devices: 17.1 us -> 11.4 us  [joined(): other = lax.ppermute(theirs, axis, [(i, i ^ step) for i in range(size)])]
    all_to_all x0 -> x1, starting transfers between devices: none -> 4.88 us  [kernel_pass(): small = lax.all_to_all(copies, 'obj', 0, 0, tiled=True)]
    all_to_all x2 -> x1, starting transfers between devices: 8.41 us -> 3.54 us  [sent_to_all(): return lax.all_to_all(copies, axes, 0, 0, tiled=True)]
    unnamed x33 -> x25, local copies, waits for them, and re-layouts: 7.79 us -> 6.79 us
  transfers between devices with their start and end apart: 17 -> 17, of which waited for: 14 -> 13; matrix products, arithmetic and copies ran while one was open for 10% -> 10% of each run, Pallas kernels for 20% -> 20%
where the time goes in v5:
time: 262 us; the launch traced here: 261 us
  Pallas kernels  119 us (45%)
  waiting for transfers between devices  54.4 us (21%)
  starting transfers between devices  44.8 us (17%)
  local copies, waits for them, and re-layouts  18.4 us (7%)
  matrix products  13.3 us (5%)
  other arithmetic  9.96 us (4%)
    pallas_call x9, Pallas kernels, call(): pl.pallas_call(kernel, grid=(planes,), in_specs=[spec(a.shape, kind) for...  119 us
    all_to_all x4, starting transfers between devices, contexts(): parts = lax.all_to_all(parts, BANDS, 0, 0, tiled=True)  18.1 us
    all_to_all x4, waiting for transfers between devices, contexts(): parts = lax.all_to_all(parts, BANDS, 0, 0, tiled=True)  15.1 us
    ppermute x5, waiting for transfers between devices, joined(): other = lax.ppermute(theirs, axis, [(i, i ^ step) for i in range(size)])  11.4 us
    all_to_all x1, waiting for transfers between devices, scattered(): return jnp.sum(lax.all_to_all(parts, axes, 0, 0, tiled=True).astype(F32), 0)  10.7 us
    ppermute x4, starting transfers between devices, shifted(): return lax.ppermute(array, axis, pairs)  8.41 us
    all_to_all x1, waiting for transfers between devices, kernel_pass(): small = lax.all_to_all(copies, 'obj', 0, 0, tiled=True)  7.84 us
    dot_general x1, matrix products, kernel_pass(): lax.dot_general(tap_grads, deconv_weight, (((1,), (1,)), ((), ())), prefe...  7.74 us
  transfers between devices with their start and end apart: 17, of which 13 were waited for; matrix products, arithmetic and copies ran while one was open for 10% of the time, Pallas kernels for 20%

profile of v5, /device:TPU:0, one launch (start us, length us, event | category | flops | bytes accessed | tf_op | source)
XLA Modules:
  0.0 260.7 jit_solution(1416128158128302805)
XLA Ops:
  0.6 10.9 %shard_map.101 = (f32[6,2048,128]{2,1,0:T(8,128)}, bf16[8,6,96,128]{3,2,1,0:T(8,128)(2,1)}, bf16[6,256,128]{2,1,0:T(8,128)(2,1)}, bf16[6,256,128]{2,1,0:T(8,128)(2,1)}, f32[6,1,128]{2,1,0:T(1,128)}) custom-call(bf16[6,128,1024]{2,1,0:T(8,128)(2,1)} %bitcast.110, bf16[6,2048,128]{2,1,0:T(8,128)(2,1)} %bitcast.101, bf16[1024,2048]{1,0:T(8,128)(2,1)} %weight_ref.1), custom_call_target="tpu_custom_call" | custom-call | flops 3221225472 | bytes 17825792 | tf_op jit(solution)/shard_map/pallas_call | solution.py:158
  34.2 7.1 %all-to-all-start = ((bf16[8,6,96,128]{3,2,1,0:T(8,128)(2,1)}), bf16[8,6,96,128]{3,2,1,0:T(8,128)(2,1)S(1)}, u32[]{:S(2)}, u32[]{:S(2)}) async-start(bf16[8,6,96,128]{3,2,1,0:T(8,128)(2,1)} %get-tuple-element.80), calls=%async_computation | async-start | bytes 2359296 | tf_op jit(solution)/shard_map/all_to_all | solution.py:787
  43.9 9.3 %shard_map.102 = (bf16[3,2880,128]{2,1,0:T(8,128)(2,1)}, bf16[3,2720,128]{2,1,0:T(8,128)(2,1)}) custom-call(bf16[6,2048,128]{2,1,0:T(8,128)(2,1)} %bitcast.103, bf16[6,256,128]{2,1,0:T(8,128)(2,1)} %copy-done.6, bf16[6,256,128]{2,1,0:T(8,128)(2,1)} %copy-done.7, f32[6,576,128]{2,1,0:T(8,128)} %bitcast.85, ...), custom_call_target="tpu_custom_call" | custom-call | flops 2406481920 | bytes 15532032 | tf_op jit(solution)/shard_map/pallas_call | solution.py:158
  53.2 4.2 %all-to-all-done.parts_ref = bf16[8,6,96,128]{3,2,1,0:T(8,128)(2,1)S(1)} async-done(((bf16[8,6,96,128]{3,2,1,0:T(8,128)(2,1)}), bf16[8,6,96,128]{3,2,1,0:T(8,128)(2,1)S(1)}, u32[]{:S(2)}, u32[]{:S(2)}) %all-to-all-start) | async-done | bytes 1179680 | tf_op jit(solution)/shard_map/all_to_all | solution.py:787
  58.5 21.9 %shard_map.103 = (bf16[6,2880,128]{2,1,0:T(8,128)(2,1)}, bf16[6,2880,128]{2,1,0:T(8,128)(2,1)}, bf16[6,2720,128]{2,1,0:T(8,128)(2,1)}, bf16[8,6,96,128]{3,2,1,0:T(8,128)(2,1)}) custom-call(bf16[8,6,96,128]{3,2,1,0:T(8,128)(2,1)} %copy-done.4, f32[1,128]{1,0:T(1,128)} %bitcast.112, f32[6,2048,128]{2,1,0:T(8,128)} %get-tuple-element.70.refs_0_, ...), custom_call_target="tpu_custom_call" | custom-call | flops 4812963840 | bytes 24183808 | tf_op jit(solution)/shard_map/pallas_call | solution.py:158
  80.4 3.7 %all-to-all-start.1 = ((bf16[8,6,96,128]{3,2,1,0:T(8,128)(2,1)}), bf16[8,6,96,128]{3,2,1,0:T(8,128)(2,1)S(1)}, u32[]{:S(2)}, u32[]{:S(2)}) async-start(bf16[8,6,96,128]{3,2,1,0:T(8,128)(2,1)} %get-tuple-element.86), calls=%async_computation.1 | async-start | bytes 2359296 | tf_op jit(solution)/shard_map/all_to_all | solution.py:787
  84.7 9.2 %shard_map.104 = (bf16[3,2880,128]{2,1,0:T(8,128)(2,1)}, bf16[3,2720,128]{2,1,0:T(8,128)(2,1)}) custom-call(bf16[6,2048,128]{2,1,0:T(8,128)(2,1)} %bitcast.104, bf16[6,256,128]{2,1,0:T(8,128)(2,1)} %copy-done.6, bf16[6,256,128]{2,1,0:T(8,128)(2,1)} %copy-done.7, f32[6,576,128]{2,1,0:T(8,128)} %bitcast.87, ...), custom_call_target="tpu_custom_call" | custom-call | flops 2406481920 | bytes 15532032 | tf_op jit(solution)/shard_map/pallas_call | solution.py:158
  93.9 6.4 %all-to-all-done.1.parts_ref = bf16[8,6,96,128]{3,2,1,0:T(8,128)(2,1)S(1)} async-done(((bf16[8,6,96,128]{3,2,1,0:T(8,128)(2,1)}), bf16[8,6,96,128]{3,2,1,0:T(8,128)(2,1)S(1)}, u32[]{:S(2)}, u32[]{:S(2)}) %all-to-all-start.1) | async-done | bytes 1179680 | tf_op jit(solution)/shard_map/all_to_all | solution.py:787
  101.3 15.2 %shard_map.105 = (bf16[6,2720,128]{2,1,0:T(8,128)(2,1)}, bf16[6,2720,128]{2,1,0:T(8,128)(2,1)}, bf16[8,6,96,128]{3,2,1,0:T(8,128)(2,1)}) custom-call(bf16[8,6,96,128]{3,2,1,0:T(8,128)(2,1)} %copy-done.1, f32[1,128]{1,0:T(1,128)} %fusion.2.bias_ref, bf16[6,2720,128]{2,1,0:T(8,128)(2,1)} %get-tuple-element.90.refs_0_, ...), custom_call_target="tpu_custom_call" | custom-call | bytes 27919360 | tf_op jit(solution)/shard_map/pallas_call | solution.py:158
  116.4 3.7 %all-to-all-start.2 = ((bf16[8,6,96,128]{3,2,1,0:T(8,128)(2,1)}), bf16[8,6,96,128]{3,2,1,0:T(8,128)(2,1)S(1)}, u32[]{:S(2)}, u32[]{:S(2)}) async-start(bf16[8,6,96,128]{3,2,1,0:T(8,128)(2,1)} %get-tuple-element.95), calls=%async_computation.2 | async-start | bytes 2359296 | tf_op jit(solution)/shard_map/all_to_all | solution.py:787
  120.9 13.3 %shard_map.106.refs_0_ = bf16[1152,128]{1,0:T(8,128)(2,1)} custom-call(bf16[6,2720,128]{2,1,0:T(8,128)(2,1)} %get-tuple-element.96.act_ref, bf16[6,2048,128]{2,1,0:T(8,128)(2,1)} %bitcast.105), custom_call_target="tpu_custom_call" | custom-call | flops 4529848320 | bytes 14647296 | tf_op jit(solution)/shard_map/pallas_call | solution.py:158
  137.2 18.6 %shard_map.107 = (bf16[6,2720,128]{2,1,0:T(8,128)(2,1)}, bf16[6,2048,128]{2,1,0:T(8,128)(2,1)}, bf16[8,6,96,128]{3,2,1,0:T(8,128)(2,1)}, f32[6,1,128]{2,1,0:T(1,128)}) custom-call(bf16[8,6,96,128]{3,2,1,0:T(8,128)(2,1)} %copy-done.5, f32[1,128]{1,0:T(1,128)} %broadcast_1_bias_ref.2.bias_ref, bf16[6,2720,128]{2,1,0:T(8,128)(2,1)} %get-tuple-element.98.refs_0_, ...), custom_call_target="tpu_custom_call" | custom-call | flops 4529848320 | bytes 20153344 | tf_op jit(solution)/shard_map/pallas_call | solution.py:158
  155.8 3.6 %all-to-all-start.3 = ((bf16[8,6,96,128]{3,2,1,0:T(8,128)(2,1)}), bf16[8,6,96,128]{3,2,1,0:T(8,128)(2,1)S(1)}, u32[]{:S(2)}, u32[]{:S(2)}) async-start(bf16[8,6,96,128]{3,2,1,0:T(8,128)(2,1)} %get-tuple-element.100), calls=%async_computation.3 | async-start | bytes 2359296 | tf_op jit(solution)/shard_map/all_to_all | solution.py:787
  159.4 13.6 %shard_map.108 = bf16[2432,128]{1,0:T(8,128)(2,1)} custom-call(bf16[6,2880,128]{2,1,0:T(8,128)(2,1)} %get-tuple-element.101.act_ref, bf16[6,2720,128]{2,1,0:T(8,128)(2,1)} %get-tuple-element.102.grad_ref, bf16[1152,128]{1,0:T(8,128)(2,1)} %shard_map.106.refs_0_, f32[6,1,128]{2,1,0:T(1,128)} %get-tuple-element.104.refs_1_, ...), custom_call_target="tpu_custom_call" | custom-call | flops 4529848320 | bytes 17805312 | tf_op jit(solution)/shard_map/pallas_call | solution.py:158
  175.5 3.5 %all-to-all-start.4 = ((bf16[8,304,128]{2,1,0:T(8,128)(2,1)}), bf16[8,304,128]{2,1,0:T(8,128)(2,1)S(1)}, u32[]{:S(2)}, u32[]{:S(2)}) async-start(bf16[8,304,128]{2,1,0:T(8,128)(2,1)} %bitcast.94), calls=%async_computation.4 | async-start | bytes 1245184 | tf_op jit(solution)/shard_map/all_to_all | solution.py:891
  179.1 6.6 %shard_map.109 = (bf16[6,128,2048]{2,1,0:T(8,128)(2,1)}, f32[6,1,128]{2,1,0:T(1,128)}) custom-call(bf16[8,6,96,128]{3,2,1,0:T(8,128)(2,1)} %copy-done, f32[1,128]{1,0:T(1,128)} %broadcast_1_bias_ref.2.bias_ref, bf16[6,2048,128]{2,1,0:T(8,128)(2,1)} %get-tuple-element.107.refs_0_), custom_call_target="tpu_custom_call" | custom-call | bytes 8651776 | tf_op jit(solution)/shard_map/pallas_call | solution.py:158
  190.1 5.6 %convolution_convert_fusion = bf16[2048,1024]{0,1:T(8,128)(2,1)S(1)} fusion(bf16[768,2048]{1,0:T(8,128)(2,1)} %bitcast.108, bf16[768,1024]{1,0:T(8,128)(2,1)S(1)} %bitcast.111), kind=kOutput, calls=%fused_computation.1 | convolution fusion | flops 3223322624 | bytes 8912896 | tf_op jit(solution)/shard_map/dot_general | solution.py:903
  198.0 4.9 %all-to-all-start.5 = ((bf16[4,320,128]{2,1,0:T(8,128)(2,1)}), bf16[4,320,128]{2,1,0:T(8,128)(2,1)S(1)}, u32[]{:S(2)}, u32[]{:S(2)}) async-start(bf16[4,320,128]{2,1,0:T(8,128)(2,1)} %broadcast_in_dim.8), calls=%async_computation.5 | async-start | bytes 655360 | tf_op jit(solution)/shard_map/all_to_all | solution.py:902
  205.9 7.8 %all-to-all-done.5 = bf16[4,320,128]{2,1,0:T(8,128)(2,1)S(1)} async-done(((bf16[4,320,128]{2,1,0:T(8,128)(2,1)}), bf16[4,320,128]{2,1,0:T(8,128)(2,1)S(1)}, u32[]{:S(2)}, u32[]{:S(2)}) %all-to-all-start.5) | async-done | bytes 327712 | tf_op jit(solution)/shard_map/all_to_all | solution.py:902
  218.3 3.5 %all-to-all-start.6 = ((bf16[8,320,128]{2,1,0:T(8,128)(2,1)}), bf16[8,320,128]{2,1,0:T(8,128)(2,1)S(1)}, u32[]{:S(2)}, u32[]{:S(2)}) async-start(bf16[8,320,128]{2,1,0:T(8,128)(2,1)} %broadcast_in_dim.18), calls=%async_computation.6 | async-start | bytes 1310720 | tf_op jit(solution)/shard_map/all_to_all | solution.py:669
  221.8 7.7 %convolution_convert_fusion.1 = bf16[768,1024]{1,0:T(8,128)(2,1)} fusion(bf16[768,2048]{1,0:T(8,128)(2,1)} %bitcast.109, bf16[1024,2048]{1,0:T(8,128)(2,1)} %weight_ref.1), kind=kOutput, calls=%fused_computation.2 | convolution fusion | flops 3222011904 | bytes 8912896 | tf_op jit(solution)/shard_map/dot_general | solution.py:910
  231.8 3.5 %collective-permute-done.5 = bf16[2,1,1,2,32,2048]{5,4,3,2,1,0:T(8,128)(2,1)S(1)} collective-permute-done((bf16[2,1,1,2,32,2048]{5,4,3,2,1,0:T(8,128)(2,1)}, bf16[2,1,1,2,32,2048]{5,4,3,2,1,0:T(8,128)(2,1)S(1)}, u32[]{:S(2)}, u32[]{:S(2)}) %collective-permute-start.5) | collective-permute-done | bytes 524320 | tf_op jit(solution)/shard_map/ppermute | solution.py:707
  235.5 6.9 %collective-permute-done.8 = bf16[2,1,1,1,32,2048]{5,4,3,2,1,0:T(8,128)(2,1)S(1)} collective-permute-done((bf16[2,1,1,1,32,2048]{5,4,3,2,1,0:T(8,128)(2,1)S(1)}, bf16[2,1,1,1,32,2048]{5,4,3,2,1,0:T(8,128)(2,1)S(1)}, u32[]{:S(2)}, u32[]{:S(2)}) %collective-permute-start.8) | collective-permute-done | bytes 262176 | tf_op jit(solution)/shard_map/ppermute | solution.py:707
  249.2 10.7 %all-to-all-done.7 = bf16[4,32,2048]{2,1,0:T(8,128)(2,1)S(1)} async-done(((bf16[4,32,2048]{2,1,0:T(8,128)(2,1)}), bf16[4,32,2048]{2,1,0:T(8,128)(2,1)S(1)}, u32[]{:S(2)}, u32[]{:S(2)}) %all-to-all-start.7) | async-done | bytes 524320 | tf_op jit(solution)/shard_map/all_to_all | solution.py:128
  (92 shorter events, 58.0 us)
Async XLA Ops:
  11.6 6.6 %collective-permute-start = (bf16[6,256,128]{2,1,0:T(8,128)(2,1)}, bf16[6,256,128]{2,1,0:T(8,128)(2,1)S(1)}, u32[]{:S(2)}, u32[]{:S(2)}) collective-permute-start(bf16[6,256,128]{2,1,0:T(8,128)(2,1)} %get-tuple-element.65), channel_id=1, source_target_pairs={{0,2},{2,4},{4,6},{1,3},{3,5},{5,7},{8,10},{10,12},{12,14},{9,11},... | collective-permute-start | bytes 1179656 | tf_op jit(solution)/shard_map/ppermute | solution.py:20
  14.0 5.9 %collective-permute-start.1 = (bf16[6,256,128]{2,1,0:T(8,128)(2,1)}, bf16[6,256,128]{2,1,0:T(8,128)(2,1)S(1)}, u32[]{:S(2)}, u32[]{:S(2)}) collective-permute-start(bf16[6,256,128]{2,1,0:T(8,128)(2,1)} %get-tuple-element.66), channel_id=1, source_target_pairs={{2,0},{4,2},{6,4},{3,1},{5,3},{7,5},{10,8},{12,10},{14,12},{11,9},... | collective-permute-start | bytes 1179656 | tf_op jit(solution)/shard_map/ppermute | solution.py:20
  18.1 7.9 %copy-start.6 = (bf16[6,256,128]{2,1,0:T(8,128)(2,1)}, bf16[6,256,128]{2,1,0:T(8,128)(2,1)S(1)}, u32[]{:S(2)}) copy-start(bf16[6,256,128]{2,1,0:T(8,128)(2,1)S(1)} %collective-permute-done.above_ref.refs_1_) | copy-start | bytes 1179652
  19.9 7.6 %copy-start.7 = (bf16[6,256,128]{2,1,0:T(8,128)(2,1)}, bf16[6,256,128]{2,1,0:T(8,128)(2,1)S(1)}, u32[]{:S(2)}) copy-start(bf16[6,256,128]{2,1,0:T(8,128)(2,1)S(1)} %collective-permute-done.1.below_ref.refs_2_) | copy-start | bytes 1179652
  20.7 6.8 %collective-permute-start.2 = (bf16[6,36,2,2,128]{4,3,1,0,2:T(2,128)(2,1)S(1)}, bf16[6,36,2,2,128]{4,3,1,0,2:T(2,128)(2,1)S(1)}, u32[]{:S(2)}, u32[]{:S(2)}) collective-permute-start(bf16[6,36,2,2,128]{4,3,1,0,2:T(2,128)(2,1)S(1)} %pad_maximum_fusion), channel_id=1, source_target_pairs={{0,1},{2,3},{4,5},{6,7},{8,9},{10,11},{12,13},{14,15},{16,17},{18,... | collective-permute-start | bytes 663560 | tf_op jit(solution)/shard_map/ppermute | solution.py:20
  24.7 7.8 %collective-permute-start.3 = (bf16[6,36,2,2,128]{4,3,2,1,0:T(2,128)(2,1)S(1)}, bf16[6,36,2,2,128]{4,3,2,1,0:T(2,128)(2,1)S(1)}, u32[]{:S(2)}, u32[]{:S(2)}) collective-permute-start(bf16[6,36,2,2,128]{4,3,2,1,0:T(2,128)(2,1)S(1)} %pad_maximum_fusion.1), channel_id=1, source_target_pairs={{1,0},{3,2},{5,4},{7,6},{9,8},{11,10},{13,12},{15,14},{17,16},{19,... | collective-permute-start | bytes 663560 | tf_op jit(solution)/shard_map/ppermute | solution.py:20
  32.7 8.5 %copy-start.3 = (bf16[2,1152,128]{2,1,0:T(8,128)(2,1)S(1)}, bf16[2,1152,128]{2,1,0:T(8,128)(2,1)}, u32[]{:S(2)}) copy-start(bf16[2,1152,128]{2,1,0:T(8,128)(2,1)} %param.10) | copy-start | bytes 1769476
  34.2 23.3 %all-to-all-start = ((bf16[8,6,96,128]{3,2,1,0:T(8,128)(2,1)}), bf16[8,6,96,128]{3,2,1,0:T(8,128)(2,1)S(1)}, u32[]{:S(2)}, u32[]{:S(2)}) async-start(bf16[8,6,96,128]{3,2,1,0:T(8,128)(2,1)} %get-tuple-element.80), calls=%async_computation | async-start | bytes 2359296 | tf_op jit(solution)/shard_map/all_to_all | solution.py:787
  80.4 3.7 %copy-start.9 = (f32[2,128]{1,0:T(2,128)S(1)}, f32[2,128]{1,0:T(2,128)}, u32[]{:S(2)}) copy-start(f32[2,128]{1,0:T(2,128)} %param.11) | copy-start | bytes 3076
  80.4 3.7 %copy-start.10 = (f32[128]{0:T(128)S(1)}, f32[128]{0:T(128)}, u32[]{:S(2)}) copy-start(f32[128]{0:T(128)} %param.9) | copy-start | bytes 1540
  80.4 19.9 %all-to-all-start.1 = ((bf16[8,6,96,128]{3,2,1,0:T(8,128)(2,1)}), bf16[8,6,96,128]{3,2,1,0:T(8,128)(2,1)S(1)}, u32[]{:S(2)}, u32[]{:S(2)}) async-start(bf16[8,6,96,128]{3,2,1,0:T(8,128)(2,1)} %get-tuple-element.86), calls=%async_computation.1 | async-start | bytes 2359296 | tf_op jit(solution)/shard_map/all_to_all | solution.py:787
  116.4 19.7 %all-to-all-start.2 = ((bf16[8,6,96,128]{3,2,1,0:T(8,128)(2,1)}), bf16[8,6,96,128]{3,2,1,0:T(8,128)(2,1)S(1)}, u32[]{:S(2)}, u32[]{:S(2)}) async-start(bf16[8,6,96,128]{3,2,1,0:T(8,128)(2,1)} %get-tuple-element.95), calls=%async_computation.2 | async-start | bytes 2359296 | tf_op jit(solution)/shard_map/all_to_all | solution.py:787
  155.8 19.7 %all-to-all-start.3 = ((bf16[8,6,96,128]{3,2,1,0:T(8,128)(2,1)}), bf16[8,6,96,128]{3,2,1,0:T(8,128)(2,1)S(1)}, u32[]{:S(2)}, u32[]{:S(2)}) async-start(bf16[8,6,96,128]{3,2,1,0:T(8,128)(2,1)} %get-tuple-element.100), calls=%async_computation.3 | async-start | bytes 2359296 | tf_op jit(solution)/shard_map/all_to_all | solution.py:787
  175.5 3.6 %copy-start = (bf16[8,6,96,128]{3,2,1,0:T(8,128)(2,1)}, bf16[8,6,96,128]{3,2,1,0:T(8,128)(2,1)S(1)}, u32[]{:S(2)}) copy-start(bf16[8,6,96,128]{3,2,1,0:T(8,128)(2,1)S(1)} %all-to-all-done.3.parts_ref) | copy-start | bytes 3538948
  175.5 13.7 %all-to-all-start.4 = ((bf16[8,304,128]{2,1,0:T(8,128)(2,1)}), bf16[8,304,128]{2,1,0:T(8,128)(2,1)S(1)}, u32[]{:S(2)}, u32[]{:S(2)}) async-start(bf16[8,304,128]{2,1,0:T(8,128)(2,1)} %bitcast.94), calls=%async_computation.4 | async-start | bytes 1245184 | tf_op jit(solution)/shard_map/all_to_all | solution.py:891
  179.1 11.0 %copy-start.8 = (bf16[2,3,8,16,1024]{4,3,2,1,0:T(8,128)(2,1)S(1)}, bf16[2,3,8,16,1024]{4,3,2,1,0:T(8,128)(2,1)}, u32[]{:S(2)}) copy-start(bf16[2,3,8,16,1024]{4,3,2,1,0:T(8,128)(2,1)} %param.6) | copy-start | bytes 4718596
  197.8 5.0 %collective-permute-start.4 = (bf16[4,2,1,2,32,2048]{5,4,3,2,1,0:T(8,128)(2,1)S(1)}, bf16[4,2,1,2,32,2048]{5,4,3,2,1,0:T(8,128)(2,1)}, u32[]{:S(2)}, u32[]{:S(2)}) collective-permute-start(bf16[4,2,1,2,32,2048]{5,4,3,2,1,0:T(8,128)(2,1)S(1)} %constant_dynamic-slice_fusion.6), channel_id=1, source_target_pairs={{0,2},{2,0},{4,6},{6,4},{1,3},{3,1},{5,7},{7,5},{8,10},{10,8},{12,... | collective-permute-start | bytes 6291464 | tf_op jit(solution)/shard_map/ppermute | solution.py:707
  198.0 15.7 %all-to-all-start.5 = ((bf16[4,320,128]{2,1,0:T(8,128)(2,1)}), bf16[4,320,128]{2,1,0:T(8,128)(2,1)S(1)}, u32[]{:S(2)}, u32[]{:S(2)}) async-start(bf16[4,320,128]{2,1,0:T(8,128)(2,1)} %broadcast_in_dim.8), calls=%async_computation.5 | async-start | bytes 655360 | tf_op jit(solution)/shard_map/all_to_all | solution.py:902
  215.6 15.0 %collective-permute-start.7 = (bf16[2,2,1,1,32,2048]{5,4,3,2,1,0:T(8,128)(2,1)}, bf16[2,2,1,1,32,2048]{5,4,3,2,1,0:T(8,128)(2,1)S(1)}, u32[]{:S(2)}, u32[]{:S(2)}) collective-permute-start(bf16[2,2,1,1,32,2048]{5,4,3,2,1,0:T(8,128)(2,1)} %get-tuple-element.117), channel_id=1, source_target_pairs={{0,1},{1,0},{2,3},{3,2},{4,5},{5,4},{6,7},{7,6},{8,9},{9,8},{10,11... | collective-permute-start | bytes 1572872 | tf_op jit(solution)/shard_map/ppermute | solution.py:707
  216.7 18.5 %collective-permute-start.5 = (bf16[2,1,1,2,32,2048]{5,4,3,2,1,0:T(8,128)(2,1)}, bf16[2,1,1,2,32,2048]{5,4,3,2,1,0:T(8,128)(2,1)S(1)}, u32[]{:S(2)}, u32[]{:S(2)}) collective-permute-start(bf16[2,1,1,2,32,2048]{5,4,3,2,1,0:T(8,128)(2,1)} %get-tuple-element.115), channel_id=1, source_target_pairs={{0,4},{2,6},{4,0},{6,2},{1,5},{3,7},{5,1},{7,3},{8,12},{10,14},{12... | collective-permute-start | bytes 1572872 | tf_op jit(solution)/shard_map/ppermute | solution.py:707
  218.3 25.1 %all-to-all-start.6 = ((bf16[8,320,128]{2,1,0:T(8,128)(2,1)}), bf16[8,320,128]{2,1,0:T(8,128)(2,1)S(1)}, u32[]{:S(2)}, u32[]{:S(2)}) async-start(bf16[8,320,128]{2,1,0:T(8,128)(2,1)} %broadcast_in_dim.18), calls=%async_computation.6 | async-start | bytes 1310720 | tf_op jit(solution)/shard_map/all_to_all | solution.py:669
  230.8 11.6 %collective-permute-start.8 = (bf16[2,1,1,1,32,2048]{5,4,3,2,1,0:T(8,128)(2,1)S(1)}, bf16[2,1,1,1,32,2048]{5,4,3,2,1,0:T(8,128)(2,1)S(1)}, u32[]{:S(2)}, u32[]{:S(2)}) collective-permute-start(bf16[2,1,1,1,32,2048]{5,4,3,2,1,0:T(8,128)(2,1)S(1)} %constant_dynamic-slice_fusion), channel_id=1, source_target_pairs={{0,4},{2,6},{4,0},{6,2},{1,5},{3,7},{5,1},{7,3},{8,12},{10,14},{12... | collective-permute-start | bytes 786440 | tf_op jit(solution)/shard_map/ppermute | solution.py:707
  235.4 7.1 %collective-permute-start.6 = (bf16[2,1,1,1,32,2048]{5,4,3,2,1,0:T(8,128)(2,1)S(1)}, bf16[2,1,1,1,32,2048]{5,4,3,2,1,0:T(8,128)(2,1)S(1)}, u32[]{:S(2)}, u32[]{:S(2)}) collective-permute-start(bf16[2,1,1,1,32,2048]{5,4,3,2,1,0:T(8,128)(2,1)S(1)} %constant_dynamic-slice_fusion.1), channel_id=1, source_target_pairs={{0,1},{1,0},{2,3},{3,2},{4,5},{5,4},{6,7},{7,6},{8,9},{9,8},{10,11... | collective-permute-start | bytes 786440 | tf_op jit(solution)/shard_map/ppermute | solution.py:707
  243.4 16.5 %all-to-all-start.7 = ((bf16[4,32,2048]{2,1,0:T(8,128)(2,1)}), bf16[4,32,2048]{2,1,0:T(8,128)(2,1)S(1)}, u32[]{:S(2)}, u32[]{:S(2)}) async-start(bf16[4,32,2048]{2,1,0:T(8,128)(2,1)} %maximum_bitcast_fusion), calls=%async_computation.7 | async-start | bytes 1048576 | tf_op jit(solution)/shard_map/all_to_all | solution.py:128
  (4 other events, 5.0 us)
